TPU v7x, 128 devices: a whole 4x4x4 slice. The times are simulated.
128 devices in a mesh: mem: 8 (over x, core), tx: 4 (over z), ty: 4 (over y).
Axes of the slice: x: 4, y: 4, z: 4, core: 2. Of those that a mesh axis runs over, the one named last changes fastest.
Arguments:
- pressure: float32 [64, 1024, 1024], P('mem', 'tx', 'ty'), may hold values from -6 to 6
- elevation: float32 [1024, 1024], P('tx', 'ty'), may hold values from -4 to 4
- ks_field: float32 [1024, 1024], P('tx', 'ty'), may hold values from 0.03 to 0.24
- melt_rate: float32 [64, 1024, 1024], P('mem', 'tx', 'ty'), may hold values from -1.5 to 1.5
- obs_index: int32 [1024], replicated, may hold values from 0 to 1048575
- obs_value: float32 [1024], P(('tx', 'ty')), may hold values from -6 to 6
- obs_error: float32 [1024], P(('tx', 'ty')), may hold values from 0.3 to 1
- perturbation: float32 [1024, 64], P(('tx', 'ty'), 'mem'), may hold values from -6 to 6
Outputs:
- analysis: float32 [64, 1024, 1024], P('mem', 'tx', 'ty')
All inputs are finite; a program needn't handle non-finite values.
Results may differ from a plain program's by a relative error of at most 0.0089.
Values may be sent and summed in bfloat16 or wider, within the bound.
No kernel may reach another device: no remote copies, remote signals or barrier semaphores. Data moves between devices by JAX's collectives and lax.ppermute only.
A program may use at most 128 MiB of HBM per device.

v0:
```python
import functools

import jax
import jax.numpy as jnp
from jax import lax
from jax.experimental import pallas as pl
from jax.experimental.pallas import tpu as pltpu
from jax.sharding import PartitionSpec as P

SUBSTEPS = 4
W = SUBSTEPS
GROUP = 128 // W
ROWS = 16
F32 = jnp.float32
BF16 = jnp.bfloat16
VMEM_SPEC = pl.BlockSpec(memory_space=pltpu.VMEM)
HBM_SPEC = pl.BlockSpec(memory_space=pltpu.HBM)


def lanes():
    return lax.broadcasted_iota(jnp.int32, (8, 128), 1)


def sublanes():
    return lax.broadcasted_iota(jnp.int32, (8, 128), 0)


def wide(row):
    return jnp.broadcast_to(row, (8, 128))


def ends_kernel(
    obs_ref, p_ref, w_ref, e_ref, k_ref, top_ref, bottom_ref, code_ref, inside_ref,
    cubes, sems,
):
    _, size_x, size_y = p_ref.shape
    copies = []
    for i, lo in enumerate((0, size_x - 8)):
        for j, ref in enumerate((p_ref, w_ref)):
            copies.append((ref.at[:, pl.ds(lo, 8), :], cubes.at[2 * i + j]))
    copies = [pltpu.make_async_copy(a, b, sems.at[n]) for n, (a, b) in enumerate(copies)]
    for c in copies:
        c.start()
    bits_x, bits_y = size_x.bit_length() - 1, size_y.bit_length() - 1
    total_y = size_y * lax.axis_size("ty")
    obs = obs_ref[...]
    x = lax.shift_right_logical(obs, total_y.bit_length() - 1)
    y = obs & (total_y - 1)
    mine = (lax.shift_right_logical(x, bits_x) == lax.axis_index("tx")) & (
        lax.shift_right_logical(y, bits_y) == lax.axis_index("ty")
    )
    x, y = x & (size_x - 1), y & (size_y - 1)
    tile = x * (size_y // 128) + lax.shift_right_logical(y, 7)
    code_ref[...] = tile * 128 + ((lanes() - y) & 127)
    inside_ref[...] = jnp.where(mine, F32(1), F32(0))
    for c in copies:
        c.wait()
    sub = lax.broadcasted_iota(jnp.int32, (8, size_y), 0)
    for i, out in enumerate((top_ref, bottom_ref)):
        for j in range(2):
            turned = jnp.swapaxes(cubes[2 * i + j], 0, 1)
            for r in range(W):
                out[j * W + r] = turned[r if i == 0 else 8 - W + r]
        lo = (0, size_x - 8)[i]
        e, k = e_ref[lo : lo + 8, :], k_ref[lo : lo + 8, :]
        if i == 0:
            k = pltpu.roll(k, 4, 0)
        else:
            e = pltpu.roll(e, 4, 0)
        out[2 * W] = jnp.where(sub < 4, e, k)


def ends(obs, p, w, e, k):
    members, _, size_y = p.shape
    edge = jax.ShapeDtypeStruct((2 * W + 1, members, size_y), F32)
    return pl.pallas_call(
        ends_kernel,
        in_specs=[VMEM_SPEC] + [HBM_SPEC] * 2 + [VMEM_SPEC] * 2,
        out_specs=[VMEM_SPEC] * 4,
        out_shape=[
            edge, edge, jax.ShapeDtypeStruct(obs.shape, jnp.int32),
            jax.ShapeDtypeStruct(obs.shape, F32),
        ],
        scratch_shapes=[
            pltpu.VMEM((4, members, 8, size_y), F32),
            pltpu.SemaphoreType.DMA((4,)),
        ],
        compiler_params=pltpu.CompilerParams(vmem_limit_bytes=56 * 2**20),
        name="ends",
    )(obs, p, w, e, k)


def pack_rows(rows):
    slot = lanes() // W
    left = jnp.zeros((8, 128), F32)
    right = jnp.zeros((8, 128), F32)
    for r, a, b in rows:
        if r:
            a = pltpu.roll(a, W * r, 1)
            b = pltpu.roll(b, W * r, 1)
        left = jnp.where(slot == r, a, left)
        right = jnp.where(slot == (r - 1) % GROUP, b, right)
    return left, right


def turn_kernel(
    p_in, w_in, e_ref, k_ref, pt_out, wt_out, left_ref, right_ref,
    p_ref, w_ref, pt_ref, wt_ref, in_sems, out_sems,
):
    groups = left_ref.shape[0]

    def rows_of(g):
        return pl.ds(pl.multiple_of(g * GROUP, GROUP), GROUP)

    def fetch(g, f):
        src, dst = ((p_in, p_ref), (w_in, w_ref))[f]
        at = rows_of(g)
        return pltpu.make_async_copy(src.at[:, at, :], dst.at[:, at, :], in_sems.at[f, g])

    def leave(g, f):
        src, dst = ((pt_ref, pt_out), (wt_ref, wt_out))[f]
        at = rows_of(g)
        return pltpu.make_async_copy(src.at[at], dst.at[at], out_sems.at[f, g])

    for g in range(groups):
        for f in range(2):
            fetch(g, f).start()

    def group(g, _):
        at = rows_of(g)
        for f, (src, dst) in enumerate(((p_ref, pt_ref), (w_ref, wt_ref))):
            fetch(g, f).wait()
            rows = jnp.swapaxes(src[:, at, :] * F32(0.5), 0, 1)
            dst[at] = rows
            left_ref[g, f], right_ref[g, f] = pack_rows(
                (r, rows[r, :, 0:128], rows[r, :, 128:256]) for r in range(GROUP)
            )
            leave(g, f).start()
        fields = []
        for base, ref, factor in ((0, e_ref, 0.5), (4, k_ref, 0.25)):
            block = ref[at, :] * F32(factor)
            for q in range(GROUP // 8):
                part = block[8 * q : 8 * q + 8]
                fields.append((base + q, part[:, 0:128], part[:, 128:256]))
        left_ref[g, 2], right_ref[g, 2] = pack_rows(fields)
        return 0

    lax.fori_loop(0, groups, group, 0)
    for g in range(groups):
        for f in range(2):
            leave(g, f).wait()


def turn(p, w, e, k):
    members, size_x, size_y = p.shape
    groups = size_x // GROUP
    turned = (size_x, members, size_y)
    return pl.pallas_call(
        turn_kernel,
        in_specs=[HBM_SPEC] * 2 + [VMEM_SPEC] * 2,
        out_specs=[HBM_SPEC] * 2 + [VMEM_SPEC] * 2,
        out_shape=[jax.ShapeDtypeStruct(turned, F32)] * 2
        + [jax.ShapeDtypeStruct((groups, 3, 8, 128), F32)] * 2,
        scratch_shapes=[pltpu.VMEM(p.shape, F32)] * 2 + [pltpu.VMEM(turned, F32)] * 2
        + [pltpu.SemaphoreType.DMA((2, groups))] * 2,
        cost_estimate=pl.CostEstimate(flops=10**7, bytes_accessed=9 * 2**20, transcendentals=0),
        compiler_params=pltpu.CompilerParams(vmem_limit_bytes=52 * 2**20),
        name="turn",
    )(p, w, e, k)


def rows_kernel(
    up_ref, down_ref, top_ref, bottom_ref, left_in, right_in, above_ref, below_ref,
    left_ref, right_ref,
):
    tile, groups = lax.axis_index("tx"), left_in.shape[0]
    first, last = tile == 0, tile == lax.axis_size("tx") - 1
    left_ref[0:groups] = left_in[...]
    right_ref[0:groups] = right_in[...]
    sub = lax.broadcasted_iota(jnp.int32, (8, 256), 0)

    def mirrored(block):
        out = block
        for i in range(4):
            for base in (0, 4):
                row = block[base + 3 - i : base + 4 - i, :]
                out = jnp.where(sub == base + i, jnp.broadcast_to(row, (8, 256)), out)
        return out

    for flag, got, own, out in (
        (first, up_ref, top_ref, above_ref),
        (last, down_ref, bottom_ref, below_ref),
    ):
        for f in range(2):
            for i in range(W):
                row = jnp.where(flag, own[f * W + W - 1 - i], got[f * W + i])
                out[f * W + i] = row * F32(0.5)
        block = jnp.where(flag, mirrored(own[2 * W]), got[2 * W])
        out[2 * W] = block * jnp.where(sub < 4, F32(0.5), F32(0.25))
    for f in range(2):
        left_ref[groups, f], right_ref[groups, f] = pack_rows(
            (half * W + i, out[f * W + i, :, 0:128], out[f * W + i, :, 128:256])
            for half, out in enumerate((above_ref, below_ref))
            for i in range(W)
        )
    above, below = above_ref[2 * W], below_ref[2 * W]
    e = jnp.where(sub < 4, above, pltpu.roll(below, 4, 0))
    k = jnp.where(sub < 4, pltpu.roll(above, 4, 0), below)
    left_ref[groups, 2], right_ref[groups, 2] = pack_rows(
        (slot, v[:, 0:128], v[:, 128:256]) for slot, v in ((0, e), (4, k))
    )


def halo_rows(up, down, top, bottom, left, right):
    packs = jax.ShapeDtypeStruct((left.shape[0] + 1, *left.shape[1:]), F32)
    return pl.pallas_call(
        rows_kernel,
        in_specs=[VMEM_SPEC] * 6,
        out_specs=[VMEM_SPEC] * 4,
        out_shape=[jax.ShapeDtypeStruct(up.shape, F32)] * 2 + [packs] * 2,
        compiler_params=pltpu.CompilerParams(vmem_limit_bytes=4 * 2**20),
        name="rows",
    )(up, down, top, bottom, left, right)


def steps_kernel(
    pt_in, wt_in, e_ref, k_ref, above_ref, below_ref, fl_ref, fr_ref,
    out_ref, round_ref,
    p0, p1, w_s, fy_s, sum_s, e_s, er_s, k_s, kr_s, sems,
):
    size_x = pt_in.shape[0]
    lane = lanes()
    is_first, is_last = lane == 0, lane == 127
    groups = size_x // GROUP
    blocks = size_x // 8 + 2
    inner = (pl.ds(9, size_x), slice(None), pl.ds(0, 256))
    loads = [
        pltpu.make_async_copy(src, dst.at[inner], sems.at[i])
        for i, (src, dst) in enumerate(((pt_in, p0), (wt_in, w_s)))
    ]
    for c in loads:
        c.start()

    def halo(g, f, r):
        a, b = fr_ref[g, f], fl_ref[g, f]
        if r:
            a = pltpu.roll(a, 128 - W * r, 1)
            b = pltpu.roll(b, 128 - W * r, 1)
        return jnp.where(lane < 64, a, b)

    def spread(at, v, here, shifted):
        rolled = [pltpu.roll(u, 127, 1) for u in v]
        for t in range(3):
            here[at, :, 128 * t : 128 * t + 128] = v[t]
            shifted[at, :, 128 * t : 128 * t + 128] = jnp.where(
                is_last, rolled[(t + 1) % 3], rolled[t]
            )

    def unpack_group(g, _):
        for r in range(GROUP):
            for f, dst in ((0, p0), (1, w_s)):
                dst[g * GROUP + r + 9, :, 256:384] = halo(g, f, r)
        for q in range(GROUP // 8):
            rows = pl.ds(pl.multiple_of(g * GROUP + 8 * q, 8), 8)
            for base, ref, factor, here, shifted in (
                (0, e_ref, 0.5, e_s, er_s), (4, k_ref, 0.25, k_s, kr_s),
            ):
                v = [ref[rows, 128 * t : 128 * t + 128] * F32(factor) for t in range(2)]
                spread(g * (GROUP // 8) + q + 1, v + [halo(g, 2, base + q)], here, shifted)
        return 0

    lax.fori_loop(0, groups, unpack_group, 0)
    for r in range(2 * W):
        ref, y = (above_ref, 4 + r) if r < W else (below_ref, size_x + 4 + r)
        for f, dst in ((0, p0), (1, w_s)):
            dst[y + 1, :, 0:256] = ref[f * W + r % W]
            dst[y + 1, :, 256:384] = halo(groups, f, r)
    for base, here, shifted in ((0, e_s, er_s), (4, k_s, kr_s)):
        edge = pltpu.roll(halo(groups, 2, base), 4, 0)
        for at, ref, up in ((0, above_ref, base == 0), (blocks - 1, below_ref, base == 4)):
            v = ref[2 * W]
            v = pltpu.roll(v, 4, 0) if up else v
            spread(at, [v[:, 0:128], v[:, 128:256], edge], here, shifted)

    one, none = F32(1), F32(0)

    tile = lax.axis_index("ty")

    def edge_mask(at):
        return jnp.where(is_last & (jnp.broadcast_to(tile, (8, 128)) == at), none, one)

    mask_right, mask_left = edge_mask(lax.axis_size("ty") - 1), edge_mask(0)
    for c in loads:
        c.wait()

    def tiles(ref, at):
        return [ref[at, :, 128 * t : 128 * t + 128] for t in range(3)]

    def put(ref, at, v):
        for t in range(3):
            ref[at, :, 128 * t : 128 * t + 128] = v[t]

    def row_of(ref, b, u):
        return [wide(ref[b, u : u + 1, 128 * t : 128 * t + 128]) for t in range(3)]

    def step(src, dst):
        count = 8 * blocks // ROWS

        def body(i, carry):
            b_at = jnp.minimum(i, count - 1)
            c_at = jnp.maximum(i - 1, 0) * ROWS
            for u in range(ROWS):
                at = c_at + u
                s, fy = tiles(sum_s, at), tiles(fy_s, at)
                fr = [pltpu.roll(v, 1, 1) for v in fy]
                back = [jnp.where(is_first, fr[(t - 1) % 3], fr[t]) for t in range(3)]
                put(dst, at, [s[t] + (fy[t] - back[t]) for t in range(3)])
            p_old, h_old, c_old, fx_old = carry
            for u in range(ROWS):
                at = b_at * ROWS + u
                block = (b_at * (ROWS // 8) + u // 8, u % 8)
                p = tiles(src, at + 1)
                raw = [pltpu.roll(v, 127, 1) for v in p]
                pr = [jnp.where(is_last, raw[(t + 1) % 3], raw[t]) for t in range(3)]
                e, er = row_of(e_s, *block), row_of(er_s, *block)
                k, kr = row_of(k_s, *block), row_of(kr_s, *block)
                w = tiles(w_s, at)
                h = [p[t] + e[t] for t in range(3)]
                c = [k[t] * jnp.tanh(p[t]) + k[t] for t in range(3)]
                fy = [
                    (c[t] + (kr[t] * jnp.tanh(pr[t]) + kr[t])) * ((pr[t] + er[t]) - h[t])
                    for t in range(3)
                ]
                fy[1] = fy[1] * mask_right
                fy[2] = fy[2] * mask_left
                fx = [(c_old[t] + c[t]) * (h[t] - h_old[t]) for t in range(3)]
                put(sum_s, at, [(p_old[t] + w[t]) + (fx[t] - fx_old[t]) for t in range(3)])
                put(fy_s, at + 1, fy)
                p_old, h_old, c_old, fx_old = p, h, c, fx
            return p_old, h_old, c_old, fx_old

        zero = [jnp.zeros((8, 128), F32)] * 3
        lax.fori_loop(0, count + 1, body, (zero, zero, zero, zero))

    for s in range(SUBSTEPS):
        step(*((p0, p1) if s % 2 == 0 else (p1, p0)))
    last = p0 if SUBSTEPS % 2 == 0 else p1

    def leave(i, _):
        x = pl.multiple_of(i * 8, 8)
        for u in range(8):
            row = last[x + 9 + u, :, 0:256] * F32(2)
            out_ref[2 * x + 2 * u] = row[:, 0:128]
            out_ref[2 * x + 2 * u + 1] = row[:, 128:256]
            round_ref[x + u] = row.astype(BF16)
        return 0

    lax.fori_loop(0, size_x // 8, leave, 0)


def run_steps(pt, wt, e, k, above, below, from_left, from_right):
    size_x, members, size_y = pt.shape
    tile = pltpu.VMEM((size_x + 17, members, size_y + 128), F32)
    flat = pltpu.VMEM((size_x // 8 + 2, 8, size_y + 128), F32)
    return pl.pallas_call(
        steps_kernel,
        in_specs=[HBM_SPEC] * 2 + [VMEM_SPEC] * 6,
        out_specs=[VMEM_SPEC] * 2,
        scratch_shapes=[tile] * 5 + [flat] * 4 + [pltpu.SemaphoreType.DMA((2,))],
        out_shape=[
            jax.ShapeDtypeStruct((size_x * (size_y // 128), members, 128), F32),
            jax.ShapeDtypeStruct((size_x, members, size_y), BF16),
        ],
        compiler_params=pltpu.CompilerParams(vmem_limit_bytes=50 * 2**20),
        name="steps",
    )(pt, wt, e, k, above, below, from_left, from_right)


def pick_kernel(code_ref, f_ref, inside_ref, pick_ref):
    lane = lanes()

    def pick(g, _):
        acc = jnp.zeros((8, 128), F32)
        for u in range(128):
            code = code_ref[g, u]
            v = pltpu.roll(f_ref[lax.shift_right_logical(code, 7)], code & 127, 1)
            acc = jnp.where(lane == u, v, acc)
        keep = wide(inside_ref[pl.ds(g, 1), :]) > F32(0.5)
        pick_ref[:, pl.ds(pl.multiple_of(g * 128, 128), 128)] = jnp.where(keep, acc, F32(0))
        return 0

    lax.fori_loop(0, code_ref.shape[0], pick, 0)


def picks(code, forecast, inside):
    return pl.pallas_call(
        pick_kernel,
        grid_spec=pltpu.PrefetchScalarGridSpec(
            num_scalar_prefetch=1, grid=(), in_specs=[VMEM_SPEC] * 2, out_specs=VMEM_SPEC
        ),
        out_shape=jax.ShapeDtypeStruct((8, code.size), F32),
        compiler_params=pltpu.CompilerParams(vmem_limit_bytes=8 * 2**20),
        name="picks",
    )(code, forecast, inside)


def weights_kernel(near_ref, far_ref, innovation_ref, out_ref, x_s, m_s):
    half = near_ref.shape[0]
    members = 2 * half
    blocks = members // 8
    parts = [r[8 * b : 8 * b + 8, :] for r in (near_ref, far_ref) for b in range(half // 8)]
    total = parts[0]
    for part in parts[1:]:
        total = total + part
    mean = jnp.sum(total, axis=0, keepdims=True) * F32(1.0 / members)
    for b, part in enumerate(parts):
        x_s[8 * b : 8 * b + 8, :] = part - mean
    x = x_s[...]
    dims = (((1,), (1,)), ((), ()))
    dot = functools.partial(
        lax.dot_general, dimension_numbers=dims, precision=lax.Precision.HIGHEST,
        preferred_element_type=F32,
    )
    r = lax.broadcasted_iota(jnp.int32, (members, members), 0)
    c = lax.broadcasted_iota(jnp.int32, (members, members), 1)
    m_s[:, 0:members] = dot(x, x) + jnp.where(r == c, F32(members - 1), F32(0))
    m_s[:, members : 2 * members] = jnp.zeros((members, members), F32)
    m_s[:, members : members + 8] = dot(x, innovation_ref[...])
    m = [m_s[8 * b : 8 * b + 8, :] for b in range(blocks)]
    sub = sublanes()
    for kb in range(blocks):
        cols = [
            [jnp.broadcast_to(m[b][:, 8 * kb + j : 8 * kb + j + 1], (8, 128)) for j in range(8)]
            for b in range(blocks)
        ]
        rows = m[kb]
        piv = list(cols[kb])
        for j in range(8):
            inv = F32(1) / wide(piv[j][j : j + 1])
            here = sub == j
            factor = piv[j]
            top = wide(rows[j : j + 1]) * inv
            rows = jnp.where(here, top, rows - factor * top)
            for q in range(j + 1, 8):
                top = wide(piv[q][j : j + 1]) * inv
                piv[q] = jnp.where(here, top, piv[q] - factor * top)
        spread = [wide(rows[j : j + 1]) for j in range(8)]
        for b in range(blocks):
            if b == kb:
                m[b] = rows
            else:
                acc = cols[b][0] * spread[0]
                for j in range(1, 8):
                    acc = acc + cols[b][j] * spread[j]
                m[b] = m[b] - acc
    for b in range(blocks):
        m_s[8 * b : 8 * b + 8, :] = m[b]
    turned = jnp.transpose(m_s[...], (1, 0))
    out_ref[...] = turned[members : members + 8, 0:members]


def solve_weights(near, far, innovation):
    half, n_obs = near.shape
    members = 2 * half
    return pl.pallas_call(
        weights_kernel,
        in_specs=[VMEM_SPEC] * 3,
        out_specs=VMEM_SPEC,
        scratch_shapes=[
            pltpu.VMEM((members, n_obs), F32),
            pltpu.VMEM((members, 2 * members), F32),
        ],
        out_shape=jax.ShapeDtypeStruct((8, members), F32),
        compiler_params=pltpu.CompilerParams(vmem_limit_bytes=4 * 2**20),
        name="weights",
    )(near, far, innovation)


def update_kernel(w_ref, *refs):
    pieces, (f_ref, out_ref, row_s, done_s, sems) = refs[:-5], refs[-5:]
    step = row_s.shape[0]
    w = w_ref[...].astype(BF16)

    def leave(g):
        at = pl.ds(pl.multiple_of(g * step, step), step)
        return pltpu.make_async_copy(done_s.at[:, at, :], out_ref.at[:, at, :], sems.at[g])

    def chunk(g, _):
        x = g * step
        for r in range(step):
            rows = jnp.concatenate([v[x + r].astype(F32) for v in pieces], axis=0).astype(BF16)
            shift = jnp.dot(w, rows, preferred_element_type=F32)
            for t in range(2):
                cols = slice(128 * t, 128 * t + 128)
                row_s[r, :, cols] = f_ref[2 * (x + r) + t] + shift[:, cols]
        at = pl.ds(pl.multiple_of(x, step), step)
        done_s[:, at, :] = jnp.swapaxes(row_s[...], 0, 1)
        leave(g).start()
        return 0

    count = pieces[0].shape[0] // step
    lax.fori_loop(0, count, chunk, 0)
    for g in range(count):
        leave(g).wait()


def update(weights, pieces, forecast):
    size_x, members, size_y = pieces[0].shape
    step = 32
    whole = (members, size_x, size_y)
    return pl.pallas_call(
        update_kernel,
        in_specs=[VMEM_SPEC] * (len(pieces) + 2),
        out_specs=HBM_SPEC,
        out_shape=jax.ShapeDtypeStruct(whole, F32),
        scratch_shapes=[
            pltpu.VMEM((step, members, size_y), F32),
            pltpu.VMEM(whole, F32),
            pltpu.SemaphoreType.DMA((size_x // step,)),
        ],
        compiler_params=pltpu.CompilerParams(vmem_limit_bytes=8 * 2**20),
        name="update",
    )(weights, *pieces, forecast)


def local(pressure, elevation, ks_field, melt_rate, obs_index, obs_value, obs_error, perturbation):
    n_x, n_y, n_m = (lax.axis_size(a) for a in ("tx", "ty", "mem"))
    tile_x, tile_y = lax.axis_index("tx"), lax.axis_index("ty")

    def ring(n, by):
        return [(i, (i + by) % n) for i in range(n)]

    n_obs = obs_index.shape[0]
    top, bottom, code, inside = ends(
        obs_index.reshape(n_obs // 128, 128), pressure, melt_rate, elevation, ks_field
    )
    up = lax.ppermute(bottom, "tx", ring(n_x, 1))
    down = lax.ppermute(top, "tx", ring(n_x, -1))
    pt, wt, left, right = turn(pressure, melt_rate, elevation, ks_field)
    above, below, left, right = halo_rows(up, down, top, bottom, left, right)
    from_left = lax.ppermute(right, "ty", ring(n_y, 1))
    from_right = lax.ppermute(left, "ty", ring(n_y, -1))
    forecast, rounded = run_steps(
        pt, wt, elevation, ks_field, above, below, from_left, from_right
    )
    picked = picks(code, forecast, inside)

    def send(v, by, swap=False):
        to = [(i, (i + 2 * (by if i % 2 == 0 else -by)) % n_m) for i in range(n_m)]
        return lax.ppermute(v, "mem", [(i, i ^ 1) for i in range(n_m)] if swap else to)

    block = n_obs // (n_x * n_y)
    tile = tile_x * n_y + tile_y
    mine = jnp.concatenate(
        [
            (obs_value[:, None] + obs_error[:, None] * perturbation).T,
            jnp.broadcast_to(obs_error[None], (8, block)),
        ]
    )
    mine = lax.dynamic_update_slice(jnp.zeros((16, n_obs), F32), mine, (0, tile * block))
    line = jnp.concatenate([picked, mine])
    a, b = send(rounded, 1), send(rounded, -1)
    own_far = send(rounded, 0, True)
    for axis, n in (("ty", n_y), ("tx", n_x)):
        bit = 1
        while bit < n:
            line = line + lax.ppermute(line, axis, [(i, i ^ bit) for i in range(n)])
            if bit == 1 and axis == "ty":
                line, own_far = lax.optimization_barrier((line, own_far))
            bit *= 2
    observed, target, error = line[0:8], line[8:16], line[16:17]
    innovation = (target - observed) / error
    scaled = observed / error

    scaled, a, b = lax.optimization_barrier((scaled, a, b))
    c = send(a, 1)
    parts = [send(scaled, by) for by in (1, -1, 2)]
    near = jnp.concatenate([scaled] + parts)
    far = send(near, 0, True)
    far, a, b = lax.optimization_barrier((far, a, b))
    a_far, b_far = send(a, 0, True), send(b, 0, True)
    weights = solve_weights(near, far, innovation)
    weights, c, a_far, b_far = lax.optimization_barrier((weights, c, a_far, b_far))
    c_far = send(c, 0, True)
    return update(weights, [rounded, a, b, c, own_far, a_far, b_far, c_far], forecast)


def solution(mesh):
    placed = (
        P("mem", "tx", "ty"),
        P("tx", "ty"),
        P("tx", "ty"),
        P("mem", "tx", "ty"),
        P(),
        P(("tx", "ty")),
        P(("tx", "ty")),
        P(("tx", "ty"), "mem"),
    )
    return jax.shard_map(
        local, mesh=mesh, in_specs=placed, out_specs=P("mem", "tx", "ty"), check_vma=False
    )
```

profile of v0, /device:TPU:1, one launch (start us, length us, event | category | flops | bytes accessed | tf_op | source)
XLA Modules:
  0.0 99.9 jit_solution(12523484355082514223)
XLA Ops:
  0.0 2.8 %ends.1 = (f32[9,8,256]{2,1,0:T(8,128)}, f32[9,8,256]{2,1,0:T(8,128)}, s32[8,128]{1,0:T(8,128)}, f32[8,128]{1,0:T(8,128)}) custom-call(s32[8,128]{1,0:T(8,128)} %bitcast.5, f32[8,256,256]{2,1,0:T(8,128)} %p_in.1, f32[8,256,256]{2,1,0:T(8,128)} %w_in.1, f32[256,256]{1,0:T(8,128)} %e_ref.5, f32[256,256]{1,0:T(8,128)} %k_ref.5), custom_call_target="tpu_custom_call" | custom-call | tf_op jit(solution)/shard_map/ends/pallas_call | solution.py:76
  2.8 2.5 %collective-permute-start = (f32[9,8,256]{2,1,0:T(8,128)}, f32[9,8,256]{2,1,0:T(8,128)S(1)}, u32[]{:S(2)}, u32[]{:S(2)}) collective-permute-start(f32[9,8,256]{2,1,0:T(8,128)} %get-tuple-element.34.bottom_ref), channel_id=1, source_target_pairs={{0,4},{4,8},{8,12},{12,0},{1,5},{5,9},{9,13},{13,1},{2,6},{6,10},{... | collective-permute-start | bytes 221192 | tf_op jit(solution)/shard_map/ppermute | solution.py:537
  5.3 2.2 %collective-permute-start.1 = (f32[9,8,256]{2,1,0:T(8,128)}, f32[9,8,256]{2,1,0:T(8,128)S(1)}, u32[]{:S(2)}, u32[]{:S(2)}) collective-permute-start(f32[9,8,256]{2,1,0:T(8,128)} %get-tuple-element.35.top_ref), channel_id=1, source_target_pairs={{0,12},{4,0},{8,4},{12,8},{1,13},{5,1},{9,5},{13,9},{2,14},{6,2},{... | collective-permute-start | bytes 221192 | tf_op jit(solution)/shard_map/ppermute | solution.py:538
  7.5 0.0 copy-done
  7.5 4.3 %turn.1 = (f32[256,8,256]{2,1,0:T(8,128)}, f32[256,8,256]{2,1,0:T(8,128)}, f32[8,3,8,128]{3,2,1,0:T(8,128)S(1)}, f32[8,3,8,128]{3,2,1,0:T(8,128)S(1)}) custom-call(f32[8,256,256]{2,1,0:T(8,128)} %p_in.1, f32[8,256,256]{2,1,0:T(8,128)} %w_in.1, f32[256,256]{1,0:T(8,128)S(1)} %copy-done, f32[256,256]{1,0:T(8,128)S(1)} %copy-done.1), custom_call_target="tpu_custom_call" | custom-call | flops 10000000 | bytes 9437184 | tf_op jit(solution)/shard_map/turn/pallas_call | solution.py:158
  11.8 0.0 collective-permute-done.up_ref
  11.8 0.0 collective-permute-done.1.down_ref
  11.9 0.1 rows.1
  12.0 1.4 %collective-permute-start.2 = (f32[9,3,8,128]{3,2,1,0:T(8,128)S(1)}, f32[9,3,8,128]{3,2,1,0:T(8,128)S(1)}, u32[]{:S(2)}, u32[]{:S(2)}) collective-permute-start(f32[9,3,8,128]{3,2,1,0:T(8,128)S(1)} %get-tuple-element.40), channel_id=1, source_target_pairs={{0,1},{1,2},{2,3},{3,0},{4,5},{5,6},{6,7},{7,4},{8,9},{9,10},{10,1... | collective-permute-start | bytes 331784 | tf_op jit(solution)/shard_map/ppermute | solution.py:541
  13.3 1.5 %collective-permute-start.3 = (f32[9,3,8,128]{3,2,1,0:T(8,128)S(1)}, f32[9,3,8,128]{3,2,1,0:T(8,128)S(1)}, u32[]{:S(2)}, u32[]{:S(2)}) collective-permute-start(f32[9,3,8,128]{3,2,1,0:T(8,128)S(1)} %get-tuple-element.41), channel_id=1, source_target_pairs={{0,3},{1,0},{2,1},{3,2},{4,7},{5,4},{6,5},{7,6},{8,11},{9,8},{10,9... | collective-permute-start | bytes 331784 | tf_op jit(solution)/shard_map/ppermute | solution.py:542
  14.9 2.1 %collective-permute-done.2.fl_ref = f32[9,3,8,128]{3,2,1,0:T(8,128)S(1)} collective-permute-done((f32[9,3,8,128]{3,2,1,0:T(8,128)S(1)}, f32[9,3,8,128]{3,2,1,0:T(8,128)S(1)}, u32[]{:S(2)}, u32[]{:S(2)}) %collective-permute-start.2) | collective-permute-done | bytes 110624 | tf_op jit(solution)/shard_map/ppermute | solution.py:541
  16.9 0.0 collective-permute-done.3.fr_ref
  17.0 20.1 %steps.1 = (f32[512,8,128]{2,1,0:T(8,128)S(1)}, bf16[256,8,256]{2,1,0:T(8,128)(2,1)S(1)}) custom-call(f32[256,8,256]{2,1,0:T(8,128)} %get-tuple-element.32.pt_in, f32[256,8,256]{2,1,0:T(8,128)} %get-tuple-element.33.wt_in, f32[256,256]{1,0:T(8,128)S(1)} %copy-done, f32[256,256]{1,0:T(8,128)S(1)} %copy-done.1, f32[9,8,256]{2,1,0:T(8,128)S(1)} %get-tuple-element.38.above_ref, ...), custom_call_target="tpu_custom_call" | custom-call | tf_op jit(solution)/shard_map/steps/pallas_call | solution.py:365
  37.1 2.5 %collective-permute-start.5 = (bf16[256,8,256]{2,1,0:T(8,128)(2,1)S(1)}, bf16[256,8,256]{2,1,0:T(8,128)(2,1)}, u32[]{:S(2)}, u32[]{:S(2)}) collective-permute-start(bf16[256,8,256]{2,1,0:T(8,128)(2,1)S(1)} %get-tuple-element.44.refs_0_), channel_id=1, source_target_pairs={{0,16},{16,0},{32,48},{48,32},{64,80},{80,64},{96,112},{112,96},{1... | collective-permute-start | bytes 3145736 | tf_op jit(solution)/shard_map/ppermute | solution.py:550
  39.6 0.0 copy-done.7
  39.6 1.3 %collective-permute-start.10 = (bf16[256,8,256]{2,1,0:T(8,128)(2,1)S(1)}, bf16[256,8,256]{2,1,0:T(8,128)(2,1)}, u32[]{:S(2)}, u32[]{:S(2)}) collective-permute-start(bf16[256,8,256]{2,1,0:T(8,128)(2,1)S(1)} %get-tuple-element.44.refs_0_), channel_id=1, source_target_pairs={{0,96},{16,48},{32,0},{48,80},{64,32},{80,112},{96,64},{112,16},{1... | collective-permute-start | bytes 3145736 | tf_op jit(solution)/shard_map/ppermute | solution.py:550
  40.9 1.5 %collective-permute-start.9 = (bf16[256,8,256]{2,1,0:T(8,128)(2,1)S(1)}, bf16[256,8,256]{2,1,0:T(8,128)(2,1)}, u32[]{:S(2)}, u32[]{:S(2)}) collective-permute-start(bf16[256,8,256]{2,1,0:T(8,128)(2,1)S(1)} %get-tuple-element.44.refs_0_), channel_id=1, source_target_pairs={{0,32},{16,112},{32,64},{48,16},{64,96},{80,48},{96,0},{112,80},{1... | collective-permute-start | bytes 3145736 | tf_op jit(solution)/shard_map/ppermute | solution.py:550
  42.4 0.3 dynamic_update_slice.3
  42.7 2.7 %picks.1 = f32[8,1024]{1,0:T(8,128)S(1)} custom-call(s32[8,128]{1,0:T(8,128)S(1)} %copy-done.4, f32[512,8,128]{2,1,0:T(8,128)S(1)} %get-tuple-element.42.f_ref.refs_8_, f32[8,128]{1,0:T(8,128)S(1)} %copy-done.5), custom_call_target="tpu_custom_call" | custom-call | tf_op jit(solution)/shard_map/picks/pallas_call | solution.py:396
  45.4 1.4 %collective-permute-start.4 = (f32[24,1024]{1,0:T(8,128)S(1)}, f32[24,1024]{1,0:T(8,128)S(1)}, u32[]{:S(2)}, u32[]{:S(2)}) collective-permute-start(f32[24,1024]{1,0:T(8,128)S(1)} %pad_maximum_fusion), channel_id=1, source_target_pairs={{0,1},{1,0},{2,3},{3,2},{4,5},{5,4},{6,7},{7,6},{8,9},{9,8},{10,11... | collective-permute-start | bytes 294920 | tf_op jit(solution)/shard_map/ppermute | solution.py:567
  46.8 3.0 %collective-permute-done.4 = f32[24,1024]{1,0:T(8,128)S(1)} collective-permute-done((f32[24,1024]{1,0:T(8,128)S(1)}, f32[24,1024]{1,0:T(8,128)S(1)}, u32[]{:S(2)}, u32[]{:S(2)}) %collective-permute-start.4) | collective-permute-done | bytes 98336 | tf_op jit(solution)/shard_map/ppermute | solution.py:567
  49.8 0.0 collective-permute-done.5.refs_4_
  49.8 2.7 %collective-permute-start.6 = (f32[24,1024]{1,0:T(8,128)S(1)}, f32[24,1024]{1,0:T(8,128)S(1)}, u32[]{:S(2)}, u32[]{:S(2)}) collective-permute-start(f32[24,1024]{1,0:T(8,128)S(1)} %fusion.1), channel_id=1, source_target_pairs={{0,2},{1,3},{2,0},{3,1},{4,6},{5,7},{6,4},{7,5},{8,10},{9,11},{10,... | collective-permute-start | bytes 294920 | tf_op jit(solution)/shard_map/ppermute | solution.py:567
  52.5 2.4 %collective-permute-done.6 = f32[24,1024]{1,0:T(8,128)S(1)} collective-permute-done((f32[24,1024]{1,0:T(8,128)S(1)}, f32[24,1024]{1,0:T(8,128)S(1)}, u32[]{:S(2)}, u32[]{:S(2)}) %collective-permute-start.6) | collective-permute-done | bytes 98336 | tf_op jit(solution)/shard_map/ppermute | solution.py:567
  54.9 0.1 collective-permute-start.7
  55.0 3.9 %collective-permute-done.7 = f32[24,1024]{1,0:T(8,128)S(1)} collective-permute-done((f32[24,1024]{1,0:T(8,128)S(1)}, f32[24,1024]{1,0:T(8,128)S(1)}, u32[]{:S(2)}, u32[]{:S(2)}) %collective-permute-start.7) | collective-permute-done | bytes 98336 | tf_op jit(solution)/shard_map/ppermute | solution.py:567
  58.9 1.6 %collective-permute-start.8 = (f32[24,1024]{1,0:T(8,128)S(1)}, f32[24,1024]{1,0:T(8,128)S(1)}, u32[]{:S(2)}, u32[]{:S(2)}) collective-permute-start(f32[24,1024]{1,0:T(8,128)S(1)} %add.32), channel_id=1, source_target_pairs={{0,8},{4,12},{8,0},{12,4},{1,9},{5,13},{9,1},{13,5},{2,10},{6,14},... | collective-permute-start | bytes 294920 | tf_op jit(solution)/shard_map/ppermute | solution.py:567
  60.4 3.5 %collective-permute-done.8 = f32[24,1024]{1,0:T(8,128)S(1)} collective-permute-done((f32[24,1024]{1,0:T(8,128)S(1)}, f32[24,1024]{1,0:T(8,128)S(1)}, u32[]{:S(2)}, u32[]{:S(2)}) %collective-permute-start.8) | collective-permute-done | bytes 98336 | tf_op jit(solution)/shard_map/ppermute | solution.py:567
  64.0 0.0 collective-permute-done.10.refs_2_
  64.0 1.5 %collective-permute-done.9.refs_1_ = bf16[256,8,256]{2,1,0:T(8,128)(2,1)} collective-permute-done((bf16[256,8,256]{2,1,0:T(8,128)(2,1)S(1)}, bf16[256,8,256]{2,1,0:T(8,128)(2,1)}, u32[]{:S(2)}, u32[]{:S(2)}) %collective-permute-start.9) | collective-permute-done | bytes 1048608 | tf_op jit(solution)/shard_map/ppermute | solution.py:550
  65.5 2.6 %collective-permute-start.13 = (f32[8,1024]{1,0:T(8,128)S(1)}, f32[8,1024]{1,0:T(8,128)S(1)}, u32[]{:S(2)}, u32[]{:S(2)}) collective-permute-start(f32[8,1024]{1,0:T(8,128)S(1)} %get-tuple-element.46), channel_id=1, source_target_pairs={{0,64},{16,80},{32,96},{48,112},{64,0},{80,16},{96,32},{112,48},{1... | collective-permute-start | bytes 98312 | tf_op jit(solution)/shard_map/ppermute | solution.py:550
  68.1 1.0 %collective-permute-start.12 = (f32[8,1024]{1,0:T(8,128)S(1)}, f32[8,1024]{1,0:T(8,128)S(1)}, u32[]{:S(2)}, u32[]{:S(2)}) collective-permute-start(f32[8,1024]{1,0:T(8,128)S(1)} %get-tuple-element.46), channel_id=1, source_target_pairs={{0,96},{16,48},{32,0},{48,80},{64,32},{80,112},{96,64},{112,16},{1... | collective-permute-start | bytes 98312 | tf_op jit(solution)/shard_map/ppermute | solution.py:550
  69.1 1.7 %collective-permute-start.11 = (f32[8,1024]{1,0:T(8,128)S(1)}, f32[8,1024]{1,0:T(8,128)S(1)}, u32[]{:S(2)}, u32[]{:S(2)}) collective-permute-start(f32[8,1024]{1,0:T(8,128)S(1)} %get-tuple-element.46), channel_id=1, source_target_pairs={{0,32},{16,112},{32,64},{48,16},{64,96},{80,48},{96,0},{112,80},{1... | collective-permute-start | bytes 98312 | tf_op jit(solution)/shard_map/ppermute | solution.py:550
  70.8 1.4 %collective-permute-done.11 = f32[8,1024]{1,0:T(8,128)S(1)} collective-permute-done((f32[8,1024]{1,0:T(8,128)S(1)}, f32[8,1024]{1,0:T(8,128)S(1)}, u32[]{:S(2)}, u32[]{:S(2)}) %collective-permute-start.11) | collective-permute-done | bytes 32800 | tf_op jit(solution)/shard_map/ppermute | solution.py:550
  72.2 0.0 collective-permute-done.12
  72.2 0.0 collective-permute-done.13
  72.2 4.3 %collective-permute-start.14 = (f32[32,1024]{1,0:T(8,128)S(1)}, f32[32,1024]{1,0:T(8,128)S(1)}, u32[]{:S(2)}, u32[]{:S(2)}) collective-permute-start(f32[32,1024]{1,0:T(8,128)S(1)} %constant_dynamic-update-slice_fusion.near_ref), channel_id=1, source_target_pairs={{0,16},{16,0},{32,48},{48,32},{64,80},{80,64},{96,112},{112,96},{1... | collective-permute-start | bytes 393224 | tf_op jit(solution)/shard_map/ppermute | solution.py:550
  76.5 0.0 collective-permute-start.15
  76.5 0.9 collective-permute-done.14.far_ref
  77.5 0.4 collective-permute-start.16
  77.8 0.1 collective-permute-start.17
  78.0 2.4 %weights.1.w_ref = f32[8,64]{1,0:T(8,128)S(1)} custom-call(f32[32,1024]{1,0:T(8,128)S(1)} %constant_dynamic-update-slice_fusion.near_ref, f32[32,1024]{1,0:T(8,128)S(1)} %collective-permute-done.14.far_ref, f32[8,1024]{1,0:T(8,128)S(1)} %get-tuple-element.57.innovation_ref), custom_call_target="tpu_custom_call" | custom-call | tf_op jit(solution)/shard_map/weights/pallas_call | solution.py:465
  80.3 10.3 %collective-permute-done.15.refs_3_ = bf16[256,8,256]{2,1,0:T(8,128)(2,1)S(1)} collective-permute-done((bf16[256,8,256]{2,1,0:T(8,128)(2,1)}, bf16[256,8,256]{2,1,0:T(8,128)(2,1)S(1)}, u32[]{:S(2)}, u32[]{:S(2)}) %collective-permute-start.15) | collective-permute-done | bytes 1048608 | tf_op jit(solution)/shard_map/ppermute | solution.py:550
  90.6 0.0 collective-permute-done.16.refs_5_
  90.6 0.0 collective-permute-done.17.refs_6_
  90.6 2.1 %collective-permute-start.18 = (bf16[256,8,256]{2,1,0:T(8,128)(2,1)S(1)}, bf16[256,8,256]{2,1,0:T(8,128)(2,1)S(1)}, u32[]{:S(2)}, u32[]{:S(2)}) collective-permute-start(bf16[256,8,256]{2,1,0:T(8,128)(2,1)S(1)} %collective-permute-done.15.refs_3_), channel_id=1, source_target_pairs={{0,16},{16,0},{32,48},{48,32},{64,80},{80,64},{96,112},{112,96},{1... | collective-permute-start | bytes 3145736 | tf_op jit(solution)/shard_map/ppermute | solution.py:550
  92.8 2.3 %collective-permute-done.18.refs_7_ = bf16[256,8,256]{2,1,0:T(8,128)(2,1)S(1)} collective-permute-done((bf16[256,8,256]{2,1,0:T(8,128)(2,1)S(1)}, bf16[256,8,256]{2,1,0:T(8,128)(2,1)S(1)}, u32[]{:S(2)}, u32[]{:S(2)}) %collective-permute-start.18) | collective-permute-done | bytes 1048608 | tf_op jit(solution)/shard_map/ppermute | solution.py:550
  95.1 4.8 %update.1 = f32[8,256,256]{2,1,0:T(8,128)} custom-call(f32[8,64]{1,0:T(8,128)S(1)} %weights.1.w_ref, bf16[256,8,256]{2,1,0:T(8,128)(2,1)S(1)} %get-tuple-element.44.refs_0_, bf16[256,8,256]{2,1,0:T(8,128)(2,1)} %collective-permute-done.9.refs_1_, bf16[256,8,256]{2,1,0:T(8,128)(2,1)} %collective-permute-done.10.refs_2_, ...), custom_call_target="tpu_custom_call" | custom-call | tf_op jit(solution)/shard_map/update/pallas_call | solution.py:511
  (31 shorter events, 0.1 us)
Async XLA Ops:
  0.0 7.5 %copy-start = (f32[256,256]{1,0:T(8,128)S(1)}, f32[256,256]{1,0:T(8,128)}, u32[]{:S(2)}) copy-start(f32[256,256]{1,0:T(8,128)} %e_ref.5) | copy-start | bytes 786436
  0.0 7.5 %copy-start.1 = (f32[256,256]{1,0:T(8,128)S(1)}, f32[256,256]{1,0:T(8,128)}, u32[]{:S(2)}) copy-start(f32[256,256]{1,0:T(8,128)} %k_ref.5) | copy-start | bytes 786436
  2.8 9.1 %collective-permute-start = (f32[9,8,256]{2,1,0:T(8,128)}, f32[9,8,256]{2,1,0:T(8,128)S(1)}, u32[]{:S(2)}, u32[]{:S(2)}) collective-permute-start(f32[9,8,256]{2,1,0:T(8,128)} %get-tuple-element.34.bottom_ref), channel_id=1, source_target_pairs={{0,4},{4,8},{8,12},{12,0},{1,5},{5,9},{9,13},{13,1},{2,6},{6,10},{... | collective-permute-start | bytes 221192 | tf_op jit(solution)/shard_map/ppermute | solution.py:537
  5.3 6.5 %copy-start.2 = (f32[9,8,256]{2,1,0:T(8,128)S(1)}, f32[9,8,256]{2,1,0:T(8,128)}, u32[]{:S(2)}) copy-start(f32[9,8,256]{2,1,0:T(8,128)} %get-tuple-element.35.top_ref) | copy-start | bytes 221188
  5.3 6.6 %copy-start.3 = (f32[9,8,256]{2,1,0:T(8,128)S(1)}, f32[9,8,256]{2,1,0:T(8,128)}, u32[]{:S(2)}) copy-start(f32[9,8,256]{2,1,0:T(8,128)} %get-tuple-element.34.bottom_ref) | copy-start | bytes 221188
  5.3 6.5 %collective-permute-start.1 = (f32[9,8,256]{2,1,0:T(8,128)}, f32[9,8,256]{2,1,0:T(8,128)S(1)}, u32[]{:S(2)}, u32[]{:S(2)}) collective-permute-start(f32[9,8,256]{2,1,0:T(8,128)} %get-tuple-element.35.top_ref), channel_id=1, source_target_pairs={{0,12},{4,0},{8,4},{12,8},{1,13},{5,1},{9,5},{13,9},{2,14},{6,2},{... | collective-permute-start | bytes 221192 | tf_op jit(solution)/shard_map/ppermute | solution.py:538
  12.0 4.9 %collective-permute-start.2 = (f32[9,3,8,128]{3,2,1,0:T(8,128)S(1)}, f32[9,3,8,128]{3,2,1,0:T(8,128)S(1)}, u32[]{:S(2)}, u32[]{:S(2)}) collective-permute-start(f32[9,3,8,128]{3,2,1,0:T(8,128)S(1)} %get-tuple-element.40), channel_id=1, source_target_pairs={{0,1},{1,2},{2,3},{3,0},{4,5},{5,6},{6,7},{7,4},{8,9},{9,10},{10,1... | collective-permute-start | bytes 331784 | tf_op jit(solution)/shard_map/ppermute | solution.py:541
  13.3 3.6 %collective-permute-start.3 = (f32[9,3,8,128]{3,2,1,0:T(8,128)S(1)}, f32[9,3,8,128]{3,2,1,0:T(8,128)S(1)}, u32[]{:S(2)}, u32[]{:S(2)}) collective-permute-start(f32[9,3,8,128]{3,2,1,0:T(8,128)S(1)} %get-tuple-element.41), channel_id=1, source_target_pairs={{0,3},{1,0},{2,1},{3,2},{4,7},{5,4},{6,5},{7,6},{8,11},{9,8},{10,9... | collective-permute-start | bytes 331784 | tf_op jit(solution)/shard_map/ppermute | solution.py:542
  16.9 22.6 %copy-start.6 = (f32[64,8]{0,1:T(8,128)S(1)}, f32[64,8]{0,1:T(8,128)}, u32[]{:S(2)}) copy-start(f32[64,8]{0,1:T(8,128)} %param.15) | copy-start | bytes 6148
  16.9 22.6 %copy-start.7 = (f32[64]{0:T(128)S(1)}, f32[64]{0:T(128)}, u32[]{:S(2)}) copy-start(f32[64]{0:T(128)} %param.14) | copy-start | bytes 772
  16.9 22.6 %copy-start.8 = (f32[64]{0:T(128)S(1)}, f32[64]{0:T(128)}, u32[]{:S(2)}) copy-start(f32[64]{0:T(128)} %param.13) | copy-start | bytes 772
  17.0 25.7 %copy-start.4 = (s32[8,128]{1,0:T(8,128)S(1)}, s32[8,128]{1,0:T(8,128)}, u32[]{:S(2)}) copy-start(s32[8,128]{1,0:T(8,128)} %get-tuple-element.31.code_ref) | copy-start | bytes 12292
  17.0 25.7 %copy-start.5 = (f32[8,128]{1,0:T(8,128)S(1)}, f32[8,128]{1,0:T(8,128)}, u32[]{:S(2)}) copy-start(f32[8,128]{1,0:T(8,128)} %get-tuple-element.43.inside_ref) | copy-start | bytes 12292
  37.1 12.7 %collective-permute-start.5 = (bf16[256,8,256]{2,1,0:T(8,128)(2,1)S(1)}, bf16[256,8,256]{2,1,0:T(8,128)(2,1)}, u32[]{:S(2)}, u32[]{:S(2)}) collective-permute-start(bf16[256,8,256]{2,1,0:T(8,128)(2,1)S(1)} %get-tuple-element.44.refs_0_), channel_id=1, source_target_pairs={{0,16},{16,0},{32,48},{48,32},{64,80},{80,64},{96,112},{112,96},{1... | collective-permute-start | bytes 3145736 | tf_op jit(solution)/shard_map/ppermute | solution.py:550
  39.6 24.4 %collective-permute-start.10 = (bf16[256,8,256]{2,1,0:T(8,128)(2,1)S(1)}, bf16[256,8,256]{2,1,0:T(8,128)(2,1)}, u32[]{:S(2)}, u32[]{:S(2)}) collective-permute-start(bf16[256,8,256]{2,1,0:T(8,128)(2,1)S(1)} %get-tuple-element.44.refs_0_), channel_id=1, source_target_pairs={{0,96},{16,48},{32,0},{48,80},{64,32},{80,112},{96,64},{112,16},{1... | collective-permute-start | bytes 3145736 | tf_op jit(solution)/shard_map/ppermute | solution.py:550
  40.9 24.6 %collective-permute-start.9 = (bf16[256,8,256]{2,1,0:T(8,128)(2,1)S(1)}, bf16[256,8,256]{2,1,0:T(8,128)(2,1)}, u32[]{:S(2)}, u32[]{:S(2)}) collective-permute-start(bf16[256,8,256]{2,1,0:T(8,128)(2,1)S(1)} %get-tuple-element.44.refs_0_), channel_id=1, source_target_pairs={{0,32},{16,112},{32,64},{48,16},{64,96},{80,48},{96,0},{112,80},{1... | collective-permute-start | bytes 3145736 | tf_op jit(solution)/shard_map/ppermute | solution.py:550
  45.4 4.4 %collective-permute-start.4 = (f32[24,1024]{1,0:T(8,128)S(1)}, f32[24,1024]{1,0:T(8,128)S(1)}, u32[]{:S(2)}, u32[]{:S(2)}) collective-permute-start(f32[24,1024]{1,0:T(8,128)S(1)} %pad_maximum_fusion), channel_id=1, source_target_pairs={{0,1},{1,0},{2,3},{3,2},{4,5},{5,4},{6,7},{7,6},{8,9},{9,8},{10,11... | collective-permute-start | bytes 294920 | tf_op jit(solution)/shard_map/ppermute | solution.py:567
  49.8 5.1 %collective-permute-start.6 = (f32[24,1024]{1,0:T(8,128)S(1)}, f32[24,1024]{1,0:T(8,128)S(1)}, u32[]{:S(2)}, u32[]{:S(2)}) collective-permute-start(f32[24,1024]{1,0:T(8,128)S(1)} %fusion.1), channel_id=1, source_target_pairs={{0,2},{1,3},{2,0},{3,1},{4,6},{5,7},{6,4},{7,5},{8,10},{9,11},{10,... | collective-permute-start | bytes 294920 | tf_op jit(solution)/shard_map/ppermute | solution.py:567
  54.9 3.9 %collective-permute-start.7 = (f32[24,1024]{1,0:T(8,128)S(1)}, f32[24,1024]{1,0:T(8,128)S(1)}, u32[]{:S(2)}, u32[]{:S(2)}) collective-permute-start(f32[24,1024]{1,0:T(8,128)S(1)} %add.31), channel_id=1, source_target_pairs={{0,4},{4,0},{8,12},{12,8},{1,5},{5,1},{9,13},{13,9},{2,6},{6,2},{1... | collective-permute-start | bytes 294920 | tf_op jit(solution)/shard_map/ppermute | solution.py:567
  58.9 5.1 %collective-permute-start.8 = (f32[24,1024]{1,0:T(8,128)S(1)}, f32[24,1024]{1,0:T(8,128)S(1)}, u32[]{:S(2)}, u32[]{:S(2)}) collective-permute-start(f32[24,1024]{1,0:T(8,128)S(1)} %add.32), channel_id=1, source_target_pairs={{0,8},{4,12},{8,0},{12,4},{1,9},{5,13},{9,1},{13,5},{2,10},{6,14},... | collective-permute-start | bytes 294920 | tf_op jit(solution)/shard_map/ppermute | solution.py:567
  65.5 6.7 %collective-permute-start.13 = (f32[8,1024]{1,0:T(8,128)S(1)}, f32[8,1024]{1,0:T(8,128)S(1)}, u32[]{:S(2)}, u32[]{:S(2)}) collective-permute-start(f32[8,1024]{1,0:T(8,128)S(1)} %get-tuple-element.46), channel_id=1, source_target_pairs={{0,64},{16,80},{32,96},{48,112},{64,0},{80,16},{96,32},{112,48},{1... | collective-permute-start | bytes 98312 | tf_op jit(solution)/shard_map/ppermute | solution.py:550
  68.1 4.1 %collective-permute-start.12 = (f32[8,1024]{1,0:T(8,128)S(1)}, f32[8,1024]{1,0:T(8,128)S(1)}, u32[]{:S(2)}, u32[]{:S(2)}) collective-permute-start(f32[8,1024]{1,0:T(8,128)S(1)} %get-tuple-element.46), channel_id=1, source_target_pairs={{0,96},{16,48},{32,0},{48,80},{64,32},{80,112},{96,64},{112,16},{1... | collective-permute-start | bytes 98312 | tf_op jit(solution)/shard_map/ppermute | solution.py:550
  69.1 3.1 %collective-permute-start.11 = (f32[8,1024]{1,0:T(8,128)S(1)}, f32[8,1024]{1,0:T(8,128)S(1)}, u32[]{:S(2)}, u32[]{:S(2)}) collective-permute-start(f32[8,1024]{1,0:T(8,128)S(1)} %get-tuple-element.46), channel_id=1, source_target_pairs={{0,32},{16,112},{32,64},{48,16},{64,96},{80,48},{96,0},{112,80},{1... | collective-permute-start | bytes 98312 | tf_op jit(solution)/shard_map/ppermute | solution.py:550
  72.2 5.3 %collective-permute-start.14 = (f32[32,1024]{1,0:T(8,128)S(1)}, f32[32,1024]{1,0:T(8,128)S(1)}, u32[]{:S(2)}, u32[]{:S(2)}) collective-permute-start(f32[32,1024]{1,0:T(8,128)S(1)} %constant_dynamic-update-slice_fusion.near_ref), channel_id=1, source_target_pairs={{0,16},{16,0},{32,48},{48,32},{64,80},{80,64},{96,112},{112,96},{1... | collective-permute-start | bytes 393224 | tf_op jit(solution)/shard_map/ppermute | solution.py:550
  76.5 14.2 %collective-permute-start.15 = (bf16[256,8,256]{2,1,0:T(8,128)(2,1)}, bf16[256,8,256]{2,1,0:T(8,128)(2,1)S(1)}, u32[]{:S(2)}, u32[]{:S(2)}) collective-permute-start(bf16[256,8,256]{2,1,0:T(8,128)(2,1)} %collective-permute-done.9.refs_1_), channel_id=1, source_target_pairs={{0,32},{16,112},{32,64},{48,16},{64,96},{80,48},{96,0},{112,80},{1... | collective-permute-start | bytes 3145736 | tf_op jit(solution)/shard_map/ppermute | solution.py:550
  77.5 13.2 %collective-permute-start.16 = (bf16[256,8,256]{2,1,0:T(8,128)(2,1)}, bf16[256,8,256]{2,1,0:T(8,128)(2,1)S(1)}, u32[]{:S(2)}, u32[]{:S(2)}) collective-permute-start(bf16[256,8,256]{2,1,0:T(8,128)(2,1)} %collective-permute-done.9.refs_1_), channel_id=1, source_target_pairs={{0,16},{16,0},{32,48},{48,32},{64,80},{80,64},{96,112},{112,96},{1... | collective-permute-start | bytes 3145736 | tf_op jit(solution)/shard_map/ppermute | solution.py:550
  77.8 12.8 %collective-permute-start.17 = (bf16[256,8,256]{2,1,0:T(8,128)(2,1)}, bf16[256,8,256]{2,1,0:T(8,128)(2,1)S(1)}, u32[]{:S(2)}, u32[]{:S(2)}) collective-permute-start(bf16[256,8,256]{2,1,0:T(8,128)(2,1)} %collective-permute-done.10.refs_2_), channel_id=1, source_target_pairs={{0,16},{16,0},{32,48},{48,32},{64,80},{80,64},{96,112},{112,96},{1... | collective-permute-start | bytes 3145736 | tf_op jit(solution)/shard_map/ppermute | solution.py:550
  90.6 4.4 %collective-permute-start.18 = (bf16[256,8,256]{2,1,0:T(8,128)(2,1)S(1)}, bf16[256,8,256]{2,1,0:T(8,128)(2,1)S(1)}, u32[]{:S(2)}, u32[]{:S(2)}) collective-permute-start(bf16[256,8,256]{2,1,0:T(8,128)(2,1)S(1)} %collective-permute-done.15.refs_3_), channel_id=1, source_target_pairs={{0,16},{16,0},{32,48},{48,32},{64,80},{80,64},{96,112},{112,96},{1... | collective-permute-start | bytes 3145736 | tf_op jit(solution)/shard_map/ppermute | solution.py:550
where the time goes:
time: 100 us; the launch traced here: 99.9 us
  Pallas kernels  37.2 us (37%)
  waiting for transfers between devices  31.2 us (31%)
  starting transfers between devices  30.9 us (31%)
    pallas_call x1, Pallas kernels, run_steps(): pl.pallas_call(steps_kernel, in_specs=[HBM_SPEC] * 2 + [VMEM_SPEC] * 6, o...  20.1 us
    ppermute x11, starting transfers between devices, send(): lax.ppermute(v, 'mem', [(i, i ^ 1) for i in range(n_m)] if swap else to)  17.5 us
    ppermute x11, waiting for transfers between devices, send(): lax.ppermute(v, 'mem', [(i, i ^ 1) for i in range(n_m)] if swap else to)  16.4 us
    ppermute x4, waiting for transfers between devices, local(): line = line + lax.ppermute(line, axis, [(i, i ^ bit) for i in range(n)])  12.7 us
    ppermute x4, starting transfers between devices, local(): line = line + lax.ppermute(line, axis, [(i, i ^ bit) for i in range(n)])  5.76 us
    pallas_call x1, Pallas kernels, update(): pl.pallas_call(update_kernel, in_specs=[VMEM_SPEC] * (len(pieces) + 2), o...  4.82 us
    pallas_call x1, Pallas kernels, turn(): pl.pallas_call(turn_kernel, in_specs=[HBM_SPEC] * 2 + [VMEM_SPEC] * 2, ou...  4.29 us
    pallas_call x1, Pallas kernels, ends(): pl.pallas_call(ends_kernel, in_specs=[VMEM_SPEC] + [HBM_SPEC] * 2 + [VMEM...  2.76 us
  transfers between devices with their start and end apart: 19, of which 10 were waited for; matrix products, arithmetic and copies ran while one was open for 0% of the time, Pallas kernels for 9%

commit v1 on v0

--- a/solution.py
+++ b/solution.py
@@ -224,18 +224,20 @@
 
 
 def steps_kernel(
-    pt_in, wt_in, e_ref, k_ref, above_ref, below_ref, fl_ref, fr_ref,
-    out_ref, round_ref,
-    p0, p1, w_s, fy_s, sum_s, e_s, er_s, k_s, kr_s, sems,
+    half, pt_in, wt_in, e_ref, k_ref, outer_ref, fl_ref, fr_ref, *refs,
 ):
-    size_x = pt_in.shape[0]
+    (
+        out_ref, round_ref, p0, p1, w_s, fy_s, sum_s, e_s, er_s, k_s, kr_s, sems,
+    ) = refs[half:]
+    size_x = pt_in.shape[0] // 2
     lane = lanes()
     is_first, is_last = lane == 0, lane == 127
-    groups = size_x // GROUP
+    groups = 2 * size_x // GROUP
     blocks = size_x // 8 + 2
-    inner = (pl.ds(9, size_x), slice(None), pl.ds(0, 256))
+    first, start = half * (size_x - W), 9 - half * W
+    inner = (pl.ds(start, size_x + W), slice(None), pl.ds(0, 256))
     loads = [
-        pltpu.make_async_copy(src, dst.at[inner], sems.at[i])
+        pltpu.make_async_copy(src.at[pl.ds(first, size_x + W)], dst.at[inner], sems.at[i])
         for i, (src, dst) in enumerate(((pt_in, p0), (wt_in, w_s)))
     ]
     for c in loads:
@@ -256,31 +258,48 @@
                 is_last, rolled[(t + 1) % 3], rolled[t]
             )
 
-    def unpack_group(g, _):
+    def columns(y, g, r):
+        for f, dst in ((0, p0), (1, w_s)):
+            dst[y + 1, :, 256:384] = halo(g, f, r)
+
+    def fields(at, g, q, rows):
+        for base, ref, factor, here, shifted in (
+            (0, e_ref, 0.5, e_s, er_s), (4, k_ref, 0.25, k_s, kr_s),
+        ):
+            v = [ref[rows, 128 * t : 128 * t + 128] * F32(factor) for t in range(2)]
+            spread(at, v + [halo(g, 2, base + q)], here, shifted)
+
+    per = GROUP // 8
+
+    def unpack_group(i, _):
+        g = half * (groups // 2) + i
         for r in range(GROUP):
-            for f, dst in ((0, p0), (1, w_s)):
-                dst[g * GROUP + r + 9, :, 256:384] = halo(g, f, r)
-        for q in range(GROUP // 8):
+            columns(i * GROUP + r + 8, g, r)
+        for q in range(per):
             rows = pl.ds(pl.multiple_of(g * GROUP + 8 * q, 8), 8)
-            for base, ref, factor, here, shifted in (
-                (0, e_ref, 0.5, e_s, er_s), (4, k_ref, 0.25, k_s, kr_s),
-            ):
-                v = [ref[rows, 128 * t : 128 * t + 128] * F32(factor) for t in range(2)]
-                spread(g * (GROUP // 8) + q + 1, v + [halo(g, 2, base + q)], here, shifted)
+            fields(i * per + q + 1, g, q, rows)
         return 0
 
-    lax.fori_loop(0, groups, unpack_group, 0)
-    for r in range(2 * W):
-        ref, y = (above_ref, 4 + r) if r < W else (below_ref, size_x + 4 + r)
+    lax.fori_loop(0, groups // 2, unpack_group, 0)
+    for r in range(W):
+        if half:
+            columns(4 + r, groups // 2 - 1, GROUP - W + r)
+        else:
+            columns(size_x + 8 + r, groups // 2, r)
+    if half:
+        fields(0, groups // 2 - 1, per - 1, slice(size_x - 8, size_x))
+    else:
+        fields(blocks - 1, groups // 2, 0, slice(size_x, size_x + 8))
+    for r in range(W):
+        y = size_x + 8 + r if half else 4 + r
         for f, dst in ((0, p0), (1, w_s)):
-            dst[y + 1, :, 0:256] = ref[f * W + r % W]
-            dst[y + 1, :, 256:384] = halo(groups, f, r)
+            dst[y + 1, :, 0:256] = outer_ref[f * W + r]
+        columns(y, groups, half * W + r)
     for base, here, shifted in ((0, e_s, er_s), (4, k_s, kr_s)):
         edge = pltpu.roll(halo(groups, 2, base), 4, 0)
-        for at, ref, up in ((0, above_ref, base == 0), (blocks - 1, below_ref, base == 4)):
-            v = ref[2 * W]
-            v = pltpu.roll(v, 4, 0) if up else v
-            spread(at, [v[:, 0:128], v[:, 128:256], edge], here, shifted)
+        v = outer_ref[2 * W]
+        v = pltpu.roll(v, 4, 0) if (base == 0) != bool(half) else v
+        spread((blocks - 1) * half, [v[:, 0:128], v[:, 128:256], edge], here, shifted)
 
     one, none = F32(1), F32(0)
 
@@ -350,30 +369,33 @@
         x = pl.multiple_of(i * 8, 8)
         for u in range(8):
             row = last[x + 9 + u, :, 0:256] * F32(2)
-            out_ref[2 * x + 2 * u] = row[:, 0:128]
-            out_ref[2 * x + 2 * u + 1] = row[:, 128:256]
+            to = 2 * (half * size_x + x + u)
+            out_ref[to] = row[:, 0:128]
+            out_ref[to + 1] = row[:, 128:256]
             round_ref[x + u] = row.astype(BF16)
         return 0
 
     lax.fori_loop(0, size_x // 8, leave, 0)
 
 
-def run_steps(pt, wt, e, k, above, below, from_left, from_right):
+def run_steps(half, pt, wt, e, k, outer, from_left, from_right, *before):
     size_x, members, size_y = pt.shape
-    tile = pltpu.VMEM((size_x + 17, members, size_y + 128), F32)
-    flat = pltpu.VMEM((size_x // 8 + 2, 8, size_y + 128), F32)
+    rows = size_x // 2
+    tile = pltpu.VMEM((rows + 17, members, size_y + 128), F32)
+    flat = pltpu.VMEM((rows // 8 + 2, 8, size_y + 128), F32)
     return pl.pallas_call(
-        steps_kernel,
-        in_specs=[HBM_SPEC] * 2 + [VMEM_SPEC] * 6,
+        functools.partial(steps_kernel, half),
+        in_specs=[HBM_SPEC] * 2 + [VMEM_SPEC] * (5 + half),
         out_specs=[VMEM_SPEC] * 2,
         scratch_shapes=[tile] * 5 + [flat] * 4 + [pltpu.SemaphoreType.DMA((2,))],
         out_shape=[
             jax.ShapeDtypeStruct((size_x * (size_y // 128), members, 128), F32),
-            jax.ShapeDtypeStruct((size_x, members, size_y), BF16),
+            jax.ShapeDtypeStruct((rows, members, size_y), BF16),
         ],
+        input_output_aliases={7: 0} if half else {},
         compiler_params=pltpu.CompilerParams(vmem_limit_bytes=50 * 2**20),
         name="steps",
-    )(pt, wt, e, k, above, below, from_left, from_right)
+    )(pt, wt, e, k, outer, from_left, from_right, *before)
 
 
 def pick_kernel(code_ref, f_ref, inside_ref, pick_ref):
@@ -479,35 +501,37 @@
 def update_kernel(w_ref, *refs):
     pieces, (f_ref, out_ref, row_s, done_s, sems) = refs[:-5], refs[-5:]
     step = row_s.shape[0]
+    count = pieces[0].shape[0] // step
     w = w_ref[...].astype(BF16)
 
     def leave(g):
         at = pl.ds(pl.multiple_of(g * step, step), step)
         return pltpu.make_async_copy(done_s.at[:, at, :], out_ref.at[:, at, :], sems.at[g])
 
-    def chunk(g, _):
-        x = g * step
+    def chunk(half, i, _):
+        g = half * count + i
         for r in range(step):
-            rows = jnp.concatenate([v[x + r].astype(F32) for v in pieces], axis=0).astype(BF16)
+            parts = [v[i * step + r].astype(F32) for v in pieces[half::2]]
+            rows = jnp.concatenate(parts, axis=0).astype(BF16)
             shift = jnp.dot(w, rows, preferred_element_type=F32)
             for t in range(2):
                 cols = slice(128 * t, 128 * t + 128)
-                row_s[r, :, cols] = f_ref[2 * (x + r) + t] + shift[:, cols]
-        at = pl.ds(pl.multiple_of(x, step), step)
+                row_s[r, :, cols] = f_ref[2 * (g * step + r) + t] + shift[:, cols]
+        at = pl.ds(pl.multiple_of(g * step, step), step)
         done_s[:, at, :] = jnp.swapaxes(row_s[...], 0, 1)
         leave(g).start()
         return 0
 
-    count = pieces[0].shape[0] // step
-    lax.fori_loop(0, count, chunk, 0)
-    for g in range(count):
+    for half in range(2):
+        lax.fori_loop(0, count, functools.partial(chunk, half), 0)
+    for g in range(2 * count):
         leave(g).wait()
 
 
 def update(weights, pieces, forecast):
-    size_x, members, size_y = pieces[0].shape
+    rows, members, size_y = pieces[0].shape
     step = 32
-    whole = (members, size_x, size_y)
+    whole = (members, 2 * rows, size_y)
     return pl.pallas_call(
         update_kernel,
         in_specs=[VMEM_SPEC] * (len(pieces) + 2),
@@ -516,7 +540,7 @@
         scratch_shapes=[
             pltpu.VMEM((step, members, size_y), F32),
             pltpu.VMEM(whole, F32),
-            pltpu.SemaphoreType.DMA((size_x // step,)),
+            pltpu.SemaphoreType.DMA((2 * rows // step,)),
         ],
         compiler_params=pltpu.CompilerParams(vmem_limit_bytes=8 * 2**20),
         name="update",
@@ -540,14 +564,18 @@
     above, below, left, right = halo_rows(up, down, top, bottom, left, right)
     from_left = lax.ppermute(right, "ty", ring(n_y, 1))
     from_right = lax.ppermute(left, "ty", ring(n_y, -1))
-    forecast, rounded = run_steps(
-        pt, wt, elevation, ks_field, above, below, from_left, from_right
-    )
-    picked = picks(code, forecast, inside)
 
     def send(v, by, swap=False):
         to = [(i, (i + 2 * (by if i % 2 == 0 else -by)) % n_m) for i in range(n_m)]
         return lax.ppermute(v, "mem", [(i, i ^ 1) for i in range(n_m)] if swap else to)
+
+    columns = (from_left, from_right)
+    forecast, low = run_steps(0, pt, wt, elevation, ks_field, above, *columns)
+    a0, b0 = send(low, 1), send(low, -1)
+    forecast, high = run_steps(1, pt, wt, elevation, ks_field, below, *columns, forecast)
+    a1, b1 = send(high, 1), send(high, -1)
+    own0, own1 = send(low, 0, True), send(high, 0, True)
+    picked = picks(code, forecast, inside)
 
     block = n_obs // (n_x * n_y)
     tile = tile_x * n_y + tile_y
@@ -559,30 +587,35 @@
     )
     mine = lax.dynamic_update_slice(jnp.zeros((16, n_obs), F32), mine, (0, tile * block))
     line = jnp.concatenate([picked, mine])
-    a, b = send(rounded, 1), send(rounded, -1)
-    own_far = send(rounded, 0, True)
-    for axis, n in (("ty", n_y), ("tx", n_x)):
-        bit = 1
-        while bit < n:
-            line = line + lax.ppermute(line, axis, [(i, i ^ bit) for i in range(n)])
-            if bit == 1 and axis == "ty":
-                line, own_far = lax.optimization_barrier((line, own_far))
-            bit *= 2
+    steps = [("ty", 1), ("ty", 2), ("tx", 1), ("tx", 2)]
+    for n, (axis, bit) in enumerate(steps):
+        line = line + lax.ppermute(line, axis, [(i, i ^ bit) for i in range(lax.axis_size(axis))])
+        if n == 0:
+            line, a0, b0, own0, own1 = lax.optimization_barrier((line, a0, b0, own0, own1))
+            c0 = send(a0, 1)
+        if n == 1:
+            line, a0, b0 = lax.optimization_barrier((line, a0, b0))
+            a0_far, b0_far = send(a0, 0, True), send(b0, 0, True)
     observed, target, error = line[0:8], line[8:16], line[16:17]
     innovation = (target - observed) / error
     scaled = observed / error
 
-    scaled, a, b = lax.optimization_barrier((scaled, a, b))
-    c = send(a, 1)
+    scaled, a1, b1, c0 = lax.optimization_barrier((scaled, a1, b1, c0))
+    c1 = send(a1, 1)
     parts = [send(scaled, by) for by in (1, -1, 2)]
     near = jnp.concatenate([scaled] + parts)
+    c0_far = send(c0, 0, True)
     far = send(near, 0, True)
-    far, a, b = lax.optimization_barrier((far, a, b))
-    a_far, b_far = send(a, 0, True), send(b, 0, True)
+    far, a1, b1 = lax.optimization_barrier((far, a1, b1))
+    a1_far, b1_far = send(a1, 0, True), send(b1, 0, True)
     weights = solve_weights(near, far, innovation)
-    weights, c, a_far, b_far = lax.optimization_barrier((weights, c, a_far, b_far))
-    c_far = send(c, 0, True)
-    return update(weights, [rounded, a, b, c, own_far, a_far, b_far, c_far], forecast)
+    weights, c1, a1_far, b1_far = lax.optimization_barrier((weights, c1, a1_far, b1_far))
+    c1_far = send(c1, 0, True)
+    pieces = [
+        low, high, a0, a1, b0, b1, c0, c1,
+        own0, own1, a0_far, a1_far, b0_far, b1_far, c0_far, c1_far,
+    ]
+    return update(weights, pieces, forecast)
 
 
 def solution(mesh):

time: 100 us -> 103 us (1.030)
  waiting for transfers between devices: 31.2 us -> 25.4 us
  starting transfers between devices: 30.9 us -> 35.8 us
  Pallas kernels: 37.2 us -> 40.6 us
    ppermute x11 -> x18, waiting for transfers between devices: 16.4 us -> 10.1 us  [send(): lax.ppermute(v, 'mem', [(i, i ^ 1) for i in range(n_m)] if swap else to)]
    ppermute x11 -> x18, starting transfers between devices: 17.5 us -> 22.4 us  [send(): lax.ppermute(v, 'mem', [(i, i ^ 1) for i in range(n_m)] if swap else to)]
    pallas_call x1 -> x2, Pallas kernels: 20.1 us -> 23.8 us  [run_steps(): pl.pallas_call(functools.partial(steps_kernel, half), in_specs=[HBM_SPEC]...]
  transfers between devices with their start and end apart: 19 -> 26, of which waited for: 10 -> 11; matrix products, arithmetic and copies ran while one was open for 0% -> 0% of each run, Pallas kernels for 9% -> 21%
where the time goes in v1:
time: 103 us
  Pallas kernels  40.6 us (39%)
  starting transfers between devices  35.8 us (35%)
  waiting for transfers between devices  25.4 us (25%)
    pallas_call x2, Pallas kernels, run_steps(): pl.pallas_call(functools.partial(steps_kernel, half), in_specs=[HBM_SPEC]...  23.8 us
    ppermute x18, starting transfers between devices, send(): lax.ppermute(v, 'mem', [(i, i ^ 1) for i in range(n_m)] if swap else to)  22.4 us
    ppermute x4, waiting for transfers between devices, local(): lax.ppermute(line, axis, [(i, i ^ bit) for i in range(lax.axis_size(axis))])  13.3 us
    ppermute x18, waiting for transfers between devices, send(): lax.ppermute(v, 'mem', [(i, i ^ 1) for i in range(n_m)] if swap else to)  10.1 us
    ppermute x4, starting transfers between devices, local(): lax.ppermute(line, axis, [(i, i ^ bit) for i in range(lax.axis_size(axis))])  5.73 us
    pallas_call x1, Pallas kernels, update(): pl.pallas_call(update_kernel, in_specs=[VMEM_SPEC] * (len(pieces) + 2), o...  4.53 us
    pallas_call x1, Pallas kernels, turn(): pl.pallas_call(turn_kernel, in_specs=[HBM_SPEC] * 2 + [VMEM_SPEC] * 2, ou...  4.27 us
    pallas_call x1, Pallas kernels, ends(): pl.pallas_call(ends_kernel, in_specs=[VMEM_SPEC] + [HBM_SPEC] * 2 + [VMEM...  2.77 us
  transfers between devices with their start and end apart: 26, of which 11 were waited for; matrix products, arithmetic and copies ran while one was open for 0% of the time, Pallas kernels for 21%

profile of v1, /device:TPU:1, one launch (start us, length us, event | category | flops | bytes accessed | tf_op | source)
XLA Modules:
  0.0 102.6 jit_solution(7721687993950478957)
XLA Ops:
  0.0 2.8 %ends.1 = (f32[9,8,256]{2,1,0:T(8,128)}, f32[9,8,256]{2,1,0:T(8,128)}, s32[8,128]{1,0:T(8,128)}, f32[8,128]{1,0:T(8,128)}) custom-call(s32[8,128]{1,0:T(8,128)} %bitcast.5, f32[8,256,256]{2,1,0:T(8,128)} %p_in.1, f32[8,256,256]{2,1,0:T(8,128)} %w_in.1, f32[256,256]{1,0:T(8,128)} %e_ref.7, f32[256,256]{1,0:T(8,128)} %k_ref.7), custom_call_target="tpu_custom_call" | custom-call | tf_op jit(solution)/shard_map/ends/pallas_call | solution.py:76
  2.8 2.5 %collective-permute-start = (f32[9,8,256]{2,1,0:T(8,128)}, f32[9,8,256]{2,1,0:T(8,128)S(1)}, u32[]{:S(2)}, u32[]{:S(2)}) collective-permute-start(f32[9,8,256]{2,1,0:T(8,128)} %get-tuple-element.43.bottom_ref), channel_id=1, source_target_pairs={{0,4},{4,8},{8,12},{12,0},{1,5},{5,9},{9,13},{13,1},{2,6},{6,10},{... | collective-permute-start | bytes 221192 | tf_op jit(solution)/shard_map/ppermute | solution.py:561
  5.3 0.0 copy-start.8
  5.3 2.2 %collective-permute-start.1 = (f32[9,8,256]{2,1,0:T(8,128)}, f32[9,8,256]{2,1,0:T(8,128)S(1)}, u32[]{:S(2)}, u32[]{:S(2)}) collective-permute-start(f32[9,8,256]{2,1,0:T(8,128)} %get-tuple-element.44.top_ref), channel_id=1, source_target_pairs={{0,12},{4,0},{8,4},{12,8},{1,13},{5,1},{9,5},{13,9},{2,14},{6,2},{... | collective-permute-start | bytes 221192 | tf_op jit(solution)/shard_map/ppermute | solution.py:562
  7.6 4.3 %turn.1 = (f32[256,8,256]{2,1,0:T(8,128)}, f32[256,8,256]{2,1,0:T(8,128)}, f32[8,3,8,128]{3,2,1,0:T(8,128)S(1)}, f32[8,3,8,128]{3,2,1,0:T(8,128)S(1)}) custom-call(f32[8,256,256]{2,1,0:T(8,128)} %p_in.1, f32[8,256,256]{2,1,0:T(8,128)} %w_in.1, f32[256,256]{1,0:T(8,128)S(1)} %copy-done, f32[256,256]{1,0:T(8,128)S(1)} %copy-done.1), custom_call_target="tpu_custom_call" | custom-call | flops 10000000 | bytes 9437184 | tf_op jit(solution)/shard_map/turn/pallas_call | solution.py:158
  11.9 0.0 collective-permute-done.up_ref
  11.9 0.1 rows.1
  12.0 1.4 %collective-permute-start.2 = (f32[9,3,8,128]{3,2,1,0:T(8,128)S(1)}, f32[9,3,8,128]{3,2,1,0:T(8,128)S(1)}, u32[]{:S(2)}, u32[]{:S(2)}) collective-permute-start(f32[9,3,8,128]{3,2,1,0:T(8,128)S(1)} %get-tuple-element.48), channel_id=1, source_target_pairs={{0,1},{1,2},{2,3},{3,0},{4,5},{5,6},{6,7},{7,4},{8,9},{9,10},{10,1... | collective-permute-start | bytes 331784 | tf_op jit(solution)/shard_map/ppermute | solution.py:565
  13.4 1.5 %collective-permute-start.3 = (f32[9,3,8,128]{3,2,1,0:T(8,128)S(1)}, f32[9,3,8,128]{3,2,1,0:T(8,128)S(1)}, u32[]{:S(2)}, u32[]{:S(2)}) collective-permute-start(f32[9,3,8,128]{3,2,1,0:T(8,128)S(1)} %get-tuple-element.49), channel_id=1, source_target_pairs={{0,3},{1,0},{2,1},{3,2},{4,7},{5,4},{6,5},{7,6},{8,11},{9,8},{10,9... | collective-permute-start | bytes 331784 | tf_op jit(solution)/shard_map/ppermute | solution.py:566
  14.9 2.0 %collective-permute-done.2.fl_ref = f32[9,3,8,128]{3,2,1,0:T(8,128)S(1)} collective-permute-done((f32[9,3,8,128]{3,2,1,0:T(8,128)S(1)}, f32[9,3,8,128]{3,2,1,0:T(8,128)S(1)}, u32[]{:S(2)}, u32[]{:S(2)}) %collective-permute-start.2) | collective-permute-done | bytes 110624 | tf_op jit(solution)/shard_map/ppermute | solution.py:565
  17.0 0.0 collective-permute-done.3.fr_ref
  17.0 11.5 %steps.2 = (f32[512,8,128]{2,1,0:T(8,128)S(1)}, bf16[128,8,256]{2,1,0:T(8,128)(2,1)S(1)}) custom-call(f32[256,8,256]{2,1,0:T(8,128)} %get-tuple-element.41.pt_in, f32[256,8,256]{2,1,0:T(8,128)} %get-tuple-element.42.wt_in, f32[256,256]{1,0:T(8,128)S(1)} %copy-done, f32[256,256]{1,0:T(8,128)S(1)} %copy-done.1, f32[9,8,256]{2,1,0:T(8,128)S(1)} %get-tuple-element.50.outer_ref, ...), custom_call_target="tpu_custom_call" | custom-call | tf_op jit(solution)/shard_map/steps/pallas_call | solution.py:386
  28.5 2.5 %collective-permute-start.7 = (bf16[128,8,256]{2,1,0:T(8,128)(2,1)S(1)}, bf16[128,8,256]{2,1,0:T(8,128)(2,1)}, u32[]{:S(2)}, u32[]{:S(2)}) collective-permute-start(bf16[128,8,256]{2,1,0:T(8,128)(2,1)S(1)} %get-tuple-element.54.refs_0_), channel_id=1, source_target_pairs={{0,16},{16,0},{32,48},{48,32},{64,80},{80,64},{96,112},{112,96},{1... | collective-permute-start | bytes 1572872 | tf_op jit(solution)/shard_map/ppermute | solution.py:570
  30.9 1.2 %collective-permute-start.6 = (bf16[128,8,256]{2,1,0:T(8,128)(2,1)S(1)}, bf16[128,8,256]{2,1,0:T(8,128)(2,1)}, u32[]{:S(2)}, u32[]{:S(2)}) collective-permute-start(bf16[128,8,256]{2,1,0:T(8,128)(2,1)S(1)} %get-tuple-element.54.refs_0_), channel_id=1, source_target_pairs={{0,96},{16,48},{32,0},{48,80},{64,32},{80,112},{96,64},{112,16},{1... | collective-permute-start | bytes 1572872 | tf_op jit(solution)/shard_map/ppermute | solution.py:570
  32.2 1.5 %collective-permute-start.5 = (bf16[128,8,256]{2,1,0:T(8,128)(2,1)S(1)}, bf16[128,8,256]{2,1,0:T(8,128)(2,1)}, u32[]{:S(2)}, u32[]{:S(2)}) collective-permute-start(bf16[128,8,256]{2,1,0:T(8,128)(2,1)S(1)} %get-tuple-element.54.refs_0_), channel_id=1, source_target_pairs={{0,32},{16,112},{32,64},{48,16},{64,96},{80,48},{96,0},{112,80},{1... | collective-permute-start | bytes 1572872 | tf_op jit(solution)/shard_map/ppermute | solution.py:570
  33.6 12.3 %steps.3 = (f32[512,8,128]{2,1,0:T(8,128)S(1)}, bf16[128,8,256]{2,1,0:T(8,128)(2,1)}) custom-call(f32[256,8,256]{2,1,0:T(8,128)} %get-tuple-element.41.pt_in, f32[256,8,256]{2,1,0:T(8,128)} %get-tuple-element.42.wt_in, f32[256,256]{1,0:T(8,128)S(1)} %copy-done, f32[256,256]{1,0:T(8,128)S(1)} %copy-done.1, ...), custom_call_target="tpu_custom_call", output_to_operand_aliasing={{0}: (7, {})} | custom-call | tf_op jit(solution)/shard_map/steps/pallas_call | solution.py:386
  45.9 0.2 collective-permute-start.8
  46.2 0.3 dynamic_update_slice.3
  46.5 2.7 %picks.1 = f32[8,1024]{1,0:T(8,128)S(1)} custom-call(s32[8,128]{1,0:T(8,128)S(1)} %copy-done.4, f32[512,8,128]{2,1,0:T(8,128)S(1)} %get-tuple-element.52.f_ref.refs_16_, f32[8,128]{1,0:T(8,128)S(1)} %copy-done.5), custom_call_target="tpu_custom_call" | custom-call | tf_op jit(solution)/shard_map/picks/pallas_call | solution.py:418
  49.2 1.4 %collective-permute-start.4 = (f32[24,1024]{1,0:T(8,128)S(1)}, f32[24,1024]{1,0:T(8,128)S(1)}, u32[]{:S(2)}, u32[]{:S(2)}) collective-permute-start(f32[24,1024]{1,0:T(8,128)S(1)} %pad_maximum_fusion), channel_id=1, source_target_pairs={{0,1},{1,0},{2,3},{3,2},{4,5},{5,4},{6,7},{7,6},{8,9},{9,8},{10,11... | collective-permute-start | bytes 294920 | tf_op jit(solution)/shard_map/ppermute | solution.py:592
  50.6 2.7 %collective-permute-done.4 = f32[24,1024]{1,0:T(8,128)S(1)} collective-permute-done((f32[24,1024]{1,0:T(8,128)S(1)}, f32[24,1024]{1,0:T(8,128)S(1)}, u32[]{:S(2)}, u32[]{:S(2)}) %collective-permute-start.4) | collective-permute-done | bytes 98336 | tf_op jit(solution)/shard_map/ppermute | solution.py:592
  53.3 0.8 collective-permute-start.13
  54.1 2.6 %collective-permute-start.12 = (bf16[128,8,256]{2,1,0:T(8,128)(2,1)}, bf16[128,8,256]{2,1,0:T(8,128)(2,1)S(1)}, u32[]{:S(2)}, u32[]{:S(2)}) collective-permute-start(bf16[128,8,256]{2,1,0:T(8,128)(2,1)} %get-tuple-element.55.refs_1_), channel_id=1, source_target_pairs={{0,32},{16,112},{32,64},{48,16},{64,96},{80,48},{96,0},{112,80},{1... | collective-permute-start | bytes 1572872 | tf_op jit(solution)/shard_map/ppermute | solution.py:570
  56.7 1.5 %collective-permute-start.14 = (bf16[128,8,256]{2,1,0:T(8,128)(2,1)}, bf16[128,8,256]{2,1,0:T(8,128)(2,1)S(1)}, u32[]{:S(2)}, u32[]{:S(2)}) collective-permute-start(bf16[128,8,256]{2,1,0:T(8,128)(2,1)} %collective-permute-done.5.refs_2_), channel_id=1, source_target_pairs={{0,32},{16,112},{32,64},{48,16},{64,96},{80,48},{96,0},{112,80},{1... | collective-permute-start | bytes 1572872 | tf_op jit(solution)/shard_map/ppermute | solution.py:570
  58.2 2.6 %collective-permute-start.9 = (f32[24,1024]{1,0:T(8,128)S(1)}, f32[24,1024]{1,0:T(8,128)S(1)}, u32[]{:S(2)}, u32[]{:S(2)}) collective-permute-start(f32[24,1024]{1,0:T(8,128)S(1)} %fusion.1), channel_id=1, source_target_pairs={{0,2},{1,3},{2,0},{3,1},{4,6},{5,7},{6,4},{7,5},{8,10},{9,11},{10,... | collective-permute-start | bytes 294920 | tf_op jit(solution)/shard_map/ppermute | solution.py:592
  60.9 3.4 %collective-permute-done.9 = f32[24,1024]{1,0:T(8,128)S(1)} collective-permute-done((f32[24,1024]{1,0:T(8,128)S(1)}, f32[24,1024]{1,0:T(8,128)S(1)}, u32[]{:S(2)}, u32[]{:S(2)}) %collective-permute-start.9) | collective-permute-done | bytes 98336 | tf_op jit(solution)/shard_map/ppermute | solution.py:592
  64.3 0.1 collective-permute-start.10
  64.4 3.7 %collective-permute-done.10 = f32[24,1024]{1,0:T(8,128)S(1)} collective-permute-done((f32[24,1024]{1,0:T(8,128)S(1)}, f32[24,1024]{1,0:T(8,128)S(1)}, u32[]{:S(2)}, u32[]{:S(2)}) %collective-permute-start.10) | collective-permute-done | bytes 98336 | tf_op jit(solution)/shard_map/ppermute | solution.py:592
  68.1 1.6 %collective-permute-start.11 = (f32[24,1024]{1,0:T(8,128)S(1)}, f32[24,1024]{1,0:T(8,128)S(1)}, u32[]{:S(2)}, u32[]{:S(2)}) collective-permute-start(f32[24,1024]{1,0:T(8,128)S(1)} %add.32), channel_id=1, source_target_pairs={{0,8},{4,12},{8,0},{12,4},{1,9},{5,13},{9,1},{13,5},{2,10},{6,14},... | collective-permute-start | bytes 294920 | tf_op jit(solution)/shard_map/ppermute | solution.py:592
  69.8 3.4 %collective-permute-done.11 = f32[24,1024]{1,0:T(8,128)S(1)} collective-permute-done((f32[24,1024]{1,0:T(8,128)S(1)}, f32[24,1024]{1,0:T(8,128)S(1)}, u32[]{:S(2)}, u32[]{:S(2)}) %collective-permute-start.11) | collective-permute-done | bytes 98336 | tf_op jit(solution)/shard_map/ppermute | solution.py:592
  73.3 1.1 %collective-permute-done.14.refs_6_ = bf16[128,8,256]{2,1,0:T(8,128)(2,1)S(1)} collective-permute-done((bf16[128,8,256]{2,1,0:T(8,128)(2,1)}, bf16[128,8,256]{2,1,0:T(8,128)(2,1)S(1)}, u32[]{:S(2)}, u32[]{:S(2)}) %collective-permute-start.14) | collective-permute-done | bytes 524320 | tf_op jit(solution)/shard_map/ppermute | solution.py:570
  74.4 2.5 %collective-permute-start.17 = (f32[8,1024]{1,0:T(8,128)S(1)}, f32[8,1024]{1,0:T(8,128)S(1)}, u32[]{:S(2)}, u32[]{:S(2)}) collective-permute-start(f32[8,1024]{1,0:T(8,128)S(1)} %get-tuple-element.60), channel_id=1, source_target_pairs={{0,64},{16,80},{32,96},{48,112},{64,0},{80,16},{96,32},{112,48},{1... | collective-permute-start | bytes 98312 | tf_op jit(solution)/shard_map/ppermute | solution.py:570
  76.9 1.4 %collective-permute-start.16 = (f32[8,1024]{1,0:T(8,128)S(1)}, f32[8,1024]{1,0:T(8,128)S(1)}, u32[]{:S(2)}, u32[]{:S(2)}) collective-permute-start(f32[8,1024]{1,0:T(8,128)S(1)} %get-tuple-element.60), channel_id=1, source_target_pairs={{0,96},{16,48},{32,0},{48,80},{64,32},{80,112},{96,64},{112,16},{1... | collective-permute-start | bytes 98312 | tf_op jit(solution)/shard_map/ppermute | solution.py:570
  78.3 1.3 %collective-permute-start.15 = (f32[8,1024]{1,0:T(8,128)S(1)}, f32[8,1024]{1,0:T(8,128)S(1)}, u32[]{:S(2)}, u32[]{:S(2)}) collective-permute-start(f32[8,1024]{1,0:T(8,128)S(1)} %get-tuple-element.60), channel_id=1, source_target_pairs={{0,32},{16,112},{32,64},{48,16},{64,96},{80,48},{96,0},{112,80},{1... | collective-permute-start | bytes 98312 | tf_op jit(solution)/shard_map/ppermute | solution.py:570
  79.5 1.8 %collective-permute-done.15 = f32[8,1024]{1,0:T(8,128)S(1)} collective-permute-done((f32[8,1024]{1,0:T(8,128)S(1)}, f32[8,1024]{1,0:T(8,128)S(1)}, u32[]{:S(2)}, u32[]{:S(2)}) %collective-permute-start.15) | collective-permute-done | bytes 32800 | tf_op jit(solution)/shard_map/ppermute | solution.py:570
  81.4 3.7 %collective-permute-start.18 = (f32[32,1024]{1,0:T(8,128)S(1)}, f32[32,1024]{1,0:T(8,128)S(1)}, u32[]{:S(2)}, u32[]{:S(2)}) collective-permute-start(f32[32,1024]{1,0:T(8,128)S(1)} %constant_dynamic-update-slice_fusion.near_ref), channel_id=1, source_target_pairs={{0,16},{16,0},{32,48},{48,32},{64,80},{80,64},{96,112},{112,96},{1... | collective-permute-start | bytes 393224 | tf_op jit(solution)/shard_map/ppermute | solution.py:570
  85.1 1.0 collective-permute-done.18.far_ref
  86.1 0.4 collective-permute-start.20
  86.5 0.1 collective-permute-start.21
  86.6 0.4 collective-permute-start.22
  87.0 0.1 collective-permute-start.23
  87.1 2.4 %weights.1.w_ref = f32[8,64]{1,0:T(8,128)S(1)} custom-call(f32[32,1024]{1,0:T(8,128)S(1)} %constant_dynamic-update-slice_fusion.near_ref, f32[32,1024]{1,0:T(8,128)S(1)} %collective-permute-done.18.far_ref, f32[8,1024]{1,0:T(8,128)S(1)} %get-tuple-element.75.innovation_ref), custom_call_target="tpu_custom_call" | custom-call | tf_op jit(solution)/shard_map/weights/pallas_call | solution.py:487
  89.5 4.0 %collective-permute-done.19.refs_7_ = bf16[128,8,256]{2,1,0:T(8,128)(2,1)S(1)} collective-permute-done((bf16[128,8,256]{2,1,0:T(8,128)(2,1)S(1)}, bf16[128,8,256]{2,1,0:T(8,128)(2,1)S(1)}, u32[]{:S(2)}, u32[]{:S(2)}) %collective-permute-start.19) | collective-permute-done | bytes 524320 | tf_op jit(solution)/shard_map/ppermute | solution.py:570
  93.4 2.1 %collective-permute-start.24 = (bf16[128,8,256]{2,1,0:T(8,128)(2,1)S(1)}, bf16[128,8,256]{2,1,0:T(8,128)(2,1)S(1)}, u32[]{:S(2)}, u32[]{:S(2)}) collective-permute-start(bf16[128,8,256]{2,1,0:T(8,128)(2,1)S(1)} %collective-permute-done.14.refs_6_), channel_id=1, source_target_pairs={{0,16},{16,0},{32,48},{48,32},{64,80},{80,64},{96,112},{112,96},{1... | collective-permute-start | bytes 1572872 | tf_op jit(solution)/shard_map/ppermute | solution.py:570
  95.6 0.1 collective-permute-start.25
  95.7 1.4 %collective-permute-done.24.refs_14_ = bf16[128,8,256]{2,1,0:T(8,128)(2,1)S(1)} collective-permute-done((bf16[128,8,256]{2,1,0:T(8,128)(2,1)S(1)}, bf16[128,8,256]{2,1,0:T(8,128)(2,1)S(1)}, u32[]{:S(2)}, u32[]{:S(2)}) %collective-permute-start.24) | collective-permute-done | bytes 524320 | tf_op jit(solution)/shard_map/ppermute | solution.py:570
  97.1 0.7 collective-permute-done.25.refs_15_
  97.9 4.5 %update.1 = f32[8,256,256]{2,1,0:T(8,128)} custom-call(f32[8,64]{1,0:T(8,128)S(1)} %weights.1.w_ref, bf16[128,8,256]{2,1,0:T(8,128)(2,1)S(1)} %get-tuple-element.54.refs_0_, bf16[128,8,256]{2,1,0:T(8,128)(2,1)} %get-tuple-element.55.refs_1_, bf16[128,8,256]{2,1,0:T(8,128)(2,1)} %collective-permute-done.5.refs_2_, ...), custom_call_target="tpu_custom_call" | custom-call | tf_op jit(solution)/shard_map/update/pallas_call | solution.py:535
  (46 shorter events, 0.2 us)
Async XLA Ops:
  0.0 7.6 %copy-start = (f32[256,256]{1,0:T(8,128)S(1)}, f32[256,256]{1,0:T(8,128)}, u32[]{:S(2)}) copy-start(f32[256,256]{1,0:T(8,128)} %e_ref.7) | copy-start | bytes 786436
  0.0 7.6 %copy-start.1 = (f32[256,256]{1,0:T(8,128)S(1)}, f32[256,256]{1,0:T(8,128)}, u32[]{:S(2)}) copy-start(f32[256,256]{1,0:T(8,128)} %k_ref.7) | copy-start | bytes 786436
  2.8 9.1 %collective-permute-start = (f32[9,8,256]{2,1,0:T(8,128)}, f32[9,8,256]{2,1,0:T(8,128)S(1)}, u32[]{:S(2)}, u32[]{:S(2)}) collective-permute-start(f32[9,8,256]{2,1,0:T(8,128)} %get-tuple-element.43.bottom_ref), channel_id=1, source_target_pairs={{0,4},{4,8},{8,12},{12,0},{1,5},{5,9},{9,13},{13,1},{2,6},{6,10},{... | collective-permute-start | bytes 221192 | tf_op jit(solution)/shard_map/ppermute | solution.py:561
  5.3 6.6 %copy-start.2 = (f32[9,8,256]{2,1,0:T(8,128)S(1)}, f32[9,8,256]{2,1,0:T(8,128)}, u32[]{:S(2)}) copy-start(f32[9,8,256]{2,1,0:T(8,128)} %get-tuple-element.44.top_ref) | copy-start | bytes 221188
  5.3 6.6 %copy-start.3 = (f32[9,8,256]{2,1,0:T(8,128)S(1)}, f32[9,8,256]{2,1,0:T(8,128)}, u32[]{:S(2)}) copy-start(f32[9,8,256]{2,1,0:T(8,128)} %get-tuple-element.43.bottom_ref) | copy-start | bytes 221188
  5.3 9.6 %copy-start.6 = (f32[64,8]{0,1:T(8,128)S(1)}, f32[64,8]{0,1:T(8,128)}, u32[]{:S(2)}) copy-start(f32[64,8]{0,1:T(8,128)} %param.15) | copy-start | bytes 6148
  5.3 9.6 %copy-start.7 = (f32[64]{0:T(128)S(1)}, f32[64]{0:T(128)}, u32[]{:S(2)}) copy-start(f32[64]{0:T(128)} %param.14) | copy-start | bytes 772
  5.3 9.6 %copy-start.8 = (f32[64]{0:T(128)S(1)}, f32[64]{0:T(128)}, u32[]{:S(2)}) copy-start(f32[64]{0:T(128)} %param.13) | copy-start | bytes 772
  5.3 6.5 %collective-permute-start.1 = (f32[9,8,256]{2,1,0:T(8,128)}, f32[9,8,256]{2,1,0:T(8,128)S(1)}, u32[]{:S(2)}, u32[]{:S(2)}) collective-permute-start(f32[9,8,256]{2,1,0:T(8,128)} %get-tuple-element.44.top_ref), channel_id=1, source_target_pairs={{0,12},{4,0},{8,4},{12,8},{1,13},{5,1},{9,5},{13,9},{2,14},{6,2},{... | collective-permute-start | bytes 221192 | tf_op jit(solution)/shard_map/ppermute | solution.py:562
  12.0 4.9 %collective-permute-start.2 = (f32[9,3,8,128]{3,2,1,0:T(8,128)S(1)}, f32[9,3,8,128]{3,2,1,0:T(8,128)S(1)}, u32[]{:S(2)}, u32[]{:S(2)}) collective-permute-start(f32[9,3,8,128]{3,2,1,0:T(8,128)S(1)} %get-tuple-element.48), channel_id=1, source_target_pairs={{0,1},{1,2},{2,3},{3,0},{4,5},{5,6},{6,7},{7,4},{8,9},{9,10},{10,1... | collective-permute-start | bytes 331784 | tf_op jit(solution)/shard_map/ppermute | solution.py:565
  13.4 3.6 %collective-permute-start.3 = (f32[9,3,8,128]{3,2,1,0:T(8,128)S(1)}, f32[9,3,8,128]{3,2,1,0:T(8,128)S(1)}, u32[]{:S(2)}, u32[]{:S(2)}) collective-permute-start(f32[9,3,8,128]{3,2,1,0:T(8,128)S(1)} %get-tuple-element.49), channel_id=1, source_target_pairs={{0,3},{1,0},{2,1},{3,2},{4,7},{5,4},{6,5},{7,6},{8,11},{9,8},{10,9... | collective-permute-start | bytes 331784 | tf_op jit(solution)/shard_map/ppermute | solution.py:566
  28.5 28.2 %collective-permute-start.7 = (bf16[128,8,256]{2,1,0:T(8,128)(2,1)S(1)}, bf16[128,8,256]{2,1,0:T(8,128)(2,1)}, u32[]{:S(2)}, u32[]{:S(2)}) collective-permute-start(bf16[128,8,256]{2,1,0:T(8,128)(2,1)S(1)} %get-tuple-element.54.refs_0_), channel_id=1, source_target_pairs={{0,16},{16,0},{32,48},{48,32},{64,80},{80,64},{96,112},{112,96},{1... | collective-permute-start | bytes 1572872 | tf_op jit(solution)/shard_map/ppermute | solution.py:570
  30.9 25.8 %collective-permute-start.6 = (bf16[128,8,256]{2,1,0:T(8,128)(2,1)S(1)}, bf16[128,8,256]{2,1,0:T(8,128)(2,1)}, u32[]{:S(2)}, u32[]{:S(2)}) collective-permute-start(bf16[128,8,256]{2,1,0:T(8,128)(2,1)S(1)} %get-tuple-element.54.refs_0_), channel_id=1, source_target_pairs={{0,96},{16,48},{32,0},{48,80},{64,32},{80,112},{96,64},{112,16},{1... | collective-permute-start | bytes 1572872 | tf_op jit(solution)/shard_map/ppermute | solution.py:570
  32.2 24.6 %collective-permute-start.5 = (bf16[128,8,256]{2,1,0:T(8,128)(2,1)S(1)}, bf16[128,8,256]{2,1,0:T(8,128)(2,1)}, u32[]{:S(2)}, u32[]{:S(2)}) collective-permute-start(bf16[128,8,256]{2,1,0:T(8,128)(2,1)S(1)} %get-tuple-element.54.refs_0_), channel_id=1, source_target_pairs={{0,32},{16,112},{32,64},{48,16},{64,96},{80,48},{96,0},{112,80},{1... | collective-permute-start | bytes 1572872 | tf_op jit(solution)/shard_map/ppermute | solution.py:570
  33.6 12.9 %copy-start.4 = (s32[8,128]{1,0:T(8,128)S(1)}, s32[8,128]{1,0:T(8,128)}, u32[]{:S(2)}) copy-start(s32[8,128]{1,0:T(8,128)} %get-tuple-element.40.code_ref) | copy-start | bytes 12292
  33.6 12.9 %copy-start.5 = (f32[8,128]{1,0:T(8,128)S(1)}, f32[8,128]{1,0:T(8,128)}, u32[]{:S(2)}) copy-start(f32[8,128]{1,0:T(8,128)} %get-tuple-element.53.inside_ref) | copy-start | bytes 12292
  45.9 8.2 %collective-permute-start.8 = (bf16[128,8,256]{2,1,0:T(8,128)(2,1)}, bf16[128,8,256]{2,1,0:T(8,128)(2,1)S(1)}, u32[]{:S(2)}, u32[]{:S(2)}) collective-permute-start(bf16[128,8,256]{2,1,0:T(8,128)(2,1)} %get-tuple-element.55.refs_1_), channel_id=1, source_target_pairs={{0,16},{16,0},{32,48},{48,32},{64,80},{80,64},{96,112},{112,96},{1... | collective-permute-start | bytes 1572872 | tf_op jit(solution)/shard_map/ppermute | solution.py:570
  49.2 4.1 %collective-permute-start.4 = (f32[24,1024]{1,0:T(8,128)S(1)}, f32[24,1024]{1,0:T(8,128)S(1)}, u32[]{:S(2)}, u32[]{:S(2)}) collective-permute-start(f32[24,1024]{1,0:T(8,128)S(1)} %pad_maximum_fusion), channel_id=1, source_target_pairs={{0,1},{1,0},{2,3},{3,2},{4,5},{5,4},{6,7},{7,6},{8,9},{9,8},{10,11... | collective-permute-start | bytes 294920 | tf_op jit(solution)/shard_map/ppermute | solution.py:592
  53.3 19.9 %collective-permute-start.13 = (bf16[128,8,256]{2,1,0:T(8,128)(2,1)}, bf16[128,8,256]{2,1,0:T(8,128)(2,1)S(1)}, u32[]{:S(2)}, u32[]{:S(2)}) collective-permute-start(bf16[128,8,256]{2,1,0:T(8,128)(2,1)} %get-tuple-element.55.refs_1_), channel_id=1, source_target_pairs={{0,96},{16,48},{32,0},{48,80},{64,32},{80,112},{96,64},{112,16},{1... | collective-permute-start | bytes 1572872 | tf_op jit(solution)/shard_map/ppermute | solution.py:570
  54.1 19.1 %collective-permute-start.12 = (bf16[128,8,256]{2,1,0:T(8,128)(2,1)}, bf16[128,8,256]{2,1,0:T(8,128)(2,1)S(1)}, u32[]{:S(2)}, u32[]{:S(2)}) collective-permute-start(bf16[128,8,256]{2,1,0:T(8,128)(2,1)} %get-tuple-element.55.refs_1_), channel_id=1, source_target_pairs={{0,32},{16,112},{32,64},{48,16},{64,96},{80,48},{96,0},{112,80},{1... | collective-permute-start | bytes 1572872 | tf_op jit(solution)/shard_map/ppermute | solution.py:570
  56.7 17.7 %collective-permute-start.14 = (bf16[128,8,256]{2,1,0:T(8,128)(2,1)}, bf16[128,8,256]{2,1,0:T(8,128)(2,1)S(1)}, u32[]{:S(2)}, u32[]{:S(2)}) collective-permute-start(bf16[128,8,256]{2,1,0:T(8,128)(2,1)} %collective-permute-done.5.refs_2_), channel_id=1, source_target_pairs={{0,32},{16,112},{32,64},{48,16},{64,96},{80,48},{96,0},{112,80},{1... | collective-permute-start | bytes 1572872 | tf_op jit(solution)/shard_map/ppermute | solution.py:570
  58.2 6.0 %collective-permute-start.9 = (f32[24,1024]{1,0:T(8,128)S(1)}, f32[24,1024]{1,0:T(8,128)S(1)}, u32[]{:S(2)}, u32[]{:S(2)}) collective-permute-start(f32[24,1024]{1,0:T(8,128)S(1)} %fusion.1), channel_id=1, source_target_pairs={{0,2},{1,3},{2,0},{3,1},{4,6},{5,7},{6,4},{7,5},{8,10},{9,11},{10,... | collective-permute-start | bytes 294920 | tf_op jit(solution)/shard_map/ppermute | solution.py:592
  64.3 3.8 %collective-permute-start.10 = (f32[24,1024]{1,0:T(8,128)S(1)}, f32[24,1024]{1,0:T(8,128)S(1)}, u32[]{:S(2)}, u32[]{:S(2)}) collective-permute-start(f32[24,1024]{1,0:T(8,128)S(1)} %add.31), channel_id=1, source_target_pairs={{0,4},{4,0},{8,12},{12,8},{1,5},{5,1},{9,13},{13,9},{2,6},{6,2},{1... | collective-permute-start | bytes 294920 | tf_op jit(solution)/shard_map/ppermute | solution.py:592
  68.1 5.1 %collective-permute-start.11 = (f32[24,1024]{1,0:T(8,128)S(1)}, f32[24,1024]{1,0:T(8,128)S(1)}, u32[]{:S(2)}, u32[]{:S(2)}) collective-permute-start(f32[24,1024]{1,0:T(8,128)S(1)} %add.32), channel_id=1, source_target_pairs={{0,8},{4,12},{8,0},{12,4},{1,9},{5,13},{9,1},{13,5},{2,10},{6,14},... | collective-permute-start | bytes 294920 | tf_op jit(solution)/shard_map/ppermute | solution.py:592
  74.4 7.0 %collective-permute-start.17 = (f32[8,1024]{1,0:T(8,128)S(1)}, f32[8,1024]{1,0:T(8,128)S(1)}, u32[]{:S(2)}, u32[]{:S(2)}) collective-permute-start(f32[8,1024]{1,0:T(8,128)S(1)} %get-tuple-element.60), channel_id=1, source_target_pairs={{0,64},{16,80},{32,96},{48,112},{64,0},{80,16},{96,32},{112,48},{1... | collective-permute-start | bytes 98312 | tf_op jit(solution)/shard_map/ppermute | solution.py:570
  76.9 4.5 %collective-permute-start.16 = (f32[8,1024]{1,0:T(8,128)S(1)}, f32[8,1024]{1,0:T(8,128)S(1)}, u32[]{:S(2)}, u32[]{:S(2)}) collective-permute-start(f32[8,1024]{1,0:T(8,128)S(1)} %get-tuple-element.60), channel_id=1, source_target_pairs={{0,96},{16,48},{32,0},{48,80},{64,32},{80,112},{96,64},{112,16},{1... | collective-permute-start | bytes 98312 | tf_op jit(solution)/shard_map/ppermute | solution.py:570
  78.3 3.1 %collective-permute-start.15 = (f32[8,1024]{1,0:T(8,128)S(1)}, f32[8,1024]{1,0:T(8,128)S(1)}, u32[]{:S(2)}, u32[]{:S(2)}) collective-permute-start(f32[8,1024]{1,0:T(8,128)S(1)} %get-tuple-element.60), channel_id=1, source_target_pairs={{0,32},{16,112},{32,64},{48,16},{64,96},{80,48},{96,0},{112,80},{1... | collective-permute-start | bytes 98312 | tf_op jit(solution)/shard_map/ppermute | solution.py:570
  81.4 4.7 %collective-permute-start.18 = (f32[32,1024]{1,0:T(8,128)S(1)}, f32[32,1024]{1,0:T(8,128)S(1)}, u32[]{:S(2)}, u32[]{:S(2)}) collective-permute-start(f32[32,1024]{1,0:T(8,128)S(1)} %constant_dynamic-update-slice_fusion.near_ref), channel_id=1, source_target_pairs={{0,16},{16,0},{32,48},{48,32},{64,80},{80,64},{96,112},{112,96},{1... | collective-permute-start | bytes 393224 | tf_op jit(solution)/shard_map/ppermute | solution.py:570
  85.1 8.3 %collective-permute-start.19 = (bf16[128,8,256]{2,1,0:T(8,128)(2,1)S(1)}, bf16[128,8,256]{2,1,0:T(8,128)(2,1)S(1)}, u32[]{:S(2)}, u32[]{:S(2)}) collective-permute-start(bf16[128,8,256]{2,1,0:T(8,128)(2,1)S(1)} %collective-permute-done.12.refs_3_), channel_id=1, source_target_pairs={{0,32},{16,112},{32,64},{48,16},{64,96},{80,48},{96,0},{112,80},{1... | collective-permute-start | bytes 1572872 | tf_op jit(solution)/shard_map/ppermute | solution.py:570
  86.1 9.5 %collective-permute-start.20 = (bf16[128,8,256]{2,1,0:T(8,128)(2,1)S(1)}, bf16[128,8,256]{2,1,0:T(8,128)(2,1)S(1)}, u32[]{:S(2)}, u32[]{:S(2)}) collective-permute-start(bf16[128,8,256]{2,1,0:T(8,128)(2,1)S(1)} %collective-permute-done.12.refs_3_), channel_id=1, source_target_pairs={{0,16},{16,0},{32,48},{48,32},{64,80},{80,64},{96,112},{112,96},{1... | collective-permute-start | bytes 1572872 | tf_op jit(solution)/shard_map/ppermute | solution.py:570
  86.5 9.1 %collective-permute-start.21 = (bf16[128,8,256]{2,1,0:T(8,128)(2,1)S(1)}, bf16[128,8,256]{2,1,0:T(8,128)(2,1)S(1)}, u32[]{:S(2)}, u32[]{:S(2)}) collective-permute-start(bf16[128,8,256]{2,1,0:T(8,128)(2,1)S(1)} %collective-permute-done.13.refs_5_), channel_id=1, source_target_pairs={{0,16},{16,0},{32,48},{48,32},{64,80},{80,64},{96,112},{112,96},{1... | collective-permute-start | bytes 1572872 | tf_op jit(solution)/shard_map/ppermute | solution.py:570
  86.6 9.1 %collective-permute-start.22 = (bf16[128,8,256]{2,1,0:T(8,128)(2,1)}, bf16[128,8,256]{2,1,0:T(8,128)(2,1)S(1)}, u32[]{:S(2)}, u32[]{:S(2)}) collective-permute-start(bf16[128,8,256]{2,1,0:T(8,128)(2,1)} %collective-permute-done.5.refs_2_), channel_id=1, source_target_pairs={{0,16},{16,0},{32,48},{48,32},{64,80},{80,64},{96,112},{112,96},{1... | collective-permute-start | bytes 1572872 | tf_op jit(solution)/shard_map/ppermute | solution.py:570
  87.0 8.7 %collective-permute-start.23 = (bf16[128,8,256]{2,1,0:T(8,128)(2,1)}, bf16[128,8,256]{2,1,0:T(8,128)(2,1)S(1)}, u32[]{:S(2)}, u32[]{:S(2)}) collective-permute-start(bf16[128,8,256]{2,1,0:T(8,128)(2,1)} %collective-permute-done.6.refs_4_), channel_id=1, source_target_pairs={{0,16},{16,0},{32,48},{48,32},{64,80},{80,64},{96,112},{112,96},{1... | collective-permute-start | bytes 1572872 | tf_op jit(solution)/shard_map/ppermute | solution.py:570
  93.4 3.7 %collective-permute-start.24 = (bf16[128,8,256]{2,1,0:T(8,128)(2,1)S(1)}, bf16[128,8,256]{2,1,0:T(8,128)(2,1)S(1)}, u32[]{:S(2)}, u32[]{:S(2)}) collective-permute-start(bf16[128,8,256]{2,1,0:T(8,128)(2,1)S(1)} %collective-permute-done.14.refs_6_), channel_id=1, source_target_pairs={{0,16},{16,0},{32,48},{48,32},{64,80},{80,64},{96,112},{112,96},{1... | collective-permute-start | bytes 1572872 | tf_op jit(solution)/shard_map/ppermute | solution.py:570
  95.6 2.3 %collective-permute-start.25 = (bf16[128,8,256]{2,1,0:T(8,128)(2,1)S(1)}, bf16[128,8,256]{2,1,0:T(8,128)(2,1)S(1)}, u32[]{:S(2)}, u32[]{:S(2)}) collective-permute-start(bf16[128,8,256]{2,1,0:T(8,128)(2,1)S(1)} %collective-permute-done.19.refs_7_), channel_id=1, source_target_pairs={{0,16},{16,0},{32,48},{48,32},{64,80},{80,64},{96,112},{112,96},{1... | collective-permute-start | bytes 1572872 | tf_op jit(solution)/shard_map/ppermute | solution.py:570

commit v2 on v0

--- a/solution.py
+++ b/solution.py
@@ -404,7 +404,7 @@
     )(code, forecast, inside)
 
 
-def weights_kernel(near_ref, far_ref, innovation_ref, out_ref, x_s, m_s):
+def weights_kernel(near_ref, far_ref, target_ref, error_ref, first_ref, last_ref, x_s, m_s):
     half = near_ref.shape[0]
     members = 2 * half
     blocks = members // 8
@@ -413,8 +413,11 @@
     for part in parts[1:]:
         total = total + part
     mean = jnp.sum(total, axis=0, keepdims=True) * F32(1.0 / members)
+    error = jnp.concatenate([error_ref[r : r + 1, :] for r in range(error_ref.shape[0])], axis=1)
+    inverse = F32(1) / error
     for b, part in enumerate(parts):
-        x_s[8 * b : 8 * b + 8, :] = part - mean
+        x_s[8 * b : 8 * b + 8, :] = (part - mean) * inverse
+    innovation = (target_ref[...] - parts[0]) * inverse
     x = x_s[...]
     dims = (((1,), (1,)), ((), ()))
     dot = functools.partial(
@@ -425,7 +428,7 @@
     c = lax.broadcasted_iota(jnp.int32, (members, members), 1)
     m_s[:, 0:members] = dot(x, x) + jnp.where(r == c, F32(members - 1), F32(0))
     m_s[:, members : 2 * members] = jnp.zeros((members, members), F32)
-    m_s[:, members : members + 8] = dot(x, innovation_ref[...])
+    m_s[:, members : members + 8] = dot(x, innovation)
     m = [m_s[8 * b : 8 * b + 8, :] for b in range(blocks)]
     sub = sublanes()
     for kb in range(blocks):
@@ -456,24 +459,50 @@
     for b in range(blocks):
         m_s[8 * b : 8 * b + 8, :] = m[b]
     turned = jnp.transpose(m_s[...], (1, 0))
-    out_ref[...] = turned[members : members + 8, 0:members]
-
-
-def solve_weights(near, far, innovation):
+    turned = turned[members : members + 8, :]
+    for h in range(2):
+        at = h * half
+        first_ref[:, h * (half - 8) : (h + 1) * (half - 8)] = turned[:, at : at + half - 8]
+        last_ref[:, 8 * h : 8 * h + 8] = turned[:, at + half - 8 : at + half]
+
+
+def solve_weights(near, far, target, error):
     half, n_obs = near.shape
     members = 2 * half
     return pl.pallas_call(
         weights_kernel,
-        in_specs=[VMEM_SPEC] * 3,
-        out_specs=VMEM_SPEC,
+        in_specs=[VMEM_SPEC] * 4,
+        out_specs=[VMEM_SPEC] * 2,
         scratch_shapes=[
             pltpu.VMEM((members, n_obs), F32),
             pltpu.VMEM((members, 2 * members), F32),
         ],
-        out_shape=jax.ShapeDtypeStruct((8, members), F32),
+        out_shape=[
+            jax.ShapeDtypeStruct((8, members - 16), F32), jax.ShapeDtypeStruct((8, 16), F32),
+        ],
         compiler_params=pltpu.CompilerParams(vmem_limit_bytes=4 * 2**20),
         name="weights",
-    )(near, far, innovation)
+    )(near, far, target, error)
+
+
+def shifted(w, pieces, f_ref, x):
+    rows = jnp.concatenate([v[x].astype(F32) for v in pieces], axis=0).astype(BF16)
+    shift = jnp.dot(w, rows, preferred_element_type=F32)
+    return [f_ref[2 * x + t] + shift[:, 128 * t : 128 * t + 128] for t in range(2)]
+
+
+def begin_kernel(w_ref, *refs):
+    pieces, (f_ref, out_ref) = refs[:-2], refs[-2:]
+    w = w_ref[...].astype(BF16)
+
+    def chunk(g, _):
+        for r in range(16):
+            x = g * 16 + r
+            for t, v in enumerate(shifted(w, pieces, f_ref, x)):
+                out_ref[2 * x + t] = v
+        return 0
+
+    lax.fori_loop(0, pieces[0].shape[0] // 16, chunk, 0)
 
 
 def update_kernel(w_ref, *refs):
@@ -486,14 +515,10 @@
         return pltpu.make_async_copy(done_s.at[:, at, :], out_ref.at[:, at, :], sems.at[g])
 
     def chunk(g, _):
-        x = g * step
         for r in range(step):
-            rows = jnp.concatenate([v[x + r].astype(F32) for v in pieces], axis=0).astype(BF16)
-            shift = jnp.dot(w, rows, preferred_element_type=F32)
-            for t in range(2):
-                cols = slice(128 * t, 128 * t + 128)
-                row_s[r, :, cols] = f_ref[2 * (x + r) + t] + shift[:, cols]
-        at = pl.ds(pl.multiple_of(x, step), step)
+            for t, v in enumerate(shifted(w, pieces, f_ref, g * step + r)):
+                row_s[r, :, 128 * t : 128 * t + 128] = v
+        at = pl.ds(pl.multiple_of(g * step, step), step)
         done_s[:, at, :] = jnp.swapaxes(row_s[...], 0, 1)
         leave(g).start()
         return 0
@@ -502,6 +527,17 @@
     lax.fori_loop(0, count, chunk, 0)
     for g in range(count):
         leave(g).wait()
+
+
+def begin(weights, pieces, forecast):
+    return pl.pallas_call(
+        begin_kernel,
+        in_specs=[VMEM_SPEC] * (len(pieces) + 2),
+        out_specs=VMEM_SPEC,
+        out_shape=jax.ShapeDtypeStruct(forecast.shape, F32),
+        compiler_params=pltpu.CompilerParams(vmem_limit_bytes=12 * 2**20),
+        name="begin",
+    )(weights, *pieces, forecast)
 
 
 def update(weights, pieces, forecast):
@@ -551,14 +587,14 @@
 
     block = n_obs // (n_x * n_y)
     tile = tile_x * n_y + tile_y
-    mine = jnp.concatenate(
-        [
-            (obs_value[:, None] + obs_error[:, None] * perturbation).T,
-            jnp.broadcast_to(obs_error[None], (8, block)),
-        ]
-    )
-    mine = lax.dynamic_update_slice(jnp.zeros((16, n_obs), F32), mine, (0, tile * block))
-    line = jnp.concatenate([picked, mine])
+    target = (obs_value[:, None] + obs_error[:, None] * perturbation).T
+    target = lax.dynamic_update_slice(jnp.zeros((8, n_obs), F32), target, (0, tile * block))
+    per_row = 128 // block
+    error = lax.dynamic_update_slice(
+        jnp.zeros((n_obs // 128, 128), F32), obs_error[None],
+        (tile // per_row, tile % per_row * block),
+    )
+    line = jnp.concatenate([picked, target, error], axis=1)
     a, b = send(rounded, 1), send(rounded, -1)
     own_far = send(rounded, 0, True)
     for axis, n in (("ty", n_y), ("tx", n_x)):
@@ -568,21 +604,20 @@
             if bit == 1 and axis == "ty":
                 line, own_far = lax.optimization_barrier((line, own_far))
             bit *= 2
-    observed, target, error = line[0:8], line[8:16], line[16:17]
-    innovation = (target - observed) / error
-    scaled = observed / error
-
-    scaled, a, b = lax.optimization_barrier((scaled, a, b))
+    observed, target, error = (
+        line[:, 0:n_obs], line[:, n_obs : 2 * n_obs], line[:, 2 * n_obs :]
+    )
+    observed, a, b = lax.optimization_barrier((observed, a, b))
     c = send(a, 1)
-    parts = [send(scaled, by) for by in (1, -1, 2)]
-    near = jnp.concatenate([scaled] + parts)
+    parts = [send(observed, by) for by in (1, -1, 2)]
+    near = jnp.concatenate([observed] + parts)
     far = send(near, 0, True)
     far, a, b = lax.optimization_barrier((far, a, b))
     a_far, b_far = send(a, 0, True), send(b, 0, True)
-    weights = solve_weights(near, far, innovation)
-    weights, c, a_far, b_far = lax.optimization_barrier((weights, c, a_far, b_far))
+    w_first, w_last = solve_weights(near, far, target, error)
+    begun = begin(w_first, [rounded, a, b, own_far, a_far, b_far], forecast)
     c_far = send(c, 0, True)
-    return update(weights, [rounded, a, b, c, own_far, a_far, b_far, c_far], forecast)
+    return update(w_last, [c, c_far], begun)
 
 
 def solution(mesh):

time: 100 us -> 99.5 us (level)
  starting transfers between devices: 30.9 us -> 28 us
  waiting for transfers between devices: 31.2 us -> 32.4 us
    ppermute x11, waiting for transfers between devices: 16.4 us -> 22.1 us  [send(): lax.ppermute(v, 'mem', [(i, i ^ 1) for i in range(n_m)] if swap else to)]
    ppermute x4, waiting for transfers between devices: 12.7 us -> 8.75 us  [local(): line = line + lax.ppermute(line, axis, [(i, i ^ bit) for i in range(n)])]
    pallas_call x1 -> x2, Pallas kernels: 2.36 us -> 5.63 us  [the longest x1 3.02 us: begin(): pl.pallas_call(begin_kernel, in_specs=[VMEM_SPEC] * (len(pieces) + 2), ou...]
    ppermute x11, starting transfers between devices: 17.5 us -> 14.8 us  [send(): lax.ppermute(v, 'mem', [(i, i ^ 1) for i in range(n_m)] if swap else to)]
    pallas_call x1, Pallas kernels: 4.82 us -> 2.46 us  [update(): pl.pallas_call(update_kernel, in_specs=[VMEM_SPEC] * (len(pieces) + 2), o...]
  transfers between devices with their start and end apart: 19 -> 19, of which waited for: 10 -> 9; matrix products, arithmetic and copies ran while one was open for 0% -> 1% of each run, Pallas kernels for 9% -> 13%
where the time goes in v2:
time: 99.5 us; the launch traced here: 99.4 us
  Pallas kernels  38.1 us (38%)
  waiting for transfers between devices  32.4 us (33%)
  starting transfers between devices  28 us (28%)
    ppermute x11, waiting for transfers between devices, send(): lax.ppermute(v, 'mem', [(i, i ^ 1) for i in range(n_m)] if swap else to)  22.1 us
    pallas_call x1, Pallas kernels, run_steps(): pl.pallas_call(steps_kernel, in_specs=[HBM_SPEC] * 2 + [VMEM_SPEC] * 6, o...  20.1 us
    ppermute x11, starting transfers between devices, send(): lax.ppermute(v, 'mem', [(i, i ^ 1) for i in range(n_m)] if swap else to)  14.8 us
    ppermute x4, waiting for transfers between devices, local(): line = line + lax.ppermute(line, axis, [(i, i ^ bit) for i in range(n)])  8.75 us
    ppermute x4, starting transfers between devices, local(): line = line + lax.ppermute(line, axis, [(i, i ^ bit) for i in range(n)])  5.64 us
    pallas_call x1, Pallas kernels, turn(): pl.pallas_call(turn_kernel, in_specs=[HBM_SPEC] * 2 + [VMEM_SPEC] * 2, ou...  4.29 us
    pallas_call x1, Pallas kernels, begin(): pl.pallas_call(begin_kernel, in_specs=[VMEM_SPEC] * (len(pieces) + 2), ou...  3.02 us
    pallas_call x1, Pallas kernels, ends(): pl.pallas_call(ends_kernel, in_specs=[VMEM_SPEC] + [HBM_SPEC] * 2 + [VMEM...  2.75 us
  transfers between devices with their start and end apart: 19, of which 9 were waited for; matrix products, arithmetic and copies ran while one was open for 1% of the time, Pallas kernels for 13%

profile of v2, /device:TPU:1, one launch (start us, length us, event | category | flops | bytes accessed | tf_op | source)
XLA Modules:
  0.0 99.4 jit_solution(16733447616442478784)
XLA Ops:
  0.0 2.8 %ends.1 = (f32[9,8,256]{2,1,0:T(8,128)}, f32[9,8,256]{2,1,0:T(8,128)}, s32[8,128]{1,0:T(8,128)}, f32[8,128]{1,0:T(8,128)}) custom-call(s32[8,128]{1,0:T(8,128)} %bitcast.4, f32[8,256,256]{2,1,0:T(8,128)} %p_in.1, f32[8,256,256]{2,1,0:T(8,128)} %w_in.1, f32[256,256]{1,0:T(8,128)} %e_ref.5, f32[256,256]{1,0:T(8,128)} %k_ref.5), custom_call_target="tpu_custom_call" | custom-call | tf_op jit(solution)/shard_map/ends/pallas_call | solution.py:76
  2.8 2.5 %collective-permute-start = (f32[9,8,256]{2,1,0:T(8,128)}, f32[9,8,256]{2,1,0:T(8,128)S(1)}, u32[]{:S(2)}, u32[]{:S(2)}) collective-permute-start(f32[9,8,256]{2,1,0:T(8,128)} %get-tuple-element.32.bottom_ref), channel_id=1, source_target_pairs={{0,4},{4,8},{8,12},{12,0},{1,5},{5,9},{9,13},{13,1},{2,6},{6,10},{... | collective-permute-start | bytes 221192 | tf_op jit(solution)/shard_map/ppermute | solution.py:573
  5.3 0.0 copy-start.8
  5.3 2.2 %collective-permute-start.1 = (f32[9,8,256]{2,1,0:T(8,128)}, f32[9,8,256]{2,1,0:T(8,128)S(1)}, u32[]{:S(2)}, u32[]{:S(2)}) collective-permute-start(f32[9,8,256]{2,1,0:T(8,128)} %get-tuple-element.33.top_ref), channel_id=1, source_target_pairs={{0,12},{4,0},{8,4},{12,8},{1,13},{5,1},{9,5},{13,9},{2,14},{6,2},{... | collective-permute-start | bytes 221192 | tf_op jit(solution)/shard_map/ppermute | solution.py:574
  7.6 4.3 %turn.1 = (f32[256,8,256]{2,1,0:T(8,128)}, f32[256,8,256]{2,1,0:T(8,128)}, f32[8,3,8,128]{3,2,1,0:T(8,128)S(1)}, f32[8,3,8,128]{3,2,1,0:T(8,128)S(1)}) custom-call(f32[8,256,256]{2,1,0:T(8,128)} %p_in.1, f32[8,256,256]{2,1,0:T(8,128)} %w_in.1, f32[256,256]{1,0:T(8,128)S(1)} %copy-done, f32[256,256]{1,0:T(8,128)S(1)} %copy-done.1), custom_call_target="tpu_custom_call" | custom-call | flops 10000000 | bytes 9437184 | tf_op jit(solution)/shard_map/turn/pallas_call | solution.py:158
  11.8 0.0 collective-permute-done.up_ref
  11.9 0.0 collective-permute-done.1.down_ref
  11.9 0.1 rows.1
  12.0 1.4 %collective-permute-start.2 = (f32[9,3,8,128]{3,2,1,0:T(8,128)S(1)}, f32[9,3,8,128]{3,2,1,0:T(8,128)S(1)}, u32[]{:S(2)}, u32[]{:S(2)}) collective-permute-start(f32[9,3,8,128]{3,2,1,0:T(8,128)S(1)} %get-tuple-element.38), channel_id=1, source_target_pairs={{0,1},{1,2},{2,3},{3,0},{4,5},{5,6},{6,7},{7,4},{8,9},{9,10},{10,1... | collective-permute-start | bytes 331784 | tf_op jit(solution)/shard_map/ppermute | solution.py:577
  13.4 1.5 %collective-permute-start.3 = (f32[9,3,8,128]{3,2,1,0:T(8,128)S(1)}, f32[9,3,8,128]{3,2,1,0:T(8,128)S(1)}, u32[]{:S(2)}, u32[]{:S(2)}) collective-permute-start(f32[9,3,8,128]{3,2,1,0:T(8,128)S(1)} %get-tuple-element.39), channel_id=1, source_target_pairs={{0,3},{1,0},{2,1},{3,2},{4,7},{5,4},{6,5},{7,6},{8,11},{9,8},{10,9... | collective-permute-start | bytes 331784 | tf_op jit(solution)/shard_map/ppermute | solution.py:578
  15.0 0.3 dynamic_update_slice.6
  15.2 0.2 dynamic_update_slice.7
  15.4 1.5 %collective-permute-done.2.fl_ref = f32[9,3,8,128]{3,2,1,0:T(8,128)S(1)} collective-permute-done((f32[9,3,8,128]{3,2,1,0:T(8,128)S(1)}, f32[9,3,8,128]{3,2,1,0:T(8,128)S(1)}, u32[]{:S(2)}, u32[]{:S(2)}) %collective-permute-start.2) | collective-permute-done | bytes 110624 | tf_op jit(solution)/shard_map/ppermute | solution.py:577
  16.9 0.0 collective-permute-done.3.fr_ref
  17.0 20.1 %steps.1 = (f32[512,8,128]{2,1,0:T(8,128)S(1)}, bf16[256,8,256]{2,1,0:T(8,128)(2,1)S(1)}) custom-call(f32[256,8,256]{2,1,0:T(8,128)} %get-tuple-element.30.pt_in, f32[256,8,256]{2,1,0:T(8,128)} %get-tuple-element.31.wt_in, f32[256,256]{1,0:T(8,128)S(1)} %copy-done, f32[256,256]{1,0:T(8,128)S(1)} %copy-done.1, f32[9,8,256]{2,1,0:T(8,128)S(1)} %get-tuple-element.36.above_ref, ...), custom_call_target="tpu_custom_call" | custom-call | tf_op jit(solution)/shard_map/steps/pallas_call | solution.py:365
  37.1 2.5 %collective-permute-start.5 = (bf16[256,8,256]{2,1,0:T(8,128)(2,1)S(1)}, bf16[256,8,256]{2,1,0:T(8,128)(2,1)S(1)}, u32[]{:S(2)}, u32[]{:S(2)}) collective-permute-start(bf16[256,8,256]{2,1,0:T(8,128)(2,1)S(1)} %get-tuple-element.42.refs_0_), channel_id=1, source_target_pairs={{0,16},{16,0},{32,48},{48,32},{64,80},{80,64},{96,112},{112,96},{1... | collective-permute-start | bytes 3145736 | tf_op jit(solution)/shard_map/ppermute | solution.py:586
  39.6 2.7 %picks.1 = f32[8,1024]{1,0:T(8,128)S(1)} custom-call(s32[8,128]{1,0:T(8,128)S(1)} %copy-done.4, f32[512,8,128]{2,1,0:T(8,128)S(1)} %get-tuple-element.40.f_ref.refs_6_, f32[8,128]{1,0:T(8,128)S(1)} %copy-done.5), custom_call_target="tpu_custom_call" | custom-call | tf_op jit(solution)/shard_map/picks/pallas_call | solution.py:396
  42.3 1.4 %collective-permute-start.4 = (f32[8,2176]{1,0:T(8,128)S(1)}, f32[8,2176]{1,0:T(8,128)S(1)}, u32[]{:S(2)}, u32[]{:S(2)}) collective-permute-start(f32[8,2176]{1,0:T(8,128)S(1)} %pad_maximum_fusion), channel_id=1, source_target_pairs={{0,1},{1,0},{2,3},{3,2},{4,5},{5,4},{6,7},{7,6},{8,9},{9,8},{10,11... | collective-permute-start | bytes 208904 | tf_op jit(solution)/shard_map/ppermute | solution.py:603
  43.7 1.2 %collective-permute-start.10 = (bf16[256,8,256]{2,1,0:T(8,128)(2,1)S(1)}, bf16[256,8,256]{2,1,0:T(8,128)(2,1)S(1)}, u32[]{:S(2)}, u32[]{:S(2)}) collective-permute-start(bf16[256,8,256]{2,1,0:T(8,128)(2,1)S(1)} %get-tuple-element.42.refs_0_), channel_id=1, source_target_pairs={{0,96},{16,48},{32,0},{48,80},{64,32},{80,112},{96,64},{112,16},{1... | collective-permute-start | bytes 3145736 | tf_op jit(solution)/shard_map/ppermute | solution.py:586
  44.9 1.5 %collective-permute-start.9 = (bf16[256,8,256]{2,1,0:T(8,128)(2,1)S(1)}, bf16[256,8,256]{2,1,0:T(8,128)(2,1)S(1)}, u32[]{:S(2)}, u32[]{:S(2)}) collective-permute-start(bf16[256,8,256]{2,1,0:T(8,128)(2,1)S(1)} %get-tuple-element.42.refs_0_), channel_id=1, source_target_pairs={{0,32},{16,112},{32,64},{48,16},{64,96},{80,48},{96,0},{112,80},{1... | collective-permute-start | bytes 3145736 | tf_op jit(solution)/shard_map/ppermute | solution.py:586
  46.4 0.0 collective-permute-done.4
  46.4 0.0 collective-permute-done.5.refs_3_
  46.4 2.6 %collective-permute-start.6 = (f32[8,2176]{1,0:T(8,128)S(1)}, f32[8,2176]{1,0:T(8,128)S(1)}, u32[]{:S(2)}, u32[]{:S(2)}) collective-permute-start(f32[8,2176]{1,0:T(8,128)S(1)} %fusion), channel_id=1, source_target_pairs={{0,2},{1,3},{2,0},{3,1},{4,6},{5,7},{6,4},{7,5},{8,10},{9,11},{10,... | collective-permute-start | bytes 208904 | tf_op jit(solution)/shard_map/ppermute | solution.py:603
  48.9 2.2 %collective-permute-done.6 = f32[8,2176]{1,0:T(8,128)S(1)} collective-permute-done((f32[8,2176]{1,0:T(8,128)S(1)}, f32[8,2176]{1,0:T(8,128)S(1)}, u32[]{:S(2)}, u32[]{:S(2)}) %collective-permute-start.6) | collective-permute-done | bytes 69664 | tf_op jit(solution)/shard_map/ppermute | solution.py:603
  51.1 0.1 collective-permute-start.7
  51.2 3.4 %collective-permute-done.7 = f32[8,2176]{1,0:T(8,128)S(1)} collective-permute-done((f32[8,2176]{1,0:T(8,128)S(1)}, f32[8,2176]{1,0:T(8,128)S(1)}, u32[]{:S(2)}, u32[]{:S(2)}) %collective-permute-start.7) | collective-permute-done | bytes 69664 | tf_op jit(solution)/shard_map/ppermute | solution.py:603
  54.7 1.6 %collective-permute-start.8 = (f32[8,2176]{1,0:T(8,128)S(1)}, f32[8,2176]{1,0:T(8,128)S(1)}, u32[]{:S(2)}, u32[]{:S(2)}) collective-permute-start(f32[8,2176]{1,0:T(8,128)S(1)} %add.46), channel_id=1, source_target_pairs={{0,8},{4,12},{8,0},{12,4},{1,9},{5,13},{9,1},{13,5},{2,10},{6,14},... | collective-permute-start | bytes 208904 | tf_op jit(solution)/shard_map/ppermute | solution.py:603
  56.3 3.1 %collective-permute-done.8 = f32[8,2176]{1,0:T(8,128)S(1)} collective-permute-done((f32[8,2176]{1,0:T(8,128)S(1)}, f32[8,2176]{1,0:T(8,128)S(1)}, u32[]{:S(2)}, u32[]{:S(2)}) %collective-permute-start.8) | collective-permute-done | bytes 69664 | tf_op jit(solution)/shard_map/ppermute | solution.py:603
  59.5 7.1 %collective-permute-done.10.refs_2_ = bf16[256,8,256]{2,1,0:T(8,128)(2,1)S(1)} collective-permute-done((bf16[256,8,256]{2,1,0:T(8,128)(2,1)S(1)}, bf16[256,8,256]{2,1,0:T(8,128)(2,1)S(1)}, u32[]{:S(2)}, u32[]{:S(2)}) %collective-permute-start.10) | collective-permute-done | bytes 1048608 | tf_op jit(solution)/shard_map/ppermute | solution.py:586
  66.5 3.1 %collective-permute-done.9.refs_1_ = bf16[256,8,256]{2,1,0:T(8,128)(2,1)S(1)} collective-permute-done((bf16[256,8,256]{2,1,0:T(8,128)(2,1)S(1)}, bf16[256,8,256]{2,1,0:T(8,128)(2,1)S(1)}, u32[]{:S(2)}, u32[]{:S(2)}) %collective-permute-start.9) | collective-permute-done | bytes 1048608 | tf_op jit(solution)/shard_map/ppermute | solution.py:586
  69.6 2.5 %collective-permute-start.15 = (bf16[256,8,256]{2,1,0:T(8,128)(2,1)S(1)}, bf16[256,8,256]{2,1,0:T(8,128)(2,1)S(1)}, u32[]{:S(2)}, u32[]{:S(2)}) collective-permute-start(bf16[256,8,256]{2,1,0:T(8,128)(2,1)S(1)} %collective-permute-done.9.refs_1_), channel_id=1, source_target_pairs={{0,32},{16,112},{32,64},{48,16},{64,96},{80,48},{96,0},{112,80},{1... | collective-permute-start | bytes 3145736 | tf_op jit(solution)/shard_map/ppermute | solution.py:586
  72.2 0.2 collective-permute-start.13
  72.3 0.7 collective-permute-start.12
  73.1 1.9 %collective-permute-start.11 = (f32[8,1024]{1,0:T(8,128)S(1)}, f32[8,1024]{1,0:T(8,128)S(1)}, u32[]{:S(2)}, u32[]{:S(2)}) collective-permute-start(f32[8,1024]{1,0:T(8,128)S(1)} %get-tuple-element.44), channel_id=1, source_target_pairs={{0,32},{16,112},{32,64},{48,16},{64,96},{80,48},{96,0},{112,80},{1... | collective-permute-start | bytes 98312 | tf_op jit(solution)/shard_map/ppermute | solution.py:586
  75.0 10.3 %collective-permute-done.11 = f32[8,1024]{1,0:T(8,128)S(1)} collective-permute-done((f32[8,1024]{1,0:T(8,128)S(1)}, f32[8,1024]{1,0:T(8,128)S(1)}, u32[]{:S(2)}, u32[]{:S(2)}) %collective-permute-start.11) | collective-permute-done | bytes 32800 | tf_op jit(solution)/shard_map/ppermute | solution.py:586
  85.3 0.0 collective-permute-done.12
  85.3 0.0 collective-permute-done.13
  85.4 3.4 %collective-permute-start.14 = (f32[32,1024]{1,0:T(8,128)S(1)}, f32[32,1024]{1,0:T(8,128)S(1)}, u32[]{:S(2)}, u32[]{:S(2)}) collective-permute-start(f32[32,1024]{1,0:T(8,128)S(1)} %constant_dynamic-update-slice_fusion.near_ref), channel_id=1, source_target_pairs={{0,16},{16,0},{32,48},{48,32},{64,80},{80,64},{96,112},{112,96},{1... | collective-permute-start | bytes 393224 | tf_op jit(solution)/shard_map/ppermute | solution.py:586
  88.7 1.0 collective-permute-done.14.far_ref
  89.7 0.4 collective-permute-start.17
  90.1 0.1 collective-permute-start.18
  90.2 0.4 collective-permute-start.16
  90.6 2.6 %weights.1 = (f32[8,48]{1,0:T(8,128)S(1)}, f32[8,16]{1,0:T(8,128)S(1)}) custom-call(f32[32,1024]{1,0:T(8,128)S(1)} %constant_dynamic-update-slice_fusion.near_ref, f32[32,1024]{1,0:T(8,128)S(1)} %collective-permute-done.14.far_ref, f32[8,1024]{1,0:T(8,128)S(1)} %get-tuple-element.53.target_ref, f32[8,128]{1,0:T(8,128)S(1)} %slice.14.error_ref), custom_call_target="tpu_custom_call" | custom-call | tf_op jit(solution)/shard_map/weights/pallas_call | solution.py:472
  93.2 0.0 collective-permute-done.17.refs_4_
  93.2 0.7 collective-permute-done.18.refs_5_
  93.9 3.0 %begin.1.refs_2_ = f32[512,8,128]{2,1,0:T(8,128)S(1)} custom-call(f32[8,48]{1,0:T(8,128)S(1)} %get-tuple-element.49.w_ref, bf16[256,8,256]{2,1,0:T(8,128)(2,1)S(1)} %get-tuple-element.42.refs_0_, bf16[256,8,256]{2,1,0:T(8,128)(2,1)S(1)} %collective-permute-done.9.refs_1_, bf16[256,8,256]{2,1,0:T(8,128)(2,1)S(1)} %collective-permute-done.10.refs_2_, ...), custom_call_target="tpu_custom_call" | custom-call | tf_op jit(solution)/shard_map/begin/pallas_call | solution.py:533
  96.9 0.0 collective-permute-done.16.refs_1_
  96.9 2.5 %update.1 = f32[8,256,256]{2,1,0:T(8,128)} custom-call(f32[8,16]{1,0:T(8,128)S(1)} %get-tuple-element.48.w_ref, bf16[256,8,256]{2,1,0:T(8,128)(2,1)S(1)} %collective-permute-done.15.refs_0_, bf16[256,8,256]{2,1,0:T(8,128)(2,1)S(1)} %collective-permute-done.16.refs_1_, f32[512,8,128]{2,1,0:T(8,128)S(1)} %begin.1.refs_2_), custom_call_target="tpu_custom_call" | custom-call | tf_op jit(solution)/shard_map/update/pallas_call | solution.py:547
  (32 shorter events, 0.1 us)
Async XLA Ops:
  0.0 7.5 %copy-start = (f32[256,256]{1,0:T(8,128)S(1)}, f32[256,256]{1,0:T(8,128)}, u32[]{:S(2)}) copy-start(f32[256,256]{1,0:T(8,128)} %e_ref.5) | copy-start | bytes 786436
  0.0 7.5 %copy-start.1 = (f32[256,256]{1,0:T(8,128)S(1)}, f32[256,256]{1,0:T(8,128)}, u32[]{:S(2)}) copy-start(f32[256,256]{1,0:T(8,128)} %k_ref.5) | copy-start | bytes 786436
  2.8 9.1 %collective-permute-start = (f32[9,8,256]{2,1,0:T(8,128)}, f32[9,8,256]{2,1,0:T(8,128)S(1)}, u32[]{:S(2)}, u32[]{:S(2)}) collective-permute-start(f32[9,8,256]{2,1,0:T(8,128)} %get-tuple-element.32.bottom_ref), channel_id=1, source_target_pairs={{0,4},{4,8},{8,12},{12,0},{1,5},{5,9},{9,13},{13,1},{2,6},{6,10},{... | collective-permute-start | bytes 221192 | tf_op jit(solution)/shard_map/ppermute | solution.py:573
  5.3 6.6 %copy-start.2 = (f32[9,8,256]{2,1,0:T(8,128)S(1)}, f32[9,8,256]{2,1,0:T(8,128)}, u32[]{:S(2)}) copy-start(f32[9,8,256]{2,1,0:T(8,128)} %get-tuple-element.33.top_ref) | copy-start | bytes 221188
  5.3 6.6 %copy-start.3 = (f32[9,8,256]{2,1,0:T(8,128)S(1)}, f32[9,8,256]{2,1,0:T(8,128)}, u32[]{:S(2)}) copy-start(f32[9,8,256]{2,1,0:T(8,128)} %get-tuple-element.32.bottom_ref) | copy-start | bytes 221188
  5.3 9.6 %copy-start.6 = (f32[64,8]{0,1:T(8,128)S(1)}, f32[64,8]{0,1:T(8,128)}, u32[]{:S(2)}) copy-start(f32[64,8]{0,1:T(8,128)} %param.15) | copy-start | bytes 6148
  5.3 9.6 %copy-start.7 = (f32[64]{0:T(128)S(1)}, f32[64]{0:T(128)}, u32[]{:S(2)}) copy-start(f32[64]{0:T(128)} %param.14) | copy-start | bytes 772
  5.3 9.6 %copy-start.8 = (f32[64]{0:T(128)S(1)}, f32[64]{0:T(128)}, u32[]{:S(2)}) copy-start(f32[64]{0:T(128)} %param.13) | copy-start | bytes 772
  5.3 6.5 %collective-permute-start.1 = (f32[9,8,256]{2,1,0:T(8,128)}, f32[9,8,256]{2,1,0:T(8,128)S(1)}, u32[]{:S(2)}, u32[]{:S(2)}) collective-permute-start(f32[9,8,256]{2,1,0:T(8,128)} %get-tuple-element.33.top_ref), channel_id=1, source_target_pairs={{0,12},{4,0},{8,4},{12,8},{1,13},{5,1},{9,5},{13,9},{2,14},{6,2},{... | collective-permute-start | bytes 221192 | tf_op jit(solution)/shard_map/ppermute | solution.py:574
  12.0 4.9 %collective-permute-start.2 = (f32[9,3,8,128]{3,2,1,0:T(8,128)S(1)}, f32[9,3,8,128]{3,2,1,0:T(8,128)S(1)}, u32[]{:S(2)}, u32[]{:S(2)}) collective-permute-start(f32[9,3,8,128]{3,2,1,0:T(8,128)S(1)} %get-tuple-element.38), channel_id=1, source_target_pairs={{0,1},{1,2},{2,3},{3,0},{4,5},{5,6},{6,7},{7,4},{8,9},{9,10},{10,1... | collective-permute-start | bytes 331784 | tf_op jit(solution)/shard_map/ppermute | solution.py:577
  13.4 3.6 %collective-permute-start.3 = (f32[9,3,8,128]{3,2,1,0:T(8,128)S(1)}, f32[9,3,8,128]{3,2,1,0:T(8,128)S(1)}, u32[]{:S(2)}, u32[]{:S(2)}) collective-permute-start(f32[9,3,8,128]{3,2,1,0:T(8,128)S(1)} %get-tuple-element.39), channel_id=1, source_target_pairs={{0,3},{1,0},{2,1},{3,2},{4,7},{5,4},{6,5},{7,6},{8,11},{9,8},{10,9... | collective-permute-start | bytes 331784 | tf_op jit(solution)/shard_map/ppermute | solution.py:578
  17.0 22.6 %copy-start.4 = (s32[8,128]{1,0:T(8,128)S(1)}, s32[8,128]{1,0:T(8,128)}, u32[]{:S(2)}) copy-start(s32[8,128]{1,0:T(8,128)} %get-tuple-element.29.code_ref) | copy-start | bytes 12292
  17.0 22.6 %copy-start.5 = (f32[8,128]{1,0:T(8,128)S(1)}, f32[8,128]{1,0:T(8,128)}, u32[]{:S(2)}) copy-start(f32[8,128]{1,0:T(8,128)} %get-tuple-element.41.inside_ref) | copy-start | bytes 12292
  37.1 9.3 %collective-permute-start.5 = (bf16[256,8,256]{2,1,0:T(8,128)(2,1)S(1)}, bf16[256,8,256]{2,1,0:T(8,128)(2,1)S(1)}, u32[]{:S(2)}, u32[]{:S(2)}) collective-permute-start(bf16[256,8,256]{2,1,0:T(8,128)(2,1)S(1)} %get-tuple-element.42.refs_0_), channel_id=1, source_target_pairs={{0,16},{16,0},{32,48},{48,32},{64,80},{80,64},{96,112},{112,96},{1... | collective-permute-start | bytes 3145736 | tf_op jit(solution)/shard_map/ppermute | solution.py:586
  42.3 4.1 %collective-permute-start.4 = (f32[8,2176]{1,0:T(8,128)S(1)}, f32[8,2176]{1,0:T(8,128)S(1)}, u32[]{:S(2)}, u32[]{:S(2)}) collective-permute-start(f32[8,2176]{1,0:T(8,128)S(1)} %pad_maximum_fusion), channel_id=1, source_target_pairs={{0,1},{1,0},{2,3},{3,2},{4,5},{5,4},{6,7},{7,6},{8,9},{9,8},{10,11... | collective-permute-start | bytes 208904 | tf_op jit(solution)/shard_map/ppermute | solution.py:603
  43.7 22.9 %collective-permute-start.10 = (bf16[256,8,256]{2,1,0:T(8,128)(2,1)S(1)}, bf16[256,8,256]{2,1,0:T(8,128)(2,1)S(1)}, u32[]{:S(2)}, u32[]{:S(2)}) collective-permute-start(bf16[256,8,256]{2,1,0:T(8,128)(2,1)S(1)} %get-tuple-element.42.refs_0_), channel_id=1, source_target_pairs={{0,96},{16,48},{32,0},{48,80},{64,32},{80,112},{96,64},{112,16},{1... | collective-permute-start | bytes 3145736 | tf_op jit(solution)/shard_map/ppermute | solution.py:586
  44.9 24.7 %collective-permute-start.9 = (bf16[256,8,256]{2,1,0:T(8,128)(2,1)S(1)}, bf16[256,8,256]{2,1,0:T(8,128)(2,1)S(1)}, u32[]{:S(2)}, u32[]{:S(2)}) collective-permute-start(bf16[256,8,256]{2,1,0:T(8,128)(2,1)S(1)} %get-tuple-element.42.refs_0_), channel_id=1, source_target_pairs={{0,32},{16,112},{32,64},{48,16},{64,96},{80,48},{96,0},{112,80},{1... | collective-permute-start | bytes 3145736 | tf_op jit(solution)/shard_map/ppermute | solution.py:586
  46.4 4.7 %collective-permute-start.6 = (f32[8,2176]{1,0:T(8,128)S(1)}, f32[8,2176]{1,0:T(8,128)S(1)}, u32[]{:S(2)}, u32[]{:S(2)}) collective-permute-start(f32[8,2176]{1,0:T(8,128)S(1)} %fusion), channel_id=1, source_target_pairs={{0,2},{1,3},{2,0},{3,1},{4,6},{5,7},{6,4},{7,5},{8,10},{9,11},{10,... | collective-permute-start | bytes 208904 | tf_op jit(solution)/shard_map/ppermute | solution.py:603
  51.1 3.5 %collective-permute-start.7 = (f32[8,2176]{1,0:T(8,128)S(1)}, f32[8,2176]{1,0:T(8,128)S(1)}, u32[]{:S(2)}, u32[]{:S(2)}) collective-permute-start(f32[8,2176]{1,0:T(8,128)S(1)} %add.45), channel_id=1, source_target_pairs={{0,4},{4,0},{8,12},{12,8},{1,5},{5,1},{9,13},{13,9},{2,6},{6,2},{1... | collective-permute-start | bytes 208904 | tf_op jit(solution)/shard_map/ppermute | solution.py:603
  54.7 4.7 %collective-permute-start.8 = (f32[8,2176]{1,0:T(8,128)S(1)}, f32[8,2176]{1,0:T(8,128)S(1)}, u32[]{:S(2)}, u32[]{:S(2)}) collective-permute-start(f32[8,2176]{1,0:T(8,128)S(1)} %add.46), channel_id=1, source_target_pairs={{0,8},{4,12},{8,0},{12,4},{1,9},{5,13},{9,1},{13,5},{2,10},{6,14},... | collective-permute-start | bytes 208904 | tf_op jit(solution)/shard_map/ppermute | solution.py:603
  69.6 20.6 %collective-permute-start.15 = (bf16[256,8,256]{2,1,0:T(8,128)(2,1)S(1)}, bf16[256,8,256]{2,1,0:T(8,128)(2,1)S(1)}, u32[]{:S(2)}, u32[]{:S(2)}) collective-permute-start(bf16[256,8,256]{2,1,0:T(8,128)(2,1)S(1)} %collective-permute-done.9.refs_1_), channel_id=1, source_target_pairs={{0,32},{16,112},{32,64},{48,16},{64,96},{80,48},{96,0},{112,80},{1... | collective-permute-start | bytes 3145736 | tf_op jit(solution)/shard_map/ppermute | solution.py:586
  72.2 13.2 %collective-permute-start.13 = (f32[8,1024]{1,0:T(8,128)S(1)}, f32[8,1024]{1,0:T(8,128)S(1)}, u32[]{:S(2)}, u32[]{:S(2)}) collective-permute-start(f32[8,1024]{1,0:T(8,128)S(1)} %get-tuple-element.44), channel_id=1, source_target_pairs={{0,64},{16,80},{32,96},{48,112},{64,0},{80,16},{96,32},{112,48},{1... | collective-permute-start | bytes 98312 | tf_op jit(solution)/shard_map/ppermute | solution.py:586
  72.3 13.0 %collective-permute-start.12 = (f32[8,1024]{1,0:T(8,128)S(1)}, f32[8,1024]{1,0:T(8,128)S(1)}, u32[]{:S(2)}, u32[]{:S(2)}) collective-permute-start(f32[8,1024]{1,0:T(8,128)S(1)} %get-tuple-element.44), channel_id=1, source_target_pairs={{0,96},{16,48},{32,0},{48,80},{64,32},{80,112},{96,64},{112,16},{1... | collective-permute-start | bytes 98312 | tf_op jit(solution)/shard_map/ppermute | solution.py:586
  73.1 12.2 %collective-permute-start.11 = (f32[8,1024]{1,0:T(8,128)S(1)}, f32[8,1024]{1,0:T(8,128)S(1)}, u32[]{:S(2)}, u32[]{:S(2)}) collective-permute-start(f32[8,1024]{1,0:T(8,128)S(1)} %get-tuple-element.44), channel_id=1, source_target_pairs={{0,32},{16,112},{32,64},{48,16},{64,96},{80,48},{96,0},{112,80},{1... | collective-permute-start | bytes 98312 | tf_op jit(solution)/shard_map/ppermute | solution.py:586
  85.4 4.3 %collective-permute-start.14 = (f32[32,1024]{1,0:T(8,128)S(1)}, f32[32,1024]{1,0:T(8,128)S(1)}, u32[]{:S(2)}, u32[]{:S(2)}) collective-permute-start(f32[32,1024]{1,0:T(8,128)S(1)} %constant_dynamic-update-slice_fusion.near_ref), channel_id=1, source_target_pairs={{0,16},{16,0},{32,48},{48,32},{64,80},{80,64},{96,112},{112,96},{1... | collective-permute-start | bytes 393224 | tf_op jit(solution)/shard_map/ppermute | solution.py:586
  89.7 3.5 %collective-permute-start.17 = (bf16[256,8,256]{2,1,0:T(8,128)(2,1)S(1)}, bf16[256,8,256]{2,1,0:T(8,128)(2,1)S(1)}, u32[]{:S(2)}, u32[]{:S(2)}) collective-permute-start(bf16[256,8,256]{2,1,0:T(8,128)(2,1)S(1)} %collective-permute-done.9.refs_1_), channel_id=1, source_target_pairs={{0,16},{16,0},{32,48},{48,32},{64,80},{80,64},{96,112},{112,96},{1... | collective-permute-start | bytes 3145736 | tf_op jit(solution)/shard_map/ppermute | solution.py:586
  90.1 3.8 %collective-permute-start.18 = (bf16[256,8,256]{2,1,0:T(8,128)(2,1)S(1)}, bf16[256,8,256]{2,1,0:T(8,128)(2,1)S(1)}, u32[]{:S(2)}, u32[]{:S(2)}) collective-permute-start(bf16[256,8,256]{2,1,0:T(8,128)(2,1)S(1)} %collective-permute-done.10.refs_2_), channel_id=1, source_target_pairs={{0,16},{16,0},{32,48},{48,32},{64,80},{80,64},{96,112},{112,96},{1... | collective-permute-start | bytes 3145736 | tf_op jit(solution)/shard_map/ppermute | solution.py:586
  90.2 6.7 %collective-permute-start.16 = (bf16[256,8,256]{2,1,0:T(8,128)(2,1)S(1)}, bf16[256,8,256]{2,1,0:T(8,128)(2,1)S(1)}, u32[]{:S(2)}, u32[]{:S(2)}) collective-permute-start(bf16[256,8,256]{2,1,0:T(8,128)(2,1)S(1)} %collective-permute-done.15.refs_0_), channel_id=1, source_target_pairs={{0,16},{16,0},{32,48},{48,32},{64,80},{80,64},{96,112},{112,96},{1... | collective-permute-start | bytes 3145736 | tf_op jit(solution)/shard_map/ppermute | solution.py:586

commit v3 on v2

--- a/solution.py
+++ b/solution.py
@@ -485,10 +485,10 @@
     )(near, far, target, error)
 
 
-def shifted(w, pieces, f_ref, x):
+def shifted(w, pieces, f_ref, x, to):
     rows = jnp.concatenate([v[x].astype(F32) for v in pieces], axis=0).astype(BF16)
     shift = jnp.dot(w, rows, preferred_element_type=F32)
-    return [f_ref[2 * x + t] + shift[:, 128 * t : 128 * t + 128] for t in range(2)]
+    return [f_ref[2 * to + t] + shift[:, 128 * t : 128 * t + 128] for t in range(2)]
 
 
 def begin_kernel(w_ref, *refs):
@@ -498,7 +498,7 @@
     def chunk(g, _):
         for r in range(16):
             x = g * 16 + r
-            for t, v in enumerate(shifted(w, pieces, f_ref, x)):
+            for t, v in enumerate(shifted(w, pieces, f_ref, x, x)):
                 out_ref[2 * x + t] = v
         return 0
 
@@ -514,18 +514,22 @@
         at = pl.ds(pl.multiple_of(g * step, step), step)
         return pltpu.make_async_copy(done_s.at[:, at, :], out_ref.at[:, at, :], sems.at[g])
 
-    def chunk(g, _):
+    count = pieces[0].shape[0] // step
+
+    def chunk(half, i, _):
+        g = half * count + i
         for r in range(step):
-            for t, v in enumerate(shifted(w, pieces, f_ref, g * step + r)):
+            at = (i * step + r, g * step + r)
+            for t, v in enumerate(shifted(w, pieces[half::2], f_ref, *at)):
                 row_s[r, :, 128 * t : 128 * t + 128] = v
         at = pl.ds(pl.multiple_of(g * step, step), step)
         done_s[:, at, :] = jnp.swapaxes(row_s[...], 0, 1)
         leave(g).start()
         return 0
 
-    count = pieces[0].shape[0] // step
-    lax.fori_loop(0, count, chunk, 0)
-    for g in range(count):
+    for half in range(2):
+        lax.fori_loop(0, count, functools.partial(chunk, half), 0)
+    for g in range(2 * count):
         leave(g).wait()
 
 
@@ -541,7 +545,8 @@
 
 
 def update(weights, pieces, forecast):
-    size_x, members, size_y = pieces[0].shape
+    rows, members, size_y = pieces[0].shape
+    size_x = 2 * rows
     step = 32
     whole = (members, size_x, size_y)
     return pl.pallas_call(
@@ -560,6 +565,7 @@
 
 
 def local(pressure, elevation, ks_field, melt_rate, obs_index, obs_value, obs_error, perturbation):
+    _, size_x, _ = pressure.shape
     n_x, n_y, n_m = (lax.axis_size(a) for a in ("tx", "ty", "mem"))
     tile_x, tile_y = lax.axis_index("tx"), lax.axis_index("ty")
 
@@ -608,7 +614,8 @@
         line[:, 0:n_obs], line[:, n_obs : 2 * n_obs], line[:, 2 * n_obs :]
     )
     observed, a, b = lax.optimization_barrier((observed, a, b))
-    c = send(a, 1)
+    half = size_x // 2
+    c0, c1 = send(a[:half], 1), send(b[half:], -1)
     parts = [send(observed, by) for by in (1, -1, 2)]
     near = jnp.concatenate([observed] + parts)
     far = send(near, 0, True)
@@ -616,8 +623,7 @@
     a_far, b_far = send(a, 0, True), send(b, 0, True)
     w_first, w_last = solve_weights(near, far, target, error)
     begun = begin(w_first, [rounded, a, b, own_far, a_far, b_far], forecast)
-    c_far = send(c, 0, True)
-    return update(w_last, [c, c_far], begun)
+    return update(w_last, [c0, c1, send(c0, 0, True), send(c1, 0, True)], begun)
 
 
 def solution(mesh):

time: 99.5 us -> 105 us (1.055)
  waiting for transfers between devices: 32.4 us -> 35.7 us
  starting transfers between devices: 28 us -> 29.8 us
    ppermute x11 -> x13, waiting for transfers between devices: 22.1 us -> 25.4 us  [send(): lax.ppermute(v, 'mem', [(i, i ^ 1) for i in range(n_m)] if swap else to)]
    ppermute x11 -> x13, starting transfers between devices: 14.8 us -> 16.6 us  [send(): lax.ppermute(v, 'mem', [(i, i ^ 1) for i in range(n_m)] if swap else to)]
  transfers between devices with their start and end apart: 19 -> 21, of which waited for: 9 -> 11; matrix products, arithmetic and copies ran while one was open for 1% -> 1% of each run, Pallas kernels for 13% -> 12%
where the time goes in v3:
time: 105 us
  Pallas kernels  38 us (36%)
  waiting for transfers between devices  35.7 us (34%)
  starting transfers between devices  29.8 us (28%)
    ppermute x13, waiting for transfers between devices, send(): lax.ppermute(v, 'mem', [(i, i ^ 1) for i in range(n_m)] if swap else to)  25.4 us
    pallas_call x1, Pallas kernels, run_steps(): pl.pallas_call(steps_kernel, in_specs=[HBM_SPEC] * 2 + [VMEM_SPEC] * 6, o...  20.1 us
    ppermute x13, starting transfers between devices, send(): lax.ppermute(v, 'mem', [(i, i ^ 1) for i in range(n_m)] if swap else to)  16.6 us
    ppermute x4, waiting for transfers between devices, local(): line = line + lax.ppermute(line, axis, [(i, i ^ bit) for i in range(n)])  8.75 us
    ppermute x4, starting transfers between devices, local(): line = line + lax.ppermute(line, axis, [(i, i ^ bit) for i in range(n)])  5.64 us
    pallas_call x1, Pallas kernels, turn(): pl.pallas_call(turn_kernel, in_specs=[HBM_SPEC] * 2 + [VMEM_SPEC] * 2, ou...  4.27 us
    pallas_call x1, Pallas kernels, begin(): pl.pallas_call(begin_kernel, in_specs=[VMEM_SPEC] * (len(pieces) + 2), ou...  2.96 us
    pallas_call x1, Pallas kernels, ends(): pl.pallas_call(ends_kernel, in_specs=[VMEM_SPEC] + [HBM_SPEC] * 2 + [VMEM...  2.76 us
  transfers between devices with their start and end apart: 21, of which 11 were waited for; matrix products, arithmetic and copies ran while one was open for 1% of the time, Pallas kernels for 12%

profile of v3, /device:TPU:1, one launch (start us, length us, event | category | flops | bytes accessed | tf_op | source)
XLA Modules:
  0.0 104.6 jit_solution(282778838881973578)
XLA Ops:
  0.0 2.8 %ends.1 = (f32[9,8,256]{2,1,0:T(8,128)}, f32[9,8,256]{2,1,0:T(8,128)}, s32[8,128]{1,0:T(8,128)}, f32[8,128]{1,0:T(8,128)}) custom-call(s32[8,128]{1,0:T(8,128)} %bitcast.4, f32[8,256,256]{2,1,0:T(8,128)} %p_in.1, f32[8,256,256]{2,1,0:T(8,128)} %w_in.1, f32[256,256]{1,0:T(8,128)} %e_ref.5, f32[256,256]{1,0:T(8,128)} %k_ref.5), custom_call_target="tpu_custom_call" | custom-call | tf_op jit(solution)/shard_map/ends/pallas_call | solution.py:76
  2.8 2.5 %collective-permute-start = (f32[9,8,256]{2,1,0:T(8,128)}, f32[9,8,256]{2,1,0:T(8,128)S(1)}, u32[]{:S(2)}, u32[]{:S(2)}) collective-permute-start(f32[9,8,256]{2,1,0:T(8,128)} %get-tuple-element.32.bottom_ref), channel_id=1, source_target_pairs={{0,4},{4,8},{8,12},{12,0},{1,5},{5,9},{9,13},{13,1},{2,6},{6,10},{... | collective-permute-start | bytes 221192 | tf_op jit(solution)/shard_map/ppermute | solution.py:579
  5.3 0.0 copy-start.8
  5.3 2.2 %collective-permute-start.1 = (f32[9,8,256]{2,1,0:T(8,128)}, f32[9,8,256]{2,1,0:T(8,128)S(1)}, u32[]{:S(2)}, u32[]{:S(2)}) collective-permute-start(f32[9,8,256]{2,1,0:T(8,128)} %get-tuple-element.33.top_ref), channel_id=1, source_target_pairs={{0,12},{4,0},{8,4},{12,8},{1,13},{5,1},{9,5},{13,9},{2,14},{6,2},{... | collective-permute-start | bytes 221192 | tf_op jit(solution)/shard_map/ppermute | solution.py:580
  7.6 4.3 %turn.1 = (f32[256,8,256]{2,1,0:T(8,128)}, f32[256,8,256]{2,1,0:T(8,128)}, f32[8,3,8,128]{3,2,1,0:T(8,128)S(1)}, f32[8,3,8,128]{3,2,1,0:T(8,128)S(1)}) custom-call(f32[8,256,256]{2,1,0:T(8,128)} %p_in.1, f32[8,256,256]{2,1,0:T(8,128)} %w_in.1, f32[256,256]{1,0:T(8,128)S(1)} %copy-done, f32[256,256]{1,0:T(8,128)S(1)} %copy-done.1), custom_call_target="tpu_custom_call" | custom-call | flops 10000000 | bytes 9437184 | tf_op jit(solution)/shard_map/turn/pallas_call | solution.py:158
  11.8 0.0 collective-permute-done.up_ref
  11.8 0.0 collective-permute-done.1.down_ref
  11.9 0.1 rows.1
  12.0 1.4 %collective-permute-start.2 = (f32[9,3,8,128]{3,2,1,0:T(8,128)S(1)}, f32[9,3,8,128]{3,2,1,0:T(8,128)S(1)}, u32[]{:S(2)}, u32[]{:S(2)}) collective-permute-start(f32[9,3,8,128]{3,2,1,0:T(8,128)S(1)} %get-tuple-element.38), channel_id=1, source_target_pairs={{0,1},{1,2},{2,3},{3,0},{4,5},{5,6},{6,7},{7,4},{8,9},{9,10},{10,1... | collective-permute-start | bytes 331784 | tf_op jit(solution)/shard_map/ppermute | solution.py:583
  13.4 1.5 %collective-permute-start.3 = (f32[9,3,8,128]{3,2,1,0:T(8,128)S(1)}, f32[9,3,8,128]{3,2,1,0:T(8,128)S(1)}, u32[]{:S(2)}, u32[]{:S(2)}) collective-permute-start(f32[9,3,8,128]{3,2,1,0:T(8,128)S(1)} %get-tuple-element.39), channel_id=1, source_target_pairs={{0,3},{1,0},{2,1},{3,2},{4,7},{5,4},{6,5},{7,6},{8,11},{9,8},{10,9... | collective-permute-start | bytes 331784 | tf_op jit(solution)/shard_map/ppermute | solution.py:584
  14.9 0.3 dynamic_update_slice.6
  15.2 0.2 dynamic_update_slice.7
  15.4 1.5 %collective-permute-done.2.fl_ref = f32[9,3,8,128]{3,2,1,0:T(8,128)S(1)} collective-permute-done((f32[9,3,8,128]{3,2,1,0:T(8,128)S(1)}, f32[9,3,8,128]{3,2,1,0:T(8,128)S(1)}, u32[]{:S(2)}, u32[]{:S(2)}) %collective-permute-start.2) | collective-permute-done | bytes 110624 | tf_op jit(solution)/shard_map/ppermute | solution.py:583
  16.9 0.0 collective-permute-done.3.fr_ref
  17.0 20.1 %steps.1 = (f32[512,8,128]{2,1,0:T(8,128)S(1)}, bf16[256,8,256]{2,1,0:T(8,128)(2,1)S(1)}) custom-call(f32[256,8,256]{2,1,0:T(8,128)} %get-tuple-element.30.pt_in, f32[256,8,256]{2,1,0:T(8,128)} %get-tuple-element.31.wt_in, f32[256,256]{1,0:T(8,128)S(1)} %copy-done, f32[256,256]{1,0:T(8,128)S(1)} %copy-done.1, f32[9,8,256]{2,1,0:T(8,128)S(1)} %get-tuple-element.36.above_ref, ...), custom_call_target="tpu_custom_call" | custom-call | tf_op jit(solution)/shard_map/steps/pallas_call | solution.py:365
  37.1 2.5 %collective-permute-start.5 = (bf16[256,8,256]{2,1,0:T(8,128)(2,1)S(1)}, bf16[256,8,256]{2,1,0:T(8,128)(2,1)S(1)}, u32[]{:S(2)}, u32[]{:S(2)}) collective-permute-start(bf16[256,8,256]{2,1,0:T(8,128)(2,1)S(1)} %get-tuple-element.42.refs_0_), channel_id=1, source_target_pairs={{0,16},{16,0},{32,48},{48,32},{64,80},{80,64},{96,112},{112,96},{1... | collective-permute-start | bytes 3145736 | tf_op jit(solution)/shard_map/ppermute | solution.py:592
  39.6 2.7 %picks.1 = f32[8,1024]{1,0:T(8,128)S(1)} custom-call(s32[8,128]{1,0:T(8,128)S(1)} %copy-done.4, f32[512,8,128]{2,1,0:T(8,128)S(1)} %get-tuple-element.40.f_ref.refs_6_, f32[8,128]{1,0:T(8,128)S(1)} %copy-done.5), custom_call_target="tpu_custom_call" | custom-call | tf_op jit(solution)/shard_map/picks/pallas_call | solution.py:396
  42.3 1.4 %collective-permute-start.4 = (f32[8,2176]{1,0:T(8,128)S(1)}, f32[8,2176]{1,0:T(8,128)S(1)}, u32[]{:S(2)}, u32[]{:S(2)}) collective-permute-start(f32[8,2176]{1,0:T(8,128)S(1)} %pad_maximum_fusion), channel_id=1, source_target_pairs={{0,1},{1,0},{2,3},{3,2},{4,5},{5,4},{6,7},{7,6},{8,9},{9,8},{10,11... | collective-permute-start | bytes 208904 | tf_op jit(solution)/shard_map/ppermute | solution.py:609
  43.7 1.2 %collective-permute-start.10 = (bf16[256,8,256]{2,1,0:T(8,128)(2,1)S(1)}, bf16[256,8,256]{2,1,0:T(8,128)(2,1)S(1)}, u32[]{:S(2)}, u32[]{:S(2)}) collective-permute-start(bf16[256,8,256]{2,1,0:T(8,128)(2,1)S(1)} %get-tuple-element.42.refs_0_), channel_id=1, source_target_pairs={{0,96},{16,48},{32,0},{48,80},{64,32},{80,112},{96,64},{112,16},{1... | collective-permute-start | bytes 3145736 | tf_op jit(solution)/shard_map/ppermute | solution.py:592
  44.9 1.5 %collective-permute-start.9 = (bf16[256,8,256]{2,1,0:T(8,128)(2,1)S(1)}, bf16[256,8,256]{2,1,0:T(8,128)(2,1)S(1)}, u32[]{:S(2)}, u32[]{:S(2)}) collective-permute-start(bf16[256,8,256]{2,1,0:T(8,128)(2,1)S(1)} %get-tuple-element.42.refs_0_), channel_id=1, source_target_pairs={{0,32},{16,112},{32,64},{48,16},{64,96},{80,48},{96,0},{112,80},{1... | collective-permute-start | bytes 3145736 | tf_op jit(solution)/shard_map/ppermute | solution.py:592
  46.3 0.0 collective-permute-done.4
  46.4 0.0 collective-permute-done.5.refs_3_
  46.4 2.6 %collective-permute-start.6 = (f32[8,2176]{1,0:T(8,128)S(1)}, f32[8,2176]{1,0:T(8,128)S(1)}, u32[]{:S(2)}, u32[]{:S(2)}) collective-permute-start(f32[8,2176]{1,0:T(8,128)S(1)} %fusion), channel_id=1, source_target_pairs={{0,2},{1,3},{2,0},{3,1},{4,6},{5,7},{6,4},{7,5},{8,10},{9,11},{10,... | collective-permute-start | bytes 208904 | tf_op jit(solution)/shard_map/ppermute | solution.py:609
  48.9 2.2 %collective-permute-done.6 = f32[8,2176]{1,0:T(8,128)S(1)} collective-permute-done((f32[8,2176]{1,0:T(8,128)S(1)}, f32[8,2176]{1,0:T(8,128)S(1)}, u32[]{:S(2)}, u32[]{:S(2)}) %collective-permute-start.6) | collective-permute-done | bytes 69664 | tf_op jit(solution)/shard_map/ppermute | solution.py:609
  51.1 0.1 collective-permute-start.7
  51.2 3.4 %collective-permute-done.7 = f32[8,2176]{1,0:T(8,128)S(1)} collective-permute-done((f32[8,2176]{1,0:T(8,128)S(1)}, f32[8,2176]{1,0:T(8,128)S(1)}, u32[]{:S(2)}, u32[]{:S(2)}) %collective-permute-start.7) | collective-permute-done | bytes 69664 | tf_op jit(solution)/shard_map/ppermute | solution.py:609
  54.7 1.6 %collective-permute-start.8 = (f32[8,2176]{1,0:T(8,128)S(1)}, f32[8,2176]{1,0:T(8,128)S(1)}, u32[]{:S(2)}, u32[]{:S(2)}) collective-permute-start(f32[8,2176]{1,0:T(8,128)S(1)} %add.46), channel_id=1, source_target_pairs={{0,8},{4,12},{8,0},{12,4},{1,9},{5,13},{9,1},{13,5},{2,10},{6,14},... | collective-permute-start | bytes 208904 | tf_op jit(solution)/shard_map/ppermute | solution.py:609
  56.3 3.1 %collective-permute-done.8 = f32[8,2176]{1,0:T(8,128)S(1)} collective-permute-done((f32[8,2176]{1,0:T(8,128)S(1)}, f32[8,2176]{1,0:T(8,128)S(1)}, u32[]{:S(2)}, u32[]{:S(2)}) %collective-permute-start.8) | collective-permute-done | bytes 69664 | tf_op jit(solution)/shard_map/ppermute | solution.py:609
  59.5 7.1 %collective-permute-done.10.refs_2_ = bf16[256,8,256]{2,1,0:T(8,128)(2,1)S(1)} collective-permute-done((bf16[256,8,256]{2,1,0:T(8,128)(2,1)S(1)}, bf16[256,8,256]{2,1,0:T(8,128)(2,1)S(1)}, u32[]{:S(2)}, u32[]{:S(2)}) %collective-permute-start.10) | collective-permute-done | bytes 1048608 | tf_op jit(solution)/shard_map/ppermute | solution.py:592
  66.5 3.1 %collective-permute-done.9.refs_1_ = bf16[256,8,256]{2,1,0:T(8,128)(2,1)S(1)} collective-permute-done((bf16[256,8,256]{2,1,0:T(8,128)(2,1)S(1)}, bf16[256,8,256]{2,1,0:T(8,128)(2,1)S(1)}, u32[]{:S(2)}, u32[]{:S(2)}) %collective-permute-start.9) | collective-permute-done | bytes 1048608 | tf_op jit(solution)/shard_map/ppermute | solution.py:592
  69.6 2.5 %collective-permute-start.11 = (f32[8,1024]{1,0:T(8,128)S(1)}, f32[8,1024]{1,0:T(8,128)S(1)}, u32[]{:S(2)}, u32[]{:S(2)}) collective-permute-start(f32[8,1024]{1,0:T(8,128)S(1)} %get-tuple-element.44), channel_id=1, source_target_pairs={{0,32},{16,112},{32,64},{48,16},{64,96},{80,48},{96,0},{112,80},{1... | collective-permute-start | bytes 98312 | tf_op jit(solution)/shard_map/ppermute | solution.py:592
  72.2 0.0 collective-permute-start.12
  72.2 1.5 %collective-permute-start.13 = (f32[8,1024]{1,0:T(8,128)S(1)}, f32[8,1024]{1,0:T(8,128)S(1)}, u32[]{:S(2)}, u32[]{:S(2)}) collective-permute-start(f32[8,1024]{1,0:T(8,128)S(1)} %get-tuple-element.44), channel_id=1, source_target_pairs={{0,64},{16,80},{32,96},{48,112},{64,0},{80,16},{96,32},{112,48},{1... | collective-permute-start | bytes 98312 | tf_op jit(solution)/shard_map/ppermute | solution.py:592
  73.7 2.5 %collective-permute-done.12 = f32[8,1024]{1,0:T(8,128)S(1)} collective-permute-done((f32[8,1024]{1,0:T(8,128)S(1)}, f32[8,1024]{1,0:T(8,128)S(1)}, u32[]{:S(2)}, u32[]{:S(2)}) %collective-permute-start.12) | collective-permute-done | bytes 32800 | tf_op jit(solution)/shard_map/ppermute | solution.py:592
  76.2 0.3 collective-permute-done.13
  76.5 2.6 %collective-permute-start.14 = (f32[32,1024]{1,0:T(8,128)S(1)}, f32[32,1024]{1,0:T(8,128)S(1)}, u32[]{:S(2)}, u32[]{:S(2)}) collective-permute-start(f32[32,1024]{1,0:T(8,128)S(1)} %constant_dynamic-update-slice_fusion.near_ref), channel_id=1, source_target_pairs={{0,16},{16,0},{32,48},{48,32},{64,80},{80,64},{96,112},{112,96},{1... | collective-permute-start | bytes 393224 | tf_op jit(solution)/shard_map/ppermute | solution.py:592
  79.1 1.0 collective-permute-done.14.far_ref
  80.1 0.4 collective-permute-start.19
  80.5 0.1 collective-permute-start.20
  80.7 1.5 %collective-permute-start.15 = (bf16[128,8,256]{2,1,0:T(8,128)(2,1)S(1)}, bf16[128,8,256]{2,1,0:T(8,128)(2,1)S(1)}, u32[]{:S(2)}, u32[]{:S(2)}) collective-permute-start(bf16[128,8,256]{2,1,0:T(8,128)(2,1)S(1)} %slice.18), channel_id=1, source_target_pairs={{0,32},{16,112},{32,64},{48,16},{64,96},{80,48},{96,0},{112,80},{1... | collective-permute-start | bytes 1572872 | tf_op jit(solution)/shard_map/ppermute | solution.py:592
  82.2 0.1 collective-permute-start.16
  82.3 11.4 %collective-permute-done.15.refs_0_ = bf16[128,8,256]{2,1,0:T(8,128)(2,1)S(1)} collective-permute-done((bf16[128,8,256]{2,1,0:T(8,128)(2,1)S(1)}, bf16[128,8,256]{2,1,0:T(8,128)(2,1)S(1)}, u32[]{:S(2)}, u32[]{:S(2)}) %collective-permute-start.15) | collective-permute-done | bytes 524320 | tf_op jit(solution)/shard_map/ppermute | solution.py:592
  93.7 2.6 %collective-permute-start.17 = (bf16[128,8,256]{2,1,0:T(8,128)(2,1)S(1)}, bf16[128,8,256]{2,1,0:T(8,128)(2,1)S(1)}, u32[]{:S(2)}, u32[]{:S(2)}) collective-permute-start(bf16[128,8,256]{2,1,0:T(8,128)(2,1)S(1)} %collective-permute-done.15.refs_0_), channel_id=1, source_target_pairs={{0,16},{16,0},{32,48},{48,32},{64,80},{80,64},{96,112},{112,96},{1... | collective-permute-start | bytes 1572872 | tf_op jit(solution)/shard_map/ppermute | solution.py:592
  96.3 0.1 collective-permute-done.16.refs_1_
  96.4 2.6 %weights.1 = (f32[8,48]{1,0:T(8,128)S(1)}, f32[8,16]{1,0:T(8,128)S(1)}) custom-call(f32[32,1024]{1,0:T(8,128)S(1)} %constant_dynamic-update-slice_fusion.near_ref, f32[32,1024]{1,0:T(8,128)S(1)} %collective-permute-done.14.far_ref, f32[8,1024]{1,0:T(8,128)S(1)} %get-tuple-element.53.target_ref, f32[8,128]{1,0:T(8,128)S(1)} %slice.22.error_ref), custom_call_target="tpu_custom_call" | custom-call | tf_op jit(solution)/shard_map/weights/pallas_call | solution.py:472
  99.0 0.0 collective-permute-done.20.refs_5_
  99.1 3.0 %begin.1.refs_4_ = f32[512,8,128]{2,1,0:T(8,128)S(1)} custom-call(f32[8,48]{1,0:T(8,128)S(1)} %get-tuple-element.49.w_ref, bf16[256,8,256]{2,1,0:T(8,128)(2,1)S(1)} %get-tuple-element.42.refs_0_, bf16[256,8,256]{2,1,0:T(8,128)(2,1)S(1)} %collective-permute-done.9.refs_1_, bf16[256,8,256]{2,1,0:T(8,128)(2,1)S(1)} %collective-permute-done.10.refs_2_, ...), custom_call_target="tpu_custom_call" | custom-call | tf_op jit(solution)/shard_map/begin/pallas_call | solution.py:537
  102.1 2.5 %update.1 = f32[8,256,256]{2,1,0:T(8,128)} custom-call(f32[8,16]{1,0:T(8,128)S(1)} %get-tuple-element.48.w_ref, bf16[128,8,256]{2,1,0:T(8,128)(2,1)S(1)} %collective-permute-done.15.refs_0_, bf16[128,8,256]{2,1,0:T(8,128)(2,1)S(1)} %collective-permute-done.16.refs_1_, bf16[128,8,256]{2,1,0:T(8,128)(2,1)S(1)} %collective-permute-done.17.refs_2_, ...), custom_call_target="tpu_custom_call" | custom-call | tf_op jit(solution)/shard_map/update/pallas_call | solution.py:552
  (38 shorter events, 0.2 us)
Async XLA Ops:
  0.0 7.6 %copy-start = (f32[256,256]{1,0:T(8,128)S(1)}, f32[256,256]{1,0:T(8,128)}, u32[]{:S(2)}) copy-start(f32[256,256]{1,0:T(8,128)} %e_ref.5) | copy-start | bytes 786436
  0.0 7.6 %copy-start.1 = (f32[256,256]{1,0:T(8,128)S(1)}, f32[256,256]{1,0:T(8,128)}, u32[]{:S(2)}) copy-start(f32[256,256]{1,0:T(8,128)} %k_ref.5) | copy-start | bytes 786436
  2.8 9.1 %collective-permute-start = (f32[9,8,256]{2,1,0:T(8,128)}, f32[9,8,256]{2,1,0:T(8,128)S(1)}, u32[]{:S(2)}, u32[]{:S(2)}) collective-permute-start(f32[9,8,256]{2,1,0:T(8,128)} %get-tuple-element.32.bottom_ref), channel_id=1, source_target_pairs={{0,4},{4,8},{8,12},{12,0},{1,5},{5,9},{9,13},{13,1},{2,6},{6,10},{... | collective-permute-start | bytes 221192 | tf_op jit(solution)/shard_map/ppermute | solution.py:579
  5.3 6.6 %copy-start.2 = (f32[9,8,256]{2,1,0:T(8,128)S(1)}, f32[9,8,256]{2,1,0:T(8,128)}, u32[]{:S(2)}) copy-start(f32[9,8,256]{2,1,0:T(8,128)} %get-tuple-element.33.top_ref) | copy-start | bytes 221188
  5.3 6.6 %copy-start.3 = (f32[9,8,256]{2,1,0:T(8,128)S(1)}, f32[9,8,256]{2,1,0:T(8,128)}, u32[]{:S(2)}) copy-start(f32[9,8,256]{2,1,0:T(8,128)} %get-tuple-element.32.bottom_ref) | copy-start | bytes 221188
  5.3 9.6 %copy-start.6 = (f32[64,8]{0,1:T(8,128)S(1)}, f32[64,8]{0,1:T(8,128)}, u32[]{:S(2)}) copy-start(f32[64,8]{0,1:T(8,128)} %param.15) | copy-start | bytes 6148
  5.3 9.6 %copy-start.7 = (f32[64]{0:T(128)S(1)}, f32[64]{0:T(128)}, u32[]{:S(2)}) copy-start(f32[64]{0:T(128)} %param.14) | copy-start | bytes 772
  5.3 9.6 %copy-start.8 = (f32[64]{0:T(128)S(1)}, f32[64]{0:T(128)}, u32[]{:S(2)}) copy-start(f32[64]{0:T(128)} %param.13) | copy-start | bytes 772
  5.3 6.5 %collective-permute-start.1 = (f32[9,8,256]{2,1,0:T(8,128)}, f32[9,8,256]{2,1,0:T(8,128)S(1)}, u32[]{:S(2)}, u32[]{:S(2)}) collective-permute-start(f32[9,8,256]{2,1,0:T(8,128)} %get-tuple-element.33.top_ref), channel_id=1, source_target_pairs={{0,12},{4,0},{8,4},{12,8},{1,13},{5,1},{9,5},{13,9},{2,14},{6,2},{... | collective-permute-start | bytes 221192 | tf_op jit(solution)/shard_map/ppermute | solution.py:580
  12.0 4.9 %collective-permute-start.2 = (f32[9,3,8,128]{3,2,1,0:T(8,128)S(1)}, f32[9,3,8,128]{3,2,1,0:T(8,128)S(1)}, u32[]{:S(2)}, u32[]{:S(2)}) collective-permute-start(f32[9,3,8,128]{3,2,1,0:T(8,128)S(1)} %get-tuple-element.38), channel_id=1, source_target_pairs={{0,1},{1,2},{2,3},{3,0},{4,5},{5,6},{6,7},{7,4},{8,9},{9,10},{10,1... | collective-permute-start | bytes 331784 | tf_op jit(solution)/shard_map/ppermute | solution.py:583
  13.4 3.6 %collective-permute-start.3 = (f32[9,3,8,128]{3,2,1,0:T(8,128)S(1)}, f32[9,3,8,128]{3,2,1,0:T(8,128)S(1)}, u32[]{:S(2)}, u32[]{:S(2)}) collective-permute-start(f32[9,3,8,128]{3,2,1,0:T(8,128)S(1)} %get-tuple-element.39), channel_id=1, source_target_pairs={{0,3},{1,0},{2,1},{3,2},{4,7},{5,4},{6,5},{7,6},{8,11},{9,8},{10,9... | collective-permute-start | bytes 331784 | tf_op jit(solution)/shard_map/ppermute | solution.py:584
  17.0 22.6 %copy-start.4 = (s32[8,128]{1,0:T(8,128)S(1)}, s32[8,128]{1,0:T(8,128)}, u32[]{:S(2)}) copy-start(s32[8,128]{1,0:T(8,128)} %get-tuple-element.29.code_ref) | copy-start | bytes 12292
  17.0 22.6 %copy-start.5 = (f32[8,128]{1,0:T(8,128)S(1)}, f32[8,128]{1,0:T(8,128)}, u32[]{:S(2)}) copy-start(f32[8,128]{1,0:T(8,128)} %get-tuple-element.41.inside_ref) | copy-start | bytes 12292
  37.1 9.3 %collective-permute-start.5 = (bf16[256,8,256]{2,1,0:T(8,128)(2,1)S(1)}, bf16[256,8,256]{2,1,0:T(8,128)(2,1)S(1)}, u32[]{:S(2)}, u32[]{:S(2)}) collective-permute-start(bf16[256,8,256]{2,1,0:T(8,128)(2,1)S(1)} %get-tuple-element.42.refs_0_), channel_id=1, source_target_pairs={{0,16},{16,0},{32,48},{48,32},{64,80},{80,64},{96,112},{112,96},{1... | collective-permute-start | bytes 3145736 | tf_op jit(solution)/shard_map/ppermute | solution.py:592
  42.3 4.1 %collective-permute-start.4 = (f32[8,2176]{1,0:T(8,128)S(1)}, f32[8,2176]{1,0:T(8,128)S(1)}, u32[]{:S(2)}, u32[]{:S(2)}) collective-permute-start(f32[8,2176]{1,0:T(8,128)S(1)} %pad_maximum_fusion), channel_id=1, source_target_pairs={{0,1},{1,0},{2,3},{3,2},{4,5},{5,4},{6,7},{7,6},{8,9},{9,8},{10,11... | collective-permute-start | bytes 208904 | tf_op jit(solution)/shard_map/ppermute | solution.py:609
  43.7 22.9 %collective-permute-start.10 = (bf16[256,8,256]{2,1,0:T(8,128)(2,1)S(1)}, bf16[256,8,256]{2,1,0:T(8,128)(2,1)S(1)}, u32[]{:S(2)}, u32[]{:S(2)}) collective-permute-start(bf16[256,8,256]{2,1,0:T(8,128)(2,1)S(1)} %get-tuple-element.42.refs_0_), channel_id=1, source_target_pairs={{0,96},{16,48},{32,0},{48,80},{64,32},{80,112},{96,64},{112,16},{1... | collective-permute-start | bytes 3145736 | tf_op jit(solution)/shard_map/ppermute | solution.py:592
  44.9 24.7 %collective-permute-start.9 = (bf16[256,8,256]{2,1,0:T(8,128)(2,1)S(1)}, bf16[256,8,256]{2,1,0:T(8,128)(2,1)S(1)}, u32[]{:S(2)}, u32[]{:S(2)}) collective-permute-start(bf16[256,8,256]{2,1,0:T(8,128)(2,1)S(1)} %get-tuple-element.42.refs_0_), channel_id=1, source_target_pairs={{0,32},{16,112},{32,64},{48,16},{64,96},{80,48},{96,0},{112,80},{1... | collective-permute-start | bytes 3145736 | tf_op jit(solution)/shard_map/ppermute | solution.py:592
  46.4 4.7 %collective-permute-start.6 = (f32[8,2176]{1,0:T(8,128)S(1)}, f32[8,2176]{1,0:T(8,128)S(1)}, u32[]{:S(2)}, u32[]{:S(2)}) collective-permute-start(f32[8,2176]{1,0:T(8,128)S(1)} %fusion), channel_id=1, source_target_pairs={{0,2},{1,3},{2,0},{3,1},{4,6},{5,7},{6,4},{7,5},{8,10},{9,11},{10,... | collective-permute-start | bytes 208904 | tf_op jit(solution)/shard_map/ppermute | solution.py:609
  51.1 3.5 %collective-permute-start.7 = (f32[8,2176]{1,0:T(8,128)S(1)}, f32[8,2176]{1,0:T(8,128)S(1)}, u32[]{:S(2)}, u32[]{:S(2)}) collective-permute-start(f32[8,2176]{1,0:T(8,128)S(1)} %add.45), channel_id=1, source_target_pairs={{0,4},{4,0},{8,12},{12,8},{1,5},{5,1},{9,13},{13,9},{2,6},{6,2},{1... | collective-permute-start | bytes 208904 | tf_op jit(solution)/shard_map/ppermute | solution.py:609
  54.7 4.7 %collective-permute-start.8 = (f32[8,2176]{1,0:T(8,128)S(1)}, f32[8,2176]{1,0:T(8,128)S(1)}, u32[]{:S(2)}, u32[]{:S(2)}) collective-permute-start(f32[8,2176]{1,0:T(8,128)S(1)} %add.46), channel_id=1, source_target_pairs={{0,8},{4,12},{8,0},{12,4},{1,9},{5,13},{9,1},{13,5},{2,10},{6,14},... | collective-permute-start | bytes 208904 | tf_op jit(solution)/shard_map/ppermute | solution.py:609
  69.6 4.1 %collective-permute-start.11 = (f32[8,1024]{1,0:T(8,128)S(1)}, f32[8,1024]{1,0:T(8,128)S(1)}, u32[]{:S(2)}, u32[]{:S(2)}) collective-permute-start(f32[8,1024]{1,0:T(8,128)S(1)} %get-tuple-element.44), channel_id=1, source_target_pairs={{0,32},{16,112},{32,64},{48,16},{64,96},{80,48},{96,0},{112,80},{1... | collective-permute-start | bytes 98312 | tf_op jit(solution)/shard_map/ppermute | solution.py:592
  72.2 4.0 %collective-permute-start.12 = (f32[8,1024]{1,0:T(8,128)S(1)}, f32[8,1024]{1,0:T(8,128)S(1)}, u32[]{:S(2)}, u32[]{:S(2)}) collective-permute-start(f32[8,1024]{1,0:T(8,128)S(1)} %get-tuple-element.44), channel_id=1, source_target_pairs={{0,96},{16,48},{32,0},{48,80},{64,32},{80,112},{96,64},{112,16},{1... | collective-permute-start | bytes 98312 | tf_op jit(solution)/shard_map/ppermute | solution.py:592
  72.2 4.3 %collective-permute-start.13 = (f32[8,1024]{1,0:T(8,128)S(1)}, f32[8,1024]{1,0:T(8,128)S(1)}, u32[]{:S(2)}, u32[]{:S(2)}) collective-permute-start(f32[8,1024]{1,0:T(8,128)S(1)} %get-tuple-element.44), channel_id=1, source_target_pairs={{0,64},{16,80},{32,96},{48,112},{64,0},{80,16},{96,32},{112,48},{1... | collective-permute-start | bytes 98312 | tf_op jit(solution)/shard_map/ppermute | solution.py:592
  76.5 3.6 %collective-permute-start.14 = (f32[32,1024]{1,0:T(8,128)S(1)}, f32[32,1024]{1,0:T(8,128)S(1)}, u32[]{:S(2)}, u32[]{:S(2)}) collective-permute-start(f32[32,1024]{1,0:T(8,128)S(1)} %constant_dynamic-update-slice_fusion.near_ref), channel_id=1, source_target_pairs={{0,16},{16,0},{32,48},{48,32},{64,80},{80,64},{96,112},{112,96},{1... | collective-permute-start | bytes 393224 | tf_op jit(solution)/shard_map/ppermute | solution.py:592
  80.1 18.9 %collective-permute-start.19 = (bf16[256,8,256]{2,1,0:T(8,128)(2,1)S(1)}, bf16[256,8,256]{2,1,0:T(8,128)(2,1)S(1)}, u32[]{:S(2)}, u32[]{:S(2)}) collective-permute-start(bf16[256,8,256]{2,1,0:T(8,128)(2,1)S(1)} %collective-permute-done.9.refs_1_), channel_id=1, source_target_pairs={{0,16},{16,0},{32,48},{48,32},{64,80},{80,64},{96,112},{112,96},{1... | collective-permute-start | bytes 3145736 | tf_op jit(solution)/shard_map/ppermute | solution.py:592
  80.5 18.6 %collective-permute-start.20 = (bf16[256,8,256]{2,1,0:T(8,128)(2,1)S(1)}, bf16[256,8,256]{2,1,0:T(8,128)(2,1)S(1)}, u32[]{:S(2)}, u32[]{:S(2)}) collective-permute-start(bf16[256,8,256]{2,1,0:T(8,128)(2,1)S(1)} %collective-permute-done.10.refs_2_), channel_id=1, source_target_pairs={{0,16},{16,0},{32,48},{48,32},{64,80},{80,64},{96,112},{112,96},{1... | collective-permute-start | bytes 3145736 | tf_op jit(solution)/shard_map/ppermute | solution.py:592
  80.7 13.1 %collective-permute-start.15 = (bf16[128,8,256]{2,1,0:T(8,128)(2,1)S(1)}, bf16[128,8,256]{2,1,0:T(8,128)(2,1)S(1)}, u32[]{:S(2)}, u32[]{:S(2)}) collective-permute-start(bf16[128,8,256]{2,1,0:T(8,128)(2,1)S(1)} %slice.18), channel_id=1, source_target_pairs={{0,32},{16,112},{32,64},{48,16},{64,96},{80,48},{96,0},{112,80},{1... | collective-permute-start | bytes 1572872 | tf_op jit(solution)/shard_map/ppermute | solution.py:592
  82.2 14.2 %collective-permute-start.16 = (bf16[128,8,256]{2,1,0:T(8,128)(2,1)S(1)}, bf16[128,8,256]{2,1,0:T(8,128)(2,1)S(1)}, u32[]{:S(2)}, u32[]{:S(2)}) collective-permute-start(bf16[128,8,256]{2,1,0:T(8,128)(2,1)S(1)} %slice.19), channel_id=1, source_target_pairs={{0,96},{16,48},{32,0},{48,80},{64,32},{80,112},{96,64},{112,16},{1... | collective-permute-start | bytes 1572872 | tf_op jit(solution)/shard_map/ppermute | solution.py:592
  93.7 8.3 %collective-permute-start.17 = (bf16[128,8,256]{2,1,0:T(8,128)(2,1)S(1)}, bf16[128,8,256]{2,1,0:T(8,128)(2,1)S(1)}, u32[]{:S(2)}, u32[]{:S(2)}) collective-permute-start(bf16[128,8,256]{2,1,0:T(8,128)(2,1)S(1)} %collective-permute-done.15.refs_0_), channel_id=1, source_target_pairs={{0,16},{16,0},{32,48},{48,32},{64,80},{80,64},{96,112},{112,96},{1... | collective-permute-start | bytes 1572872 | tf_op jit(solution)/shard_map/ppermute | solution.py:592
  96.4 5.7 %collective-permute-start.18 = (bf16[128,8,256]{2,1,0:T(8,128)(2,1)S(1)}, bf16[128,8,256]{2,1,0:T(8,128)(2,1)S(1)}, u32[]{:S(2)}, u32[]{:S(2)}) collective-permute-start(bf16[128,8,256]{2,1,0:T(8,128)(2,1)S(1)} %collective-permute-done.16.refs_1_), channel_id=1, source_target_pairs={{0,16},{16,0},{32,48},{48,32},{64,80},{80,64},{96,112},{112,96},{1... | collective-permute-start | bytes 1572872 | tf_op jit(solution)/shard_map/ppermute | solution.py:592

commit v4 on v3

--- a/solution.py
+++ b/solution.py
@@ -10,7 +10,6 @@
 SUBSTEPS = 4
 W = SUBSTEPS
 GROUP = 128 // W
-ROWS = 16
 F32 = jnp.float32
 BF16 = jnp.bfloat16
 VMEM_SPEC = pl.BlockSpec(memory_space=pltpu.VMEM)
@@ -226,7 +225,7 @@
 def steps_kernel(
     pt_in, wt_in, e_ref, k_ref, above_ref, below_ref, fl_ref, fr_ref,
     out_ref, round_ref,
-    p0, p1, w_s, fy_s, sum_s, e_s, er_s, k_s, kr_s, sems,
+    p0, p1, w_s, fy_s, sum_s, fy2_s, sum2_s, e_s, er_s, k_s, kr_s, sems,
 ):
     size_x = pt_in.shape[0]
     lane = lanes()
@@ -303,44 +302,48 @@
     def row_of(ref, b, u):
         return [wide(ref[b, u : u + 1, 128 * t : 128 * t + 128]) for t in range(3)]
 
+    def finish(dst, at, sums, fluxes):
+        for u in range(8):
+            fy = tiles(fluxes, u)
+            fr = [pltpu.roll(v, 1, 1) for v in fy]
+            s = tiles(sums, u)
+            back = [jnp.where(is_first, fr[(t - 1) % 3], fr[t]) for t in range(3)]
+            put(dst, at * 8 + u, [s[t] + (fy[t] - back[t]) for t in range(3)])
+
+    def fluxes_of(src, at, sums, fluxes, carry):
+        p_old, h_old, c_old, fx_old, fy_old = carry
+        for u in range(8):
+            p = tiles(src, at * 8 + u + 1)
+            raw = [pltpu.roll(v, 127, 1) for v in p]
+            pr = [jnp.where(is_last, raw[(t + 1) % 3], raw[t]) for t in range(3)]
+            e, er = row_of(e_s, at, u), row_of(er_s, at, u)
+            k, kr = row_of(k_s, at, u), row_of(kr_s, at, u)
+            w = tiles(w_s, at * 8 + u)
+            h = [p[t] + e[t] for t in range(3)]
+            c = [k[t] * jnp.tanh(p[t]) + k[t] for t in range(3)]
+            fy = [
+                (c[t] + (kr[t] * jnp.tanh(pr[t]) + kr[t])) * ((pr[t] + er[t]) - h[t])
+                for t in range(3)
+            ]
+            fy[1] = fy[1] * mask_right
+            fy[2] = fy[2] * mask_left
+            fx = [(c_old[t] + c[t]) * (h[t] - h_old[t]) for t in range(3)]
+            put(sums, u, [(p_old[t] + w[t]) + (fx[t] - fx_old[t]) for t in range(3)])
+            put(fluxes, u, fy_old)
+            p_old, h_old, c_old, fx_old, fy_old = p, h, c, fx, fy
+        return p_old, h_old, c_old, fx_old, fy_old
+
     def step(src, dst):
-        count = 8 * blocks // ROWS
-
         def body(i, carry):
-            b_at = jnp.minimum(i, count - 1)
-            c_at = jnp.maximum(i - 1, 0) * ROWS
-            for u in range(ROWS):
-                at = c_at + u
-                s, fy = tiles(sum_s, at), tiles(fy_s, at)
-                fr = [pltpu.roll(v, 1, 1) for v in fy]
-                back = [jnp.where(is_first, fr[(t - 1) % 3], fr[t]) for t in range(3)]
-                put(dst, at, [s[t] + (fy[t] - back[t]) for t in range(3)])
-            p_old, h_old, c_old, fx_old = carry
-            for u in range(ROWS):
-                at = b_at * ROWS + u
-                block = (b_at * (ROWS // 8) + u // 8, u % 8)
-                p = tiles(src, at + 1)
-                raw = [pltpu.roll(v, 127, 1) for v in p]
-                pr = [jnp.where(is_last, raw[(t + 1) % 3], raw[t]) for t in range(3)]
-                e, er = row_of(e_s, *block), row_of(er_s, *block)
-                k, kr = row_of(k_s, *block), row_of(kr_s, *block)
-                w = tiles(w_s, at)
-                h = [p[t] + e[t] for t in range(3)]
-                c = [k[t] * jnp.tanh(p[t]) + k[t] for t in range(3)]
-                fy = [
-                    (c[t] + (kr[t] * jnp.tanh(pr[t]) + kr[t])) * ((pr[t] + er[t]) - h[t])
-                    for t in range(3)
-                ]
-                fy[1] = fy[1] * mask_right
-                fy[2] = fy[2] * mask_left
-                fx = [(c_old[t] + c[t]) * (h[t] - h_old[t]) for t in range(3)]
-                put(sum_s, at, [(p_old[t] + w[t]) + (fx[t] - fx_old[t]) for t in range(3)])
-                put(fy_s, at + 1, fy)
-                p_old, h_old, c_old, fx_old = p, h, c, fx
-            return p_old, h_old, c_old, fx_old
+            carry = fluxes_of(src, 2 * i, sum_s, fy_s, carry)
+            finish(dst, jnp.maximum(2 * i - 1, 0), sum2_s, fy2_s)
+            carry = fluxes_of(src, 2 * i + 1, sum2_s, fy2_s, carry)
+            finish(dst, 2 * i, sum_s, fy_s)
+            return carry
 
         zero = [jnp.zeros((8, 128), F32)] * 3
-        lax.fori_loop(0, count + 1, body, (zero, zero, zero, zero))
+        lax.fori_loop(0, blocks // 2, body, (zero,) * 5)
+        finish(dst, blocks - 1, sum2_s, fy2_s)
 
     for s in range(SUBSTEPS):
         step(*((p0, p1) if s % 2 == 0 else (p1, p0)))
@@ -362,11 +365,12 @@
     size_x, members, size_y = pt.shape
     tile = pltpu.VMEM((size_x + 17, members, size_y + 128), F32)
     flat = pltpu.VMEM((size_x // 8 + 2, 8, size_y + 128), F32)
+    few = pltpu.VMEM((8, members, size_y + 128), F32)
     return pl.pallas_call(
         steps_kernel,
         in_specs=[HBM_SPEC] * 2 + [VMEM_SPEC] * 6,
         out_specs=[VMEM_SPEC] * 2,
-        scratch_shapes=[tile] * 5 + [flat] * 4 + [pltpu.SemaphoreType.DMA((2,))],
+        scratch_shapes=[tile] * 3 + [few] * 4 + [flat] * 4 + [pltpu.SemaphoreType.DMA((2,))],
         out_shape=[
             jax.ShapeDtypeStruct((size_x * (size_y // 128), members, 128), F32),
             jax.ShapeDtypeStruct((size_x, members, size_y), BF16),
@@ -383,7 +387,7 @@
         acc = jnp.zeros((8, 128), F32)
         for u in range(128):
             code = code_ref[g, u]
-            v = pltpu.roll(f_ref[lax.shift_right_logical(code, 7)], code & 127, 1)
+            v = pltpu.roll(f_ref[lax.shift_right_logical(code, 7)], code, 1)
             acc = jnp.where(lane == u, v, acc)
         keep = wide(inside_ref[pl.ds(g, 1), :]) > F32(0.5)
         pick_ref[:, pl.ds(pl.multiple_of(g * 128, 128), 128)] = jnp.where(keep, acc, F32(0))

time: 105 us -> 103 us (0.981)
  Pallas kernels: 38 us -> 36 us
    pallas_call x1, Pallas kernels: 20.1 us -> 18.1 us  [run_steps(): pl.pallas_call(steps_kernel, in_specs=[HBM_SPEC] * 2 + [VMEM_SPEC] * 6, o...]
where the time goes in v4:
time: 103 us
  Pallas kernels  36 us (35%)
  waiting for transfers between devices  35.7 us (35%)
  starting transfers between devices  29.8 us (29%)
    ppermute x13, waiting for transfers between devices, send(): lax.ppermute(v, 'mem', [(i, i ^ 1) for i in range(n_m)] if swap else to)  25.4 us
    pallas_call x1, Pallas kernels, run_steps(): pl.pallas_call(steps_kernel, in_specs=[HBM_SPEC] * 2 + [VMEM_SPEC] * 6, o...  18.1 us
    ppermute x13, starting transfers between devices, send(): lax.ppermute(v, 'mem', [(i, i ^ 1) for i in range(n_m)] if swap else to)  16.6 us
    ppermute x4, waiting for transfers between devices, local(): line = line + lax.ppermute(line, axis, [(i, i ^ bit) for i in range(n)])  8.75 us
    ppermute x4, starting transfers between devices, local(): line = line + lax.ppermute(line, axis, [(i, i ^ bit) for i in range(n)])  5.64 us
    pallas_call x1, Pallas kernels, turn(): pl.pallas_call(turn_kernel, in_specs=[HBM_SPEC] * 2 + [VMEM_SPEC] * 2, ou...  4.27 us
    pallas_call x1, Pallas kernels, begin(): pl.pallas_call(begin_kernel, in_specs=[VMEM_SPEC] * (len(pieces) + 2), ou...  2.96 us
    pallas_call x1, Pallas kernels, ends(): pl.pallas_call(ends_kernel, in_specs=[VMEM_SPEC] + [HBM_SPEC] * 2 + [VMEM...  2.76 us
  transfers between devices with their start and end apart: 21, of which 11 were waited for; matrix products, arithmetic and copies ran while one was open for 1% of the time, Pallas kernels for 12%

profile of v4, /device:TPU:1, one launch (start us, length us, event | category | flops | bytes accessed | tf_op | source)
XLA Modules:
  0.0 102.6 jit_solution(16488277155609992818)
XLA Ops:
  0.0 2.8 %ends.1 = (f32[9,8,256]{2,1,0:T(8,128)}, f32[9,8,256]{2,1,0:T(8,128)}, s32[8,128]{1,0:T(8,128)}, f32[8,128]{1,0:T(8,128)}) custom-call(s32[8,128]{1,0:T(8,128)} %bitcast.4, f32[8,256,256]{2,1,0:T(8,128)} %p_in.1, f32[8,256,256]{2,1,0:T(8,128)} %w_in.1, f32[256,256]{1,0:T(8,128)} %e_ref.5, f32[256,256]{1,0:T(8,128)} %k_ref.5), custom_call_target="tpu_custom_call" | custom-call | tf_op jit(solution)/shard_map/ends/pallas_call | solution.py:75
  2.8 2.5 %collective-permute-start = (f32[9,8,256]{2,1,0:T(8,128)}, f32[9,8,256]{2,1,0:T(8,128)S(1)}, u32[]{:S(2)}, u32[]{:S(2)}) collective-permute-start(f32[9,8,256]{2,1,0:T(8,128)} %get-tuple-element.32.bottom_ref), channel_id=1, source_target_pairs={{0,4},{4,8},{8,12},{12,0},{1,5},{5,9},{9,13},{13,1},{2,6},{6,10},{... | collective-permute-start | bytes 221192 | tf_op jit(solution)/shard_map/ppermute | solution.py:583
  5.3 0.0 copy-start.8
  5.3 2.2 %collective-permute-start.1 = (f32[9,8,256]{2,1,0:T(8,128)}, f32[9,8,256]{2,1,0:T(8,128)S(1)}, u32[]{:S(2)}, u32[]{:S(2)}) collective-permute-start(f32[9,8,256]{2,1,0:T(8,128)} %get-tuple-element.33.top_ref), channel_id=1, source_target_pairs={{0,12},{4,0},{8,4},{12,8},{1,13},{5,1},{9,5},{13,9},{2,14},{6,2},{... | collective-permute-start | bytes 221192 | tf_op jit(solution)/shard_map/ppermute | solution.py:584
  7.6 4.3 %turn.1 = (f32[256,8,256]{2,1,0:T(8,128)}, f32[256,8,256]{2,1,0:T(8,128)}, f32[8,3,8,128]{3,2,1,0:T(8,128)S(1)}, f32[8,3,8,128]{3,2,1,0:T(8,128)S(1)}) custom-call(f32[8,256,256]{2,1,0:T(8,128)} %p_in.1, f32[8,256,256]{2,1,0:T(8,128)} %w_in.1, f32[256,256]{1,0:T(8,128)S(1)} %copy-done, f32[256,256]{1,0:T(8,128)S(1)} %copy-done.1), custom_call_target="tpu_custom_call" | custom-call | flops 10000000 | bytes 9437184 | tf_op jit(solution)/shard_map/turn/pallas_call | solution.py:157
  11.8 0.0 collective-permute-done.up_ref
  11.8 0.0 collective-permute-done.1.down_ref
  11.9 0.1 rows.1
  12.0 1.4 %collective-permute-start.2 = (f32[9,3,8,128]{3,2,1,0:T(8,128)S(1)}, f32[9,3,8,128]{3,2,1,0:T(8,128)S(1)}, u32[]{:S(2)}, u32[]{:S(2)}) collective-permute-start(f32[9,3,8,128]{3,2,1,0:T(8,128)S(1)} %get-tuple-element.38), channel_id=1, source_target_pairs={{0,1},{1,2},{2,3},{3,0},{4,5},{5,6},{6,7},{7,4},{8,9},{9,10},{10,1... | collective-permute-start | bytes 331784 | tf_op jit(solution)/shard_map/ppermute | solution.py:587
  13.4 1.5 %collective-permute-start.3 = (f32[9,3,8,128]{3,2,1,0:T(8,128)S(1)}, f32[9,3,8,128]{3,2,1,0:T(8,128)S(1)}, u32[]{:S(2)}, u32[]{:S(2)}) collective-permute-start(f32[9,3,8,128]{3,2,1,0:T(8,128)S(1)} %get-tuple-element.39), channel_id=1, source_target_pairs={{0,3},{1,0},{2,1},{3,2},{4,7},{5,4},{6,5},{7,6},{8,11},{9,8},{10,9... | collective-permute-start | bytes 331784 | tf_op jit(solution)/shard_map/ppermute | solution.py:588
  14.9 0.3 dynamic_update_slice.6
  15.2 0.2 dynamic_update_slice.7
  15.4 1.5 %collective-permute-done.2.fl_ref = f32[9,3,8,128]{3,2,1,0:T(8,128)S(1)} collective-permute-done((f32[9,3,8,128]{3,2,1,0:T(8,128)S(1)}, f32[9,3,8,128]{3,2,1,0:T(8,128)S(1)}, u32[]{:S(2)}, u32[]{:S(2)}) %collective-permute-start.2) | collective-permute-done | bytes 110624 | tf_op jit(solution)/shard_map/ppermute | solution.py:587
  16.9 0.0 collective-permute-done.3.fr_ref
  17.0 18.1 %steps.1 = (f32[512,8,128]{2,1,0:T(8,128)S(1)}, bf16[256,8,256]{2,1,0:T(8,128)(2,1)S(1)}) custom-call(f32[256,8,256]{2,1,0:T(8,128)} %get-tuple-element.30.pt_in, f32[256,8,256]{2,1,0:T(8,128)} %get-tuple-element.31.wt_in, f32[256,256]{1,0:T(8,128)S(1)} %copy-done, f32[256,256]{1,0:T(8,128)S(1)} %copy-done.1, f32[9,8,256]{2,1,0:T(8,128)S(1)} %get-tuple-element.36.above_ref, ...), custom_call_target="tpu_custom_call" | custom-call | tf_op jit(solution)/shard_map/steps/pallas_call | solution.py:369
  35.1 2.5 %collective-permute-start.5 = (bf16[256,8,256]{2,1,0:T(8,128)(2,1)S(1)}, bf16[256,8,256]{2,1,0:T(8,128)(2,1)S(1)}, u32[]{:S(2)}, u32[]{:S(2)}) collective-permute-start(bf16[256,8,256]{2,1,0:T(8,128)(2,1)S(1)} %get-tuple-element.42.refs_0_), channel_id=1, source_target_pairs={{0,16},{16,0},{32,48},{48,32},{64,80},{80,64},{96,112},{112,96},{1... | collective-permute-start | bytes 3145736 | tf_op jit(solution)/shard_map/ppermute | solution.py:596
  37.6 2.7 %picks.1 = f32[8,1024]{1,0:T(8,128)S(1)} custom-call(s32[8,128]{1,0:T(8,128)S(1)} %copy-done.4, f32[512,8,128]{2,1,0:T(8,128)S(1)} %get-tuple-element.40.f_ref.refs_6_, f32[8,128]{1,0:T(8,128)S(1)} %copy-done.5), custom_call_target="tpu_custom_call" | custom-call | tf_op jit(solution)/shard_map/picks/pallas_call | solution.py:400
  40.3 1.4 %collective-permute-start.4 = (f32[8,2176]{1,0:T(8,128)S(1)}, f32[8,2176]{1,0:T(8,128)S(1)}, u32[]{:S(2)}, u32[]{:S(2)}) collective-permute-start(f32[8,2176]{1,0:T(8,128)S(1)} %pad_maximum_fusion), channel_id=1, source_target_pairs={{0,1},{1,0},{2,3},{3,2},{4,5},{5,4},{6,7},{7,6},{8,9},{9,8},{10,11... | collective-permute-start | bytes 208904 | tf_op jit(solution)/shard_map/ppermute | solution.py:613
  41.7 1.2 %collective-permute-start.10 = (bf16[256,8,256]{2,1,0:T(8,128)(2,1)S(1)}, bf16[256,8,256]{2,1,0:T(8,128)(2,1)S(1)}, u32[]{:S(2)}, u32[]{:S(2)}) collective-permute-start(bf16[256,8,256]{2,1,0:T(8,128)(2,1)S(1)} %get-tuple-element.42.refs_0_), channel_id=1, source_target_pairs={{0,96},{16,48},{32,0},{48,80},{64,32},{80,112},{96,64},{112,16},{1... | collective-permute-start | bytes 3145736 | tf_op jit(solution)/shard_map/ppermute | solution.py:596
  42.9 1.5 %collective-permute-start.9 = (bf16[256,8,256]{2,1,0:T(8,128)(2,1)S(1)}, bf16[256,8,256]{2,1,0:T(8,128)(2,1)S(1)}, u32[]{:S(2)}, u32[]{:S(2)}) collective-permute-start(bf16[256,8,256]{2,1,0:T(8,128)(2,1)S(1)} %get-tuple-element.42.refs_0_), channel_id=1, source_target_pairs={{0,32},{16,112},{32,64},{48,16},{64,96},{80,48},{96,0},{112,80},{1... | collective-permute-start | bytes 3145736 | tf_op jit(solution)/shard_map/ppermute | solution.py:596
  44.4 0.0 collective-permute-done.5.refs_3_
  44.4 2.6 %collective-permute-start.6 = (f32[8,2176]{1,0:T(8,128)S(1)}, f32[8,2176]{1,0:T(8,128)S(1)}, u32[]{:S(2)}, u32[]{:S(2)}) collective-permute-start(f32[8,2176]{1,0:T(8,128)S(1)} %fusion), channel_id=1, source_target_pairs={{0,2},{1,3},{2,0},{3,1},{4,6},{5,7},{6,4},{7,5},{8,10},{9,11},{10,... | collective-permute-start | bytes 208904 | tf_op jit(solution)/shard_map/ppermute | solution.py:613
  46.9 2.2 %collective-permute-done.6 = f32[8,2176]{1,0:T(8,128)S(1)} collective-permute-done((f32[8,2176]{1,0:T(8,128)S(1)}, f32[8,2176]{1,0:T(8,128)S(1)}, u32[]{:S(2)}, u32[]{:S(2)}) %collective-permute-start.6) | collective-permute-done | bytes 69664 | tf_op jit(solution)/shard_map/ppermute | solution.py:613
  49.1 0.1 collective-permute-start.7
  49.2 3.4 %collective-permute-done.7 = f32[8,2176]{1,0:T(8,128)S(1)} collective-permute-done((f32[8,2176]{1,0:T(8,128)S(1)}, f32[8,2176]{1,0:T(8,128)S(1)}, u32[]{:S(2)}, u32[]{:S(2)}) %collective-permute-start.7) | collective-permute-done | bytes 69664 | tf_op jit(solution)/shard_map/ppermute | solution.py:613
  52.7 1.6 %collective-permute-start.8 = (f32[8,2176]{1,0:T(8,128)S(1)}, f32[8,2176]{1,0:T(8,128)S(1)}, u32[]{:S(2)}, u32[]{:S(2)}) collective-permute-start(f32[8,2176]{1,0:T(8,128)S(1)} %add.46), channel_id=1, source_target_pairs={{0,8},{4,12},{8,0},{12,4},{1,9},{5,13},{9,1},{13,5},{2,10},{6,14},... | collective-permute-start | bytes 208904 | tf_op jit(solution)/shard_map/ppermute | solution.py:613
  54.3 3.1 %collective-permute-done.8 = f32[8,2176]{1,0:T(8,128)S(1)} collective-permute-done((f32[8,2176]{1,0:T(8,128)S(1)}, f32[8,2176]{1,0:T(8,128)S(1)}, u32[]{:S(2)}, u32[]{:S(2)}) %collective-permute-start.8) | collective-permute-done | bytes 69664 | tf_op jit(solution)/shard_map/ppermute | solution.py:613
  57.5 7.1 %collective-permute-done.10.refs_2_ = bf16[256,8,256]{2,1,0:T(8,128)(2,1)S(1)} collective-permute-done((bf16[256,8,256]{2,1,0:T(8,128)(2,1)S(1)}, bf16[256,8,256]{2,1,0:T(8,128)(2,1)S(1)}, u32[]{:S(2)}, u32[]{:S(2)}) %collective-permute-start.10) | collective-permute-done | bytes 1048608 | tf_op jit(solution)/shard_map/ppermute | solution.py:596
  64.5 3.1 %collective-permute-done.9.refs_1_ = bf16[256,8,256]{2,1,0:T(8,128)(2,1)S(1)} collective-permute-done((bf16[256,8,256]{2,1,0:T(8,128)(2,1)S(1)}, bf16[256,8,256]{2,1,0:T(8,128)(2,1)S(1)}, u32[]{:S(2)}, u32[]{:S(2)}) %collective-permute-start.9) | collective-permute-done | bytes 1048608 | tf_op jit(solution)/shard_map/ppermute | solution.py:596
  67.6 2.5 %collective-permute-start.11 = (f32[8,1024]{1,0:T(8,128)S(1)}, f32[8,1024]{1,0:T(8,128)S(1)}, u32[]{:S(2)}, u32[]{:S(2)}) collective-permute-start(f32[8,1024]{1,0:T(8,128)S(1)} %get-tuple-element.44), channel_id=1, source_target_pairs={{0,32},{16,112},{32,64},{48,16},{64,96},{80,48},{96,0},{112,80},{1... | collective-permute-start | bytes 98312 | tf_op jit(solution)/shard_map/ppermute | solution.py:596
  70.2 1.5 %collective-permute-start.13 = (f32[8,1024]{1,0:T(8,128)S(1)}, f32[8,1024]{1,0:T(8,128)S(1)}, u32[]{:S(2)}, u32[]{:S(2)}) collective-permute-start(f32[8,1024]{1,0:T(8,128)S(1)} %get-tuple-element.44), channel_id=1, source_target_pairs={{0,64},{16,80},{32,96},{48,112},{64,0},{80,16},{96,32},{112,48},{1... | collective-permute-start | bytes 98312 | tf_op jit(solution)/shard_map/ppermute | solution.py:596
  71.7 2.5 %collective-permute-done.12 = f32[8,1024]{1,0:T(8,128)S(1)} collective-permute-done((f32[8,1024]{1,0:T(8,128)S(1)}, f32[8,1024]{1,0:T(8,128)S(1)}, u32[]{:S(2)}, u32[]{:S(2)}) %collective-permute-start.12) | collective-permute-done | bytes 32800 | tf_op jit(solution)/shard_map/ppermute | solution.py:596
  74.2 0.3 collective-permute-done.13
  74.5 2.6 %collective-permute-start.14 = (f32[32,1024]{1,0:T(8,128)S(1)}, f32[32,1024]{1,0:T(8,128)S(1)}, u32[]{:S(2)}, u32[]{:S(2)}) collective-permute-start(f32[32,1024]{1,0:T(8,128)S(1)} %constant_dynamic-update-slice_fusion.near_ref), channel_id=1, source_target_pairs={{0,16},{16,0},{32,48},{48,32},{64,80},{80,64},{96,112},{112,96},{1... | collective-permute-start | bytes 393224 | tf_op jit(solution)/shard_map/ppermute | solution.py:596
  77.1 1.0 collective-permute-done.14.far_ref
  78.1 0.4 collective-permute-start.19
  78.5 0.1 collective-permute-start.20
  78.7 1.5 %collective-permute-start.15 = (bf16[128,8,256]{2,1,0:T(8,128)(2,1)S(1)}, bf16[128,8,256]{2,1,0:T(8,128)(2,1)S(1)}, u32[]{:S(2)}, u32[]{:S(2)}) collective-permute-start(bf16[128,8,256]{2,1,0:T(8,128)(2,1)S(1)} %slice.18), channel_id=1, source_target_pairs={{0,32},{16,112},{32,64},{48,16},{64,96},{80,48},{96,0},{112,80},{1... | collective-permute-start | bytes 1572872 | tf_op jit(solution)/shard_map/ppermute | solution.py:596
  80.2 0.1 collective-permute-start.16
  80.3 11.4 %collective-permute-done.15.refs_0_ = bf16[128,8,256]{2,1,0:T(8,128)(2,1)S(1)} collective-permute-done((bf16[128,8,256]{2,1,0:T(8,128)(2,1)S(1)}, bf16[128,8,256]{2,1,0:T(8,128)(2,1)S(1)}, u32[]{:S(2)}, u32[]{:S(2)}) %collective-permute-start.15) | collective-permute-done | bytes 524320 | tf_op jit(solution)/shard_map/ppermute | solution.py:596
  91.7 2.6 %collective-permute-start.17 = (bf16[128,8,256]{2,1,0:T(8,128)(2,1)S(1)}, bf16[128,8,256]{2,1,0:T(8,128)(2,1)S(1)}, u32[]{:S(2)}, u32[]{:S(2)}) collective-permute-start(bf16[128,8,256]{2,1,0:T(8,128)(2,1)S(1)} %collective-permute-done.15.refs_0_), channel_id=1, source_target_pairs={{0,16},{16,0},{32,48},{48,32},{64,80},{80,64},{96,112},{112,96},{1... | collective-permute-start | bytes 1572872 | tf_op jit(solution)/shard_map/ppermute | solution.py:596
  94.3 0.1 collective-permute-done.16.refs_1_
  94.4 2.6 %weights.1 = (f32[8,48]{1,0:T(8,128)S(1)}, f32[8,16]{1,0:T(8,128)S(1)}) custom-call(f32[32,1024]{1,0:T(8,128)S(1)} %constant_dynamic-update-slice_fusion.near_ref, f32[32,1024]{1,0:T(8,128)S(1)} %collective-permute-done.14.far_ref, f32[8,1024]{1,0:T(8,128)S(1)} %get-tuple-element.53.target_ref, f32[8,128]{1,0:T(8,128)S(1)} %slice.22.error_ref), custom_call_target="tpu_custom_call" | custom-call | tf_op jit(solution)/shard_map/weights/pallas_call | solution.py:476
  97.0 0.0 collective-permute-done.20.refs_5_
  97.1 3.0 %begin.1.refs_4_ = f32[512,8,128]{2,1,0:T(8,128)S(1)} custom-call(f32[8,48]{1,0:T(8,128)S(1)} %get-tuple-element.49.w_ref, bf16[256,8,256]{2,1,0:T(8,128)(2,1)S(1)} %get-tuple-element.42.refs_0_, bf16[256,8,256]{2,1,0:T(8,128)(2,1)S(1)} %collective-permute-done.9.refs_1_, bf16[256,8,256]{2,1,0:T(8,128)(2,1)S(1)} %collective-permute-done.10.refs_2_, ...), custom_call_target="tpu_custom_call" | custom-call | tf_op jit(solution)/shard_map/begin/pallas_call | solution.py:541
  100.1 0.0 collective-permute-done.17.refs_2_
  100.1 0.0 collective-permute-done.18.refs_3_
  100.1 2.5 %update.1 = f32[8,256,256]{2,1,0:T(8,128)} custom-call(f32[8,16]{1,0:T(8,128)S(1)} %get-tuple-element.48.w_ref, bf16[128,8,256]{2,1,0:T(8,128)(2,1)S(1)} %collective-permute-done.15.refs_0_, bf16[128,8,256]{2,1,0:T(8,128)(2,1)S(1)} %collective-permute-done.16.refs_1_, bf16[128,8,256]{2,1,0:T(8,128)(2,1)S(1)} %collective-permute-done.17.refs_2_, ...), custom_call_target="tpu_custom_call" | custom-call | tf_op jit(solution)/shard_map/update/pallas_call | solution.py:556
  (38 shorter events, 0.2 us)
Async XLA Ops:
  0.0 7.6 %copy-start = (f32[256,256]{1,0:T(8,128)S(1)}, f32[256,256]{1,0:T(8,128)}, u32[]{:S(2)}) copy-start(f32[256,256]{1,0:T(8,128)} %e_ref.5) | copy-start | bytes 786436
  0.0 7.6 %copy-start.1 = (f32[256,256]{1,0:T(8,128)S(1)}, f32[256,256]{1,0:T(8,128)}, u32[]{:S(2)}) copy-start(f32[256,256]{1,0:T(8,128)} %k_ref.5) | copy-start | bytes 786436
  2.8 9.1 %collective-permute-start = (f32[9,8,256]{2,1,0:T(8,128)}, f32[9,8,256]{2,1,0:T(8,128)S(1)}, u32[]{:S(2)}, u32[]{:S(2)}) collective-permute-start(f32[9,8,256]{2,1,0:T(8,128)} %get-tuple-element.32.bottom_ref), channel_id=1, source_target_pairs={{0,4},{4,8},{8,12},{12,0},{1,5},{5,9},{9,13},{13,1},{2,6},{6,10},{... | collective-permute-start | bytes 221192 | tf_op jit(solution)/shard_map/ppermute | solution.py:583
  5.3 6.6 %copy-start.2 = (f32[9,8,256]{2,1,0:T(8,128)S(1)}, f32[9,8,256]{2,1,0:T(8,128)}, u32[]{:S(2)}) copy-start(f32[9,8,256]{2,1,0:T(8,128)} %get-tuple-element.33.top_ref) | copy-start | bytes 221188
  5.3 6.6 %copy-start.3 = (f32[9,8,256]{2,1,0:T(8,128)S(1)}, f32[9,8,256]{2,1,0:T(8,128)}, u32[]{:S(2)}) copy-start(f32[9,8,256]{2,1,0:T(8,128)} %get-tuple-element.32.bottom_ref) | copy-start | bytes 221188
  5.3 9.6 %copy-start.6 = (f32[64,8]{0,1:T(8,128)S(1)}, f32[64,8]{0,1:T(8,128)}, u32[]{:S(2)}) copy-start(f32[64,8]{0,1:T(8,128)} %param.15) | copy-start | bytes 6148
  5.3 9.6 %copy-start.7 = (f32[64]{0:T(128)S(1)}, f32[64]{0:T(128)}, u32[]{:S(2)}) copy-start(f32[64]{0:T(128)} %param.14) | copy-start | bytes 772
  5.3 9.6 %copy-start.8 = (f32[64]{0:T(128)S(1)}, f32[64]{0:T(128)}, u32[]{:S(2)}) copy-start(f32[64]{0:T(128)} %param.13) | copy-start | bytes 772
  5.3 6.5 %collective-permute-start.1 = (f32[9,8,256]{2,1,0:T(8,128)}, f32[9,8,256]{2,1,0:T(8,128)S(1)}, u32[]{:S(2)}, u32[]{:S(2)}) collective-permute-start(f32[9,8,256]{2,1,0:T(8,128)} %get-tuple-element.33.top_ref), channel_id=1, source_target_pairs={{0,12},{4,0},{8,4},{12,8},{1,13},{5,1},{9,5},{13,9},{2,14},{6,2},{... | collective-permute-start | bytes 221192 | tf_op jit(solution)/shard_map/ppermute | solution.py:584
  12.0 4.9 %collective-permute-start.2 = (f32[9,3,8,128]{3,2,1,0:T(8,128)S(1)}, f32[9,3,8,128]{3,2,1,0:T(8,128)S(1)}, u32[]{:S(2)}, u32[]{:S(2)}) collective-permute-start(f32[9,3,8,128]{3,2,1,0:T(8,128)S(1)} %get-tuple-element.38), channel_id=1, source_target_pairs={{0,1},{1,2},{2,3},{3,0},{4,5},{5,6},{6,7},{7,4},{8,9},{9,10},{10,1... | collective-permute-start | bytes 331784 | tf_op jit(solution)/shard_map/ppermute | solution.py:587
  13.4 3.6 %collective-permute-start.3 = (f32[9,3,8,128]{3,2,1,0:T(8,128)S(1)}, f32[9,3,8,128]{3,2,1,0:T(8,128)S(1)}, u32[]{:S(2)}, u32[]{:S(2)}) collective-permute-start(f32[9,3,8,128]{3,2,1,0:T(8,128)S(1)} %get-tuple-element.39), channel_id=1, source_target_pairs={{0,3},{1,0},{2,1},{3,2},{4,7},{5,4},{6,5},{7,6},{8,11},{9,8},{10,9... | collective-permute-start | bytes 331784 | tf_op jit(solution)/shard_map/ppermute | solution.py:588
  17.0 20.6 %copy-start.4 = (s32[8,128]{1,0:T(8,128)S(1)}, s32[8,128]{1,0:T(8,128)}, u32[]{:S(2)}) copy-start(s32[8,128]{1,0:T(8,128)} %get-tuple-element.29.code_ref) | copy-start | bytes 12292
  17.0 20.6 %copy-start.5 = (f32[8,128]{1,0:T(8,128)S(1)}, f32[8,128]{1,0:T(8,128)}, u32[]{:S(2)}) copy-start(f32[8,128]{1,0:T(8,128)} %get-tuple-element.41.inside_ref) | copy-start | bytes 12292
  35.1 9.3 %collective-permute-start.5 = (bf16[256,8,256]{2,1,0:T(8,128)(2,1)S(1)}, bf16[256,8,256]{2,1,0:T(8,128)(2,1)S(1)}, u32[]{:S(2)}, u32[]{:S(2)}) collective-permute-start(bf16[256,8,256]{2,1,0:T(8,128)(2,1)S(1)} %get-tuple-element.42.refs_0_), channel_id=1, source_target_pairs={{0,16},{16,0},{32,48},{48,32},{64,80},{80,64},{96,112},{112,96},{1... | collective-permute-start | bytes 3145736 | tf_op jit(solution)/shard_map/ppermute | solution.py:596
  40.3 4.1 %collective-permute-start.4 = (f32[8,2176]{1,0:T(8,128)S(1)}, f32[8,2176]{1,0:T(8,128)S(1)}, u32[]{:S(2)}, u32[]{:S(2)}) collective-permute-start(f32[8,2176]{1,0:T(8,128)S(1)} %pad_maximum_fusion), channel_id=1, source_target_pairs={{0,1},{1,0},{2,3},{3,2},{4,5},{5,4},{6,7},{7,6},{8,9},{9,8},{10,11... | collective-permute-start | bytes 208904 | tf_op jit(solution)/shard_map/ppermute | solution.py:613
  41.7 22.9 %collective-permute-start.10 = (bf16[256,8,256]{2,1,0:T(8,128)(2,1)S(1)}, bf16[256,8,256]{2,1,0:T(8,128)(2,1)S(1)}, u32[]{:S(2)}, u32[]{:S(2)}) collective-permute-start(bf16[256,8,256]{2,1,0:T(8,128)(2,1)S(1)} %get-tuple-element.42.refs_0_), channel_id=1, source_target_pairs={{0,96},{16,48},{32,0},{48,80},{64,32},{80,112},{96,64},{112,16},{1... | collective-permute-start | bytes 3145736 | tf_op jit(solution)/shard_map/ppermute | solution.py:596
  42.9 24.7 %collective-permute-start.9 = (bf16[256,8,256]{2,1,0:T(8,128)(2,1)S(1)}, bf16[256,8,256]{2,1,0:T(8,128)(2,1)S(1)}, u32[]{:S(2)}, u32[]{:S(2)}) collective-permute-start(bf16[256,8,256]{2,1,0:T(8,128)(2,1)S(1)} %get-tuple-element.42.refs_0_), channel_id=1, source_target_pairs={{0,32},{16,112},{32,64},{48,16},{64,96},{80,48},{96,0},{112,80},{1... | collective-permute-start | bytes 3145736 | tf_op jit(solution)/shard_map/ppermute | solution.py:596
  44.4 4.7 %collective-permute-start.6 = (f32[8,2176]{1,0:T(8,128)S(1)}, f32[8,2176]{1,0:T(8,128)S(1)}, u32[]{:S(2)}, u32[]{:S(2)}) collective-permute-start(f32[8,2176]{1,0:T(8,128)S(1)} %fusion), channel_id=1, source_target_pairs={{0,2},{1,3},{2,0},{3,1},{4,6},{5,7},{6,4},{7,5},{8,10},{9,11},{10,... | collective-permute-start | bytes 208904 | tf_op jit(solution)/shard_map/ppermute | solution.py:613
  49.1 3.5 %collective-permute-start.7 = (f32[8,2176]{1,0:T(8,128)S(1)}, f32[8,2176]{1,0:T(8,128)S(1)}, u32[]{:S(2)}, u32[]{:S(2)}) collective-permute-start(f32[8,2176]{1,0:T(8,128)S(1)} %add.45), channel_id=1, source_target_pairs={{0,4},{4,0},{8,12},{12,8},{1,5},{5,1},{9,13},{13,9},{2,6},{6,2},{1... | collective-permute-start | bytes 208904 | tf_op jit(solution)/shard_map/ppermute | solution.py:613
  52.7 4.7 %collective-permute-start.8 = (f32[8,2176]{1,0:T(8,128)S(1)}, f32[8,2176]{1,0:T(8,128)S(1)}, u32[]{:S(2)}, u32[]{:S(2)}) collective-permute-start(f32[8,2176]{1,0:T(8,128)S(1)} %add.46), channel_id=1, source_target_pairs={{0,8},{4,12},{8,0},{12,4},{1,9},{5,13},{9,1},{13,5},{2,10},{6,14},... | collective-permute-start | bytes 208904 | tf_op jit(solution)/shard_map/ppermute | solution.py:613
  67.6 4.1 %collective-permute-start.11 = (f32[8,1024]{1,0:T(8,128)S(1)}, f32[8,1024]{1,0:T(8,128)S(1)}, u32[]{:S(2)}, u32[]{:S(2)}) collective-permute-start(f32[8,1024]{1,0:T(8,128)S(1)} %get-tuple-element.44), channel_id=1, source_target_pairs={{0,32},{16,112},{32,64},{48,16},{64,96},{80,48},{96,0},{112,80},{1... | collective-permute-start | bytes 98312 | tf_op jit(solution)/shard_map/ppermute | solution.py:596
  70.2 4.0 %collective-permute-start.12 = (f32[8,1024]{1,0:T(8,128)S(1)}, f32[8,1024]{1,0:T(8,128)S(1)}, u32[]{:S(2)}, u32[]{:S(2)}) collective-permute-start(f32[8,1024]{1,0:T(8,128)S(1)} %get-tuple-element.44), channel_id=1, source_target_pairs={{0,96},{16,48},{32,0},{48,80},{64,32},{80,112},{96,64},{112,16},{1... | collective-permute-start | bytes 98312 | tf_op jit(solution)/shard_map/ppermute | solution.py:596
  70.2 4.3 %collective-permute-start.13 = (f32[8,1024]{1,0:T(8,128)S(1)}, f32[8,1024]{1,0:T(8,128)S(1)}, u32[]{:S(2)}, u32[]{:S(2)}) collective-permute-start(f32[8,1024]{1,0:T(8,128)S(1)} %get-tuple-element.44), channel_id=1, source_target_pairs={{0,64},{16,80},{32,96},{48,112},{64,0},{80,16},{96,32},{112,48},{1... | collective-permute-start | bytes 98312 | tf_op jit(solution)/shard_map/ppermute | solution.py:596
  74.5 3.6 %collective-permute-start.14 = (f32[32,1024]{1,0:T(8,128)S(1)}, f32[32,1024]{1,0:T(8,128)S(1)}, u32[]{:S(2)}, u32[]{:S(2)}) collective-permute-start(f32[32,1024]{1,0:T(8,128)S(1)} %constant_dynamic-update-slice_fusion.near_ref), channel_id=1, source_target_pairs={{0,16},{16,0},{32,48},{48,32},{64,80},{80,64},{96,112},{112,96},{1... | collective-permute-start | bytes 393224 | tf_op jit(solution)/shard_map/ppermute | solution.py:596
  78.1 18.9 %collective-permute-start.19 = (bf16[256,8,256]{2,1,0:T(8,128)(2,1)S(1)}, bf16[256,8,256]{2,1,0:T(8,128)(2,1)S(1)}, u32[]{:S(2)}, u32[]{:S(2)}) collective-permute-start(bf16[256,8,256]{2,1,0:T(8,128)(2,1)S(1)} %collective-permute-done.9.refs_1_), channel_id=1, source_target_pairs={{0,16},{16,0},{32,48},{48,32},{64,80},{80,64},{96,112},{112,96},{1... | collective-permute-start | bytes 3145736 | tf_op jit(solution)/shard_map/ppermute | solution.py:596
  78.5 18.6 %collective-permute-start.20 = (bf16[256,8,256]{2,1,0:T(8,128)(2,1)S(1)}, bf16[256,8,256]{2,1,0:T(8,128)(2,1)S(1)}, u32[]{:S(2)}, u32[]{:S(2)}) collective-permute-start(bf16[256,8,256]{2,1,0:T(8,128)(2,1)S(1)} %collective-permute-done.10.refs_2_), channel_id=1, source_target_pairs={{0,16},{16,0},{32,48},{48,32},{64,80},{80,64},{96,112},{112,96},{1... | collective-permute-start | bytes 3145736 | tf_op jit(solution)/shard_map/ppermute | solution.py:596
  78.7 13.1 %collective-permute-start.15 = (bf16[128,8,256]{2,1,0:T(8,128)(2,1)S(1)}, bf16[128,8,256]{2,1,0:T(8,128)(2,1)S(1)}, u32[]{:S(2)}, u32[]{:S(2)}) collective-permute-start(bf16[128,8,256]{2,1,0:T(8,128)(2,1)S(1)} %slice.18), channel_id=1, source_target_pairs={{0,32},{16,112},{32,64},{48,16},{64,96},{80,48},{96,0},{112,80},{1... | collective-permute-start | bytes 1572872 | tf_op jit(solution)/shard_map/ppermute | solution.py:596
  80.2 14.2 %collective-permute-start.16 = (bf16[128,8,256]{2,1,0:T(8,128)(2,1)S(1)}, bf16[128,8,256]{2,1,0:T(8,128)(2,1)S(1)}, u32[]{:S(2)}, u32[]{:S(2)}) collective-permute-start(bf16[128,8,256]{2,1,0:T(8,128)(2,1)S(1)} %slice.19), channel_id=1, source_target_pairs={{0,96},{16,48},{32,0},{48,80},{64,32},{80,112},{96,64},{112,16},{1... | collective-permute-start | bytes 1572872 | tf_op jit(solution)/shard_map/ppermute | solution.py:596
  91.7 8.3 %collective-permute-start.17 = (bf16[128,8,256]{2,1,0:T(8,128)(2,1)S(1)}, bf16[128,8,256]{2,1,0:T(8,128)(2,1)S(1)}, u32[]{:S(2)}, u32[]{:S(2)}) collective-permute-start(bf16[128,8,256]{2,1,0:T(8,128)(2,1)S(1)} %collective-permute-done.15.refs_0_), channel_id=1, source_target_pairs={{0,16},{16,0},{32,48},{48,32},{64,80},{80,64},{96,112},{112,96},{1... | collective-permute-start | bytes 1572872 | tf_op jit(solution)/shard_map/ppermute | solution.py:596
  94.4 5.7 %collective-permute-start.18 = (bf16[128,8,256]{2,1,0:T(8,128)(2,1)S(1)}, bf16[128,8,256]{2,1,0:T(8,128)(2,1)S(1)}, u32[]{:S(2)}, u32[]{:S(2)}) collective-permute-start(bf16[128,8,256]{2,1,0:T(8,128)(2,1)S(1)} %collective-permute-done.16.refs_1_), channel_id=1, source_target_pairs={{0,16},{16,0},{32,48},{48,32},{64,80},{80,64},{96,112},{112,96},{1... | collective-permute-start | bytes 1572872 | tf_op jit(solution)/shard_map/ppermute | solution.py:596

commit v5 on v4

--- a/solution.py
+++ b/solution.py
@@ -608,12 +608,12 @@
     a, b = send(rounded, 1), send(rounded, -1)
     own_far = send(rounded, 0, True)
     for axis, n in (("ty", n_y), ("tx", n_x)):
-        bit = 1
-        while bit < n:
-            line = line + lax.ppermute(line, axis, [(i, i ^ bit) for i in range(n)])
-            if bit == 1 and axis == "ty":
+        span = 2
+        while span <= n:
+            line = line + lax.ppermute(line, axis, [(i, i ^ (span - 1)) for i in range(n)])
+            if span == 2 and axis == "ty":
                 line, own_far = lax.optimization_barrier((line, own_far))
-            bit *= 2
+            span *= 2
     observed, target, error = (
         line[:, 0:n_obs], line[:, n_obs : 2 * n_obs], line[:, 2 * n_obs :]
     )

time: 103 us -> 103 us (level)
  no operation moved by 1% of the time
where the time goes in v5:
time: 103 us
  Pallas kernels  36 us (35%)
  waiting for transfers between devices  35.7 us (35%)
  starting transfers between devices  29.8 us (29%)
    ppermute x13, waiting for transfers between devices, send(): lax.ppermute(v, 'mem', [(i, i ^ 1) for i in range(n_m)] if swap else to)  25.7 us
    pallas_call x1, Pallas kernels, run_steps(): pl.pallas_call(steps_kernel, in_specs=[HBM_SPEC] * 2 + [VMEM_SPEC] * 6, o...  18.1 us
    ppermute x13, starting transfers between devices, send(): lax.ppermute(v, 'mem', [(i, i ^ 1) for i in range(n_m)] if swap else to)  16.6 us
    ppermute x4, waiting for transfers between devices, local(): lax.ppermute(line, axis, [(i, i ^ span - 1) for i in range(n)])  8.46 us
    ppermute x4, starting transfers between devices, local(): lax.ppermute(line, axis, [(i, i ^ span - 1) for i in range(n)])  5.64 us
    pallas_call x1, Pallas kernels, turn(): pl.pallas_call(turn_kernel, in_specs=[HBM_SPEC] * 2 + [VMEM_SPEC] * 2, ou...  4.27 us
    pallas_call x1, Pallas kernels, begin(): pl.pallas_call(begin_kernel, in_specs=[VMEM_SPEC] * (len(pieces) + 2), ou...  2.96 us
    pallas_call x1, Pallas kernels, ends(): pl.pallas_call(ends_kernel, in_specs=[VMEM_SPEC] + [HBM_SPEC] * 2 + [VMEM...  2.76 us
  transfers between devices with their start and end apart: 21, of which 11 were waited for; matrix products, arithmetic and copies ran while one was open for 1% of the time, Pallas kernels for 12%

profile of v5, /device:TPU:1, one launch (start us, length us, event | category | flops | bytes accessed | tf_op | source)
XLA Modules:
  0.0 102.6 jit_solution(11669249976210418611)
XLA Ops:
  0.0 2.8 %ends.1 = (f32[9,8,256]{2,1,0:T(8,128)}, f32[9,8,256]{2,1,0:T(8,128)}, s32[8,128]{1,0:T(8,128)}, f32[8,128]{1,0:T(8,128)}) custom-call(s32[8,128]{1,0:T(8,128)} %bitcast.4, f32[8,256,256]{2,1,0:T(8,128)} %p_in.1, f32[8,256,256]{2,1,0:T(8,128)} %w_in.1, f32[256,256]{1,0:T(8,128)} %e_ref.5, f32[256,256]{1,0:T(8,128)} %k_ref.5), custom_call_target="tpu_custom_call" | custom-call | tf_op jit(solution)/shard_map/ends/pallas_call | solution.py:75
  2.8 2.5 %collective-permute-start = (f32[9,8,256]{2,1,0:T(8,128)}, f32[9,8,256]{2,1,0:T(8,128)S(1)}, u32[]{:S(2)}, u32[]{:S(2)}) collective-permute-start(f32[9,8,256]{2,1,0:T(8,128)} %get-tuple-element.32.bottom_ref), channel_id=1, source_target_pairs={{0,4},{4,8},{8,12},{12,0},{1,5},{5,9},{9,13},{13,1},{2,6},{6,10},{... | collective-permute-start | bytes 221192 | tf_op jit(solution)/shard_map/ppermute | solution.py:583
  5.3 0.0 copy-start.8
  5.3 2.2 %collective-permute-start.1 = (f32[9,8,256]{2,1,0:T(8,128)}, f32[9,8,256]{2,1,0:T(8,128)S(1)}, u32[]{:S(2)}, u32[]{:S(2)}) collective-permute-start(f32[9,8,256]{2,1,0:T(8,128)} %get-tuple-element.33.top_ref), channel_id=1, source_target_pairs={{0,12},{4,0},{8,4},{12,8},{1,13},{5,1},{9,5},{13,9},{2,14},{6,2},{... | collective-permute-start | bytes 221192 | tf_op jit(solution)/shard_map/ppermute | solution.py:584
  7.6 4.3 %turn.1 = (f32[256,8,256]{2,1,0:T(8,128)}, f32[256,8,256]{2,1,0:T(8,128)}, f32[8,3,8,128]{3,2,1,0:T(8,128)S(1)}, f32[8,3,8,128]{3,2,1,0:T(8,128)S(1)}) custom-call(f32[8,256,256]{2,1,0:T(8,128)} %p_in.1, f32[8,256,256]{2,1,0:T(8,128)} %w_in.1, f32[256,256]{1,0:T(8,128)S(1)} %copy-done, f32[256,256]{1,0:T(8,128)S(1)} %copy-done.1), custom_call_target="tpu_custom_call" | custom-call | flops 10000000 | bytes 9437184 | tf_op jit(solution)/shard_map/turn/pallas_call | solution.py:157
  11.8 0.0 collective-permute-done.up_ref
  11.8 0.0 collective-permute-done.1.down_ref
  11.9 0.1 rows.1
  12.0 1.4 %collective-permute-start.2 = (f32[9,3,8,128]{3,2,1,0:T(8,128)S(1)}, f32[9,3,8,128]{3,2,1,0:T(8,128)S(1)}, u32[]{:S(2)}, u32[]{:S(2)}) collective-permute-start(f32[9,3,8,128]{3,2,1,0:T(8,128)S(1)} %get-tuple-element.38), channel_id=1, source_target_pairs={{0,1},{1,2},{2,3},{3,0},{4,5},{5,6},{6,7},{7,4},{8,9},{9,10},{10,1... | collective-permute-start | bytes 331784 | tf_op jit(solution)/shard_map/ppermute | solution.py:587
  13.4 1.5 %collective-permute-start.3 = (f32[9,3,8,128]{3,2,1,0:T(8,128)S(1)}, f32[9,3,8,128]{3,2,1,0:T(8,128)S(1)}, u32[]{:S(2)}, u32[]{:S(2)}) collective-permute-start(f32[9,3,8,128]{3,2,1,0:T(8,128)S(1)} %get-tuple-element.39), channel_id=1, source_target_pairs={{0,3},{1,0},{2,1},{3,2},{4,7},{5,4},{6,5},{7,6},{8,11},{9,8},{10,9... | collective-permute-start | bytes 331784 | tf_op jit(solution)/shard_map/ppermute | solution.py:588
  14.9 0.3 dynamic_update_slice.6
  15.2 0.2 dynamic_update_slice.7
  15.4 1.5 %collective-permute-done.2.fl_ref = f32[9,3,8,128]{3,2,1,0:T(8,128)S(1)} collective-permute-done((f32[9,3,8,128]{3,2,1,0:T(8,128)S(1)}, f32[9,3,8,128]{3,2,1,0:T(8,128)S(1)}, u32[]{:S(2)}, u32[]{:S(2)}) %collective-permute-start.2) | collective-permute-done | bytes 110624 | tf_op jit(solution)/shard_map/ppermute | solution.py:587
  16.9 0.0 collective-permute-done.3.fr_ref
  17.0 18.1 %steps.1 = (f32[512,8,128]{2,1,0:T(8,128)S(1)}, bf16[256,8,256]{2,1,0:T(8,128)(2,1)S(1)}) custom-call(f32[256,8,256]{2,1,0:T(8,128)} %get-tuple-element.30.pt_in, f32[256,8,256]{2,1,0:T(8,128)} %get-tuple-element.31.wt_in, f32[256,256]{1,0:T(8,128)S(1)} %copy-done, f32[256,256]{1,0:T(8,128)S(1)} %copy-done.1, f32[9,8,256]{2,1,0:T(8,128)S(1)} %get-tuple-element.36.above_ref, ...), custom_call_target="tpu_custom_call" | custom-call | tf_op jit(solution)/shard_map/steps/pallas_call | solution.py:369
  35.1 2.5 %collective-permute-start.5 = (bf16[256,8,256]{2,1,0:T(8,128)(2,1)S(1)}, bf16[256,8,256]{2,1,0:T(8,128)(2,1)S(1)}, u32[]{:S(2)}, u32[]{:S(2)}) collective-permute-start(bf16[256,8,256]{2,1,0:T(8,128)(2,1)S(1)} %get-tuple-element.42.refs_0_), channel_id=1, source_target_pairs={{0,16},{16,0},{32,48},{48,32},{64,80},{80,64},{96,112},{112,96},{1... | collective-permute-start | bytes 3145736 | tf_op jit(solution)/shard_map/ppermute | solution.py:596
  37.6 2.7 %picks.1 = f32[8,1024]{1,0:T(8,128)S(1)} custom-call(s32[8,128]{1,0:T(8,128)S(1)} %copy-done.4, f32[512,8,128]{2,1,0:T(8,128)S(1)} %get-tuple-element.40.f_ref.refs_6_, f32[8,128]{1,0:T(8,128)S(1)} %copy-done.5), custom_call_target="tpu_custom_call" | custom-call | tf_op jit(solution)/shard_map/picks/pallas_call | solution.py:400
  40.3 1.4 %collective-permute-start.4 = (f32[8,2176]{1,0:T(8,128)S(1)}, f32[8,2176]{1,0:T(8,128)S(1)}, u32[]{:S(2)}, u32[]{:S(2)}) collective-permute-start(f32[8,2176]{1,0:T(8,128)S(1)} %pad_maximum_fusion), channel_id=1, source_target_pairs={{0,1},{1,0},{2,3},{3,2},{4,5},{5,4},{6,7},{7,6},{8,9},{9,8},{10,11... | collective-permute-start | bytes 208904 | tf_op jit(solution)/shard_map/ppermute | solution.py:613
  41.7 1.2 %collective-permute-start.10 = (bf16[256,8,256]{2,1,0:T(8,128)(2,1)S(1)}, bf16[256,8,256]{2,1,0:T(8,128)(2,1)S(1)}, u32[]{:S(2)}, u32[]{:S(2)}) collective-permute-start(bf16[256,8,256]{2,1,0:T(8,128)(2,1)S(1)} %get-tuple-element.42.refs_0_), channel_id=1, source_target_pairs={{0,96},{16,48},{32,0},{48,80},{64,32},{80,112},{96,64},{112,16},{1... | collective-permute-start | bytes 3145736 | tf_op jit(solution)/shard_map/ppermute | solution.py:596
  42.9 1.5 %collective-permute-start.9 = (bf16[256,8,256]{2,1,0:T(8,128)(2,1)S(1)}, bf16[256,8,256]{2,1,0:T(8,128)(2,1)S(1)}, u32[]{:S(2)}, u32[]{:S(2)}) collective-permute-start(bf16[256,8,256]{2,1,0:T(8,128)(2,1)S(1)} %get-tuple-element.42.refs_0_), channel_id=1, source_target_pairs={{0,32},{16,112},{32,64},{48,16},{64,96},{80,48},{96,0},{112,80},{1... | collective-permute-start | bytes 3145736 | tf_op jit(solution)/shard_map/ppermute | solution.py:596
  44.4 0.0 collective-permute-done.5.refs_3_
  44.4 2.4 %collective-permute-start.6 = (f32[8,2176]{1,0:T(8,128)S(1)}, f32[8,2176]{1,0:T(8,128)S(1)}, u32[]{:S(2)}, u32[]{:S(2)}) collective-permute-start(f32[8,2176]{1,0:T(8,128)S(1)} %fusion), channel_id=1, source_target_pairs={{0,3},{1,2},{2,1},{3,0},{4,7},{5,6},{6,5},{7,4},{8,11},{9,10},{10,... | collective-permute-start | bytes 208904 | tf_op jit(solution)/shard_map/ppermute | solution.py:613
  46.8 2.0 %collective-permute-done.6 = f32[8,2176]{1,0:T(8,128)S(1)} collective-permute-done((f32[8,2176]{1,0:T(8,128)S(1)}, f32[8,2176]{1,0:T(8,128)S(1)}, u32[]{:S(2)}, u32[]{:S(2)}) %collective-permute-start.6) | collective-permute-done | bytes 69664 | tf_op jit(solution)/shard_map/ppermute | solution.py:613
  48.8 0.1 collective-permute-start.7
  48.9 3.4 %collective-permute-done.7 = f32[8,2176]{1,0:T(8,128)S(1)} collective-permute-done((f32[8,2176]{1,0:T(8,128)S(1)}, f32[8,2176]{1,0:T(8,128)S(1)}, u32[]{:S(2)}, u32[]{:S(2)}) %collective-permute-start.7) | collective-permute-done | bytes 69664 | tf_op jit(solution)/shard_map/ppermute | solution.py:613
  52.4 1.8 %collective-permute-start.8 = (f32[8,2176]{1,0:T(8,128)S(1)}, f32[8,2176]{1,0:T(8,128)S(1)}, u32[]{:S(2)}, u32[]{:S(2)}) collective-permute-start(f32[8,2176]{1,0:T(8,128)S(1)} %add.46), channel_id=1, source_target_pairs={{0,12},{4,8},{8,4},{12,0},{1,13},{5,9},{9,5},{13,1},{2,14},{6,10},... | collective-permute-start | bytes 208904 | tf_op jit(solution)/shard_map/ppermute | solution.py:613
  54.2 3.0 %collective-permute-done.8 = f32[8,2176]{1,0:T(8,128)S(1)} collective-permute-done((f32[8,2176]{1,0:T(8,128)S(1)}, f32[8,2176]{1,0:T(8,128)S(1)}, u32[]{:S(2)}, u32[]{:S(2)}) %collective-permute-start.8) | collective-permute-done | bytes 69664 | tf_op jit(solution)/shard_map/ppermute | solution.py:613
  57.2 7.4 %collective-permute-done.10.refs_2_ = bf16[256,8,256]{2,1,0:T(8,128)(2,1)S(1)} collective-permute-done((bf16[256,8,256]{2,1,0:T(8,128)(2,1)S(1)}, bf16[256,8,256]{2,1,0:T(8,128)(2,1)S(1)}, u32[]{:S(2)}, u32[]{:S(2)}) %collective-permute-start.10) | collective-permute-done | bytes 1048608 | tf_op jit(solution)/shard_map/ppermute | solution.py:596
  64.5 3.1 %collective-permute-done.9.refs_1_ = bf16[256,8,256]{2,1,0:T(8,128)(2,1)S(1)} collective-permute-done((bf16[256,8,256]{2,1,0:T(8,128)(2,1)S(1)}, bf16[256,8,256]{2,1,0:T(8,128)(2,1)S(1)}, u32[]{:S(2)}, u32[]{:S(2)}) %collective-permute-start.9) | collective-permute-done | bytes 1048608 | tf_op jit(solution)/shard_map/ppermute | solution.py:596
  67.6 2.5 %collective-permute-start.11 = (f32[8,1024]{1,0:T(8,128)S(1)}, f32[8,1024]{1,0:T(8,128)S(1)}, u32[]{:S(2)}, u32[]{:S(2)}) collective-permute-start(f32[8,1024]{1,0:T(8,128)S(1)} %get-tuple-element.44), channel_id=1, source_target_pairs={{0,32},{16,112},{32,64},{48,16},{64,96},{80,48},{96,0},{112,80},{1... | collective-permute-start | bytes 98312 | tf_op jit(solution)/shard_map/ppermute | solution.py:596
  70.2 1.5 %collective-permute-start.13 = (f32[8,1024]{1,0:T(8,128)S(1)}, f32[8,1024]{1,0:T(8,128)S(1)}, u32[]{:S(2)}, u32[]{:S(2)}) collective-permute-start(f32[8,1024]{1,0:T(8,128)S(1)} %get-tuple-element.44), channel_id=1, source_target_pairs={{0,64},{16,80},{32,96},{48,112},{64,0},{80,16},{96,32},{112,48},{1... | collective-permute-start | bytes 98312 | tf_op jit(solution)/shard_map/ppermute | solution.py:596
  71.7 2.5 %collective-permute-done.12 = f32[8,1024]{1,0:T(8,128)S(1)} collective-permute-done((f32[8,1024]{1,0:T(8,128)S(1)}, f32[8,1024]{1,0:T(8,128)S(1)}, u32[]{:S(2)}, u32[]{:S(2)}) %collective-permute-start.12) | collective-permute-done | bytes 32800 | tf_op jit(solution)/shard_map/ppermute | solution.py:596
  74.2 0.3 collective-permute-done.13
  74.5 2.6 %collective-permute-start.14 = (f32[32,1024]{1,0:T(8,128)S(1)}, f32[32,1024]{1,0:T(8,128)S(1)}, u32[]{:S(2)}, u32[]{:S(2)}) collective-permute-start(f32[32,1024]{1,0:T(8,128)S(1)} %constant_dynamic-update-slice_fusion.near_ref), channel_id=1, source_target_pairs={{0,16},{16,0},{32,48},{48,32},{64,80},{80,64},{96,112},{112,96},{1... | collective-permute-start | bytes 393224 | tf_op jit(solution)/shard_map/ppermute | solution.py:596
  77.1 1.0 collective-permute-done.14.far_ref
  78.1 0.4 collective-permute-start.19
  78.5 0.1 collective-permute-start.20
  78.7 1.5 %collective-permute-start.15 = (bf16[128,8,256]{2,1,0:T(8,128)(2,1)S(1)}, bf16[128,8,256]{2,1,0:T(8,128)(2,1)S(1)}, u32[]{:S(2)}, u32[]{:S(2)}) collective-permute-start(bf16[128,8,256]{2,1,0:T(8,128)(2,1)S(1)} %slice.18), channel_id=1, source_target_pairs={{0,32},{16,112},{32,64},{48,16},{64,96},{80,48},{96,0},{112,80},{1... | collective-permute-start | bytes 1572872 | tf_op jit(solution)/shard_map/ppermute | solution.py:596
  80.2 0.1 collective-permute-start.16
  80.3 11.4 %collective-permute-done.15.refs_0_ = bf16[128,8,256]{2,1,0:T(8,128)(2,1)S(1)} collective-permute-done((bf16[128,8,256]{2,1,0:T(8,128)(2,1)S(1)}, bf16[128,8,256]{2,1,0:T(8,128)(2,1)S(1)}, u32[]{:S(2)}, u32[]{:S(2)}) %collective-permute-start.15) | collective-permute-done | bytes 524320 | tf_op jit(solution)/shard_map/ppermute | solution.py:596
  91.7 2.6 %collective-permute-start.17 = (bf16[128,8,256]{2,1,0:T(8,128)(2,1)S(1)}, bf16[128,8,256]{2,1,0:T(8,128)(2,1)S(1)}, u32[]{:S(2)}, u32[]{:S(2)}) collective-permute-start(bf16[128,8,256]{2,1,0:T(8,128)(2,1)S(1)} %collective-permute-done.15.refs_0_), channel_id=1, source_target_pairs={{0,16},{16,0},{32,48},{48,32},{64,80},{80,64},{96,112},{112,96},{1... | collective-permute-start | bytes 1572872 | tf_op jit(solution)/shard_map/ppermute | solution.py:596
  94.3 0.1 collective-permute-done.16.refs_1_
  94.4 2.6 %weights.1 = (f32[8,48]{1,0:T(8,128)S(1)}, f32[8,16]{1,0:T(8,128)S(1)}) custom-call(f32[32,1024]{1,0:T(8,128)S(1)} %constant_dynamic-update-slice_fusion.near_ref, f32[32,1024]{1,0:T(8,128)S(1)} %collective-permute-done.14.far_ref, f32[8,1024]{1,0:T(8,128)S(1)} %get-tuple-element.53.target_ref, f32[8,128]{1,0:T(8,128)S(1)} %slice.22.error_ref), custom_call_target="tpu_custom_call" | custom-call | tf_op jit(solution)/shard_map/weights/pallas_call | solution.py:476
  97.0 0.0 collective-permute-done.20.refs_5_
  97.1 3.0 %begin.1.refs_4_ = f32[512,8,128]{2,1,0:T(8,128)S(1)} custom-call(f32[8,48]{1,0:T(8,128)S(1)} %get-tuple-element.49.w_ref, bf16[256,8,256]{2,1,0:T(8,128)(2,1)S(1)} %get-tuple-element.42.refs_0_, bf16[256,8,256]{2,1,0:T(8,128)(2,1)S(1)} %collective-permute-done.9.refs_1_, bf16[256,8,256]{2,1,0:T(8,128)(2,1)S(1)} %collective-permute-done.10.refs_2_, ...), custom_call_target="tpu_custom_call" | custom-call | tf_op jit(solution)/shard_map/begin/pallas_call | solution.py:541
  100.1 0.0 collective-permute-done.17.refs_2_
  100.1 0.0 collective-permute-done.18.refs_3_
  100.1 2.5 %update.1 = f32[8,256,256]{2,1,0:T(8,128)} custom-call(f32[8,16]{1,0:T(8,128)S(1)} %get-tuple-element.48.w_ref, bf16[128,8,256]{2,1,0:T(8,128)(2,1)S(1)} %collective-permute-done.15.refs_0_, bf16[128,8,256]{2,1,0:T(8,128)(2,1)S(1)} %collective-permute-done.16.refs_1_, bf16[128,8,256]{2,1,0:T(8,128)(2,1)S(1)} %collective-permute-done.17.refs_2_, ...), custom_call_target="tpu_custom_call" | custom-call | tf_op jit(solution)/shard_map/update/pallas_call | solution.py:556
  (38 shorter events, 0.2 us)
Async XLA Ops:
  0.0 7.6 %copy-start = (f32[256,256]{1,0:T(8,128)S(1)}, f32[256,256]{1,0:T(8,128)}, u32[]{:S(2)}) copy-start(f32[256,256]{1,0:T(8,128)} %e_ref.5) | copy-start | bytes 786436
  0.0 7.6 %copy-start.1 = (f32[256,256]{1,0:T(8,128)S(1)}, f32[256,256]{1,0:T(8,128)}, u32[]{:S(2)}) copy-start(f32[256,256]{1,0:T(8,128)} %k_ref.5) | copy-start | bytes 786436
  2.8 9.1 %collective-permute-start = (f32[9,8,256]{2,1,0:T(8,128)}, f32[9,8,256]{2,1,0:T(8,128)S(1)}, u32[]{:S(2)}, u32[]{:S(2)}) collective-permute-start(f32[9,8,256]{2,1,0:T(8,128)} %get-tuple-element.32.bottom_ref), channel_id=1, source_target_pairs={{0,4},{4,8},{8,12},{12,0},{1,5},{5,9},{9,13},{13,1},{2,6},{6,10},{... | collective-permute-start | bytes 221192 | tf_op jit(solution)/shard_map/ppermute | solution.py:583
  5.3 6.6 %copy-start.2 = (f32[9,8,256]{2,1,0:T(8,128)S(1)}, f32[9,8,256]{2,1,0:T(8,128)}, u32[]{:S(2)}) copy-start(f32[9,8,256]{2,1,0:T(8,128)} %get-tuple-element.33.top_ref) | copy-start | bytes 221188
  5.3 6.6 %copy-start.3 = (f32[9,8,256]{2,1,0:T(8,128)S(1)}, f32[9,8,256]{2,1,0:T(8,128)}, u32[]{:S(2)}) copy-start(f32[9,8,256]{2,1,0:T(8,128)} %get-tuple-element.32.bottom_ref) | copy-start | bytes 221188
  5.3 9.6 %copy-start.6 = (f32[64,8]{0,1:T(8,128)S(1)}, f32[64,8]{0,1:T(8,128)}, u32[]{:S(2)}) copy-start(f32[64,8]{0,1:T(8,128)} %param.15) | copy-start | bytes 6148
  5.3 9.6 %copy-start.7 = (f32[64]{0:T(128)S(1)}, f32[64]{0:T(128)}, u32[]{:S(2)}) copy-start(f32[64]{0:T(128)} %param.14) | copy-start | bytes 772
  5.3 9.6 %copy-start.8 = (f32[64]{0:T(128)S(1)}, f32[64]{0:T(128)}, u32[]{:S(2)}) copy-start(f32[64]{0:T(128)} %param.13) | copy-start | bytes 772
  5.3 6.5 %collective-permute-start.1 = (f32[9,8,256]{2,1,0:T(8,128)}, f32[9,8,256]{2,1,0:T(8,128)S(1)}, u32[]{:S(2)}, u32[]{:S(2)}) collective-permute-start(f32[9,8,256]{2,1,0:T(8,128)} %get-tuple-element.33.top_ref), channel_id=1, source_target_pairs={{0,12},{4,0},{8,4},{12,8},{1,13},{5,1},{9,5},{13,9},{2,14},{6,2},{... | collective-permute-start | bytes 221192 | tf_op jit(solution)/shard_map/ppermute | solution.py:584
  12.0 4.9 %collective-permute-start.2 = (f32[9,3,8,128]{3,2,1,0:T(8,128)S(1)}, f32[9,3,8,128]{3,2,1,0:T(8,128)S(1)}, u32[]{:S(2)}, u32[]{:S(2)}) collective-permute-start(f32[9,3,8,128]{3,2,1,0:T(8,128)S(1)} %get-tuple-element.38), channel_id=1, source_target_pairs={{0,1},{1,2},{2,3},{3,0},{4,5},{5,6},{6,7},{7,4},{8,9},{9,10},{10,1... | collective-permute-start | bytes 331784 | tf_op jit(solution)/shard_map/ppermute | solution.py:587
  13.4 3.6 %collective-permute-start.3 = (f32[9,3,8,128]{3,2,1,0:T(8,128)S(1)}, f32[9,3,8,128]{3,2,1,0:T(8,128)S(1)}, u32[]{:S(2)}, u32[]{:S(2)}) collective-permute-start(f32[9,3,8,128]{3,2,1,0:T(8,128)S(1)} %get-tuple-element.39), channel_id=1, source_target_pairs={{0,3},{1,0},{2,1},{3,2},{4,7},{5,4},{6,5},{7,6},{8,11},{9,8},{10,9... | collective-permute-start | bytes 331784 | tf_op jit(solution)/shard_map/ppermute | solution.py:588
  17.0 20.6 %copy-start.4 = (s32[8,128]{1,0:T(8,128)S(1)}, s32[8,128]{1,0:T(8,128)}, u32[]{:S(2)}) copy-start(s32[8,128]{1,0:T(8,128)} %get-tuple-element.29.code_ref) | copy-start | bytes 12292
  17.0 20.6 %copy-start.5 = (f32[8,128]{1,0:T(8,128)S(1)}, f32[8,128]{1,0:T(8,128)}, u32[]{:S(2)}) copy-start(f32[8,128]{1,0:T(8,128)} %get-tuple-element.41.inside_ref) | copy-start | bytes 12292
  35.1 9.3 %collective-permute-start.5 = (bf16[256,8,256]{2,1,0:T(8,128)(2,1)S(1)}, bf16[256,8,256]{2,1,0:T(8,128)(2,1)S(1)}, u32[]{:S(2)}, u32[]{:S(2)}) collective-permute-start(bf16[256,8,256]{2,1,0:T(8,128)(2,1)S(1)} %get-tuple-element.42.refs_0_), channel_id=1, source_target_pairs={{0,16},{16,0},{32,48},{48,32},{64,80},{80,64},{96,112},{112,96},{1... | collective-permute-start | bytes 3145736 | tf_op jit(solution)/shard_map/ppermute | solution.py:596
  40.3 4.1 %collective-permute-start.4 = (f32[8,2176]{1,0:T(8,128)S(1)}, f32[8,2176]{1,0:T(8,128)S(1)}, u32[]{:S(2)}, u32[]{:S(2)}) collective-permute-start(f32[8,2176]{1,0:T(8,128)S(1)} %pad_maximum_fusion), channel_id=1, source_target_pairs={{0,1},{1,0},{2,3},{3,2},{4,5},{5,4},{6,7},{7,6},{8,9},{9,8},{10,11... | collective-permute-start | bytes 208904 | tf_op jit(solution)/shard_map/ppermute | solution.py:613
  41.7 22.9 %collective-permute-start.10 = (bf16[256,8,256]{2,1,0:T(8,128)(2,1)S(1)}, bf16[256,8,256]{2,1,0:T(8,128)(2,1)S(1)}, u32[]{:S(2)}, u32[]{:S(2)}) collective-permute-start(bf16[256,8,256]{2,1,0:T(8,128)(2,1)S(1)} %get-tuple-element.42.refs_0_), channel_id=1, source_target_pairs={{0,96},{16,48},{32,0},{48,80},{64,32},{80,112},{96,64},{112,16},{1... | collective-permute-start | bytes 3145736 | tf_op jit(solution)/shard_map/ppermute | solution.py:596
  42.9 24.7 %collective-permute-start.9 = (bf16[256,8,256]{2,1,0:T(8,128)(2,1)S(1)}, bf16[256,8,256]{2,1,0:T(8,128)(2,1)S(1)}, u32[]{:S(2)}, u32[]{:S(2)}) collective-permute-start(bf16[256,8,256]{2,1,0:T(8,128)(2,1)S(1)} %get-tuple-element.42.refs_0_), channel_id=1, source_target_pairs={{0,32},{16,112},{32,64},{48,16},{64,96},{80,48},{96,0},{112,80},{1... | collective-permute-start | bytes 3145736 | tf_op jit(solution)/shard_map/ppermute | solution.py:596
  44.4 4.5 %collective-permute-start.6 = (f32[8,2176]{1,0:T(8,128)S(1)}, f32[8,2176]{1,0:T(8,128)S(1)}, u32[]{:S(2)}, u32[]{:S(2)}) collective-permute-start(f32[8,2176]{1,0:T(8,128)S(1)} %fusion), channel_id=1, source_target_pairs={{0,3},{1,2},{2,1},{3,0},{4,7},{5,6},{6,5},{7,4},{8,11},{9,10},{10,... | collective-permute-start | bytes 208904 | tf_op jit(solution)/shard_map/ppermute | solution.py:613
  48.8 3.5 %collective-permute-start.7 = (f32[8,2176]{1,0:T(8,128)S(1)}, f32[8,2176]{1,0:T(8,128)S(1)}, u32[]{:S(2)}, u32[]{:S(2)}) collective-permute-start(f32[8,2176]{1,0:T(8,128)S(1)} %add.45), channel_id=1, source_target_pairs={{0,4},{4,0},{8,12},{12,8},{1,5},{5,1},{9,13},{13,9},{2,6},{6,2},{1... | collective-permute-start | bytes 208904 | tf_op jit(solution)/shard_map/ppermute | solution.py:613
  52.4 4.7 %collective-permute-start.8 = (f32[8,2176]{1,0:T(8,128)S(1)}, f32[8,2176]{1,0:T(8,128)S(1)}, u32[]{:S(2)}, u32[]{:S(2)}) collective-permute-start(f32[8,2176]{1,0:T(8,128)S(1)} %add.46), channel_id=1, source_target_pairs={{0,12},{4,8},{8,4},{12,0},{1,13},{5,9},{9,5},{13,1},{2,14},{6,10},... | collective-permute-start | bytes 208904 | tf_op jit(solution)/shard_map/ppermute | solution.py:613
  67.6 4.1 %collective-permute-start.11 = (f32[8,1024]{1,0:T(8,128)S(1)}, f32[8,1024]{1,0:T(8,128)S(1)}, u32[]{:S(2)}, u32[]{:S(2)}) collective-permute-start(f32[8,1024]{1,0:T(8,128)S(1)} %get-tuple-element.44), channel_id=1, source_target_pairs={{0,32},{16,112},{32,64},{48,16},{64,96},{80,48},{96,0},{112,80},{1... | collective-permute-start | bytes 98312 | tf_op jit(solution)/shard_map/ppermute | solution.py:596
  70.2 4.0 %collective-permute-start.12 = (f32[8,1024]{1,0:T(8,128)S(1)}, f32[8,1024]{1,0:T(8,128)S(1)}, u32[]{:S(2)}, u32[]{:S(2)}) collective-permute-start(f32[8,1024]{1,0:T(8,128)S(1)} %get-tuple-element.44), channel_id=1, source_target_pairs={{0,96},{16,48},{32,0},{48,80},{64,32},{80,112},{96,64},{112,16},{1... | collective-permute-start | bytes 98312 | tf_op jit(solution)/shard_map/ppermute | solution.py:596
  70.2 4.3 %collective-permute-start.13 = (f32[8,1024]{1,0:T(8,128)S(1)}, f32[8,1024]{1,0:T(8,128)S(1)}, u32[]{:S(2)}, u32[]{:S(2)}) collective-permute-start(f32[8,1024]{1,0:T(8,128)S(1)} %get-tuple-element.44), channel_id=1, source_target_pairs={{0,64},{16,80},{32,96},{48,112},{64,0},{80,16},{96,32},{112,48},{1... | collective-permute-start | bytes 98312 | tf_op jit(solution)/shard_map/ppermute | solution.py:596
  74.5 3.6 %collective-permute-start.14 = (f32[32,1024]{1,0:T(8,128)S(1)}, f32[32,1024]{1,0:T(8,128)S(1)}, u32[]{:S(2)}, u32[]{:S(2)}) collective-permute-start(f32[32,1024]{1,0:T(8,128)S(1)} %constant_dynamic-update-slice_fusion.near_ref), channel_id=1, source_target_pairs={{0,16},{16,0},{32,48},{48,32},{64,80},{80,64},{96,112},{112,96},{1... | collective-permute-start | bytes 393224 | tf_op jit(solution)/shard_map/ppermute | solution.py:596
  78.1 18.9 %collective-permute-start.19 = (bf16[256,8,256]{2,1,0:T(8,128)(2,1)S(1)}, bf16[256,8,256]{2,1,0:T(8,128)(2,1)S(1)}, u32[]{:S(2)}, u32[]{:S(2)}) collective-permute-start(bf16[256,8,256]{2,1,0:T(8,128)(2,1)S(1)} %collective-permute-done.9.refs_1_), channel_id=1, source_target_pairs={{0,16},{16,0},{32,48},{48,32},{64,80},{80,64},{96,112},{112,96},{1... | collective-permute-start | bytes 3145736 | tf_op jit(solution)/shard_map/ppermute | solution.py:596
  78.5 18.6 %collective-permute-start.20 = (bf16[256,8,256]{2,1,0:T(8,128)(2,1)S(1)}, bf16[256,8,256]{2,1,0:T(8,128)(2,1)S(1)}, u32[]{:S(2)}, u32[]{:S(2)}) collective-permute-start(bf16[256,8,256]{2,1,0:T(8,128)(2,1)S(1)} %collective-permute-done.10.refs_2_), channel_id=1, source_target_pairs={{0,16},{16,0},{32,48},{48,32},{64,80},{80,64},{96,112},{112,96},{1... | collective-permute-start | bytes 3145736 | tf_op jit(solution)/shard_map/ppermute | solution.py:596
  78.7 13.1 %collective-permute-start.15 = (bf16[128,8,256]{2,1,0:T(8,128)(2,1)S(1)}, bf16[128,8,256]{2,1,0:T(8,128)(2,1)S(1)}, u32[]{:S(2)}, u32[]{:S(2)}) collective-permute-start(bf16[128,8,256]{2,1,0:T(8,128)(2,1)S(1)} %slice.18), channel_id=1, source_target_pairs={{0,32},{16,112},{32,64},{48,16},{64,96},{80,48},{96,0},{112,80},{1... | collective-permute-start | bytes 1572872 | tf_op jit(solution)/shard_map/ppermute | solution.py:596
  80.2 14.2 %collective-permute-start.16 = (bf16[128,8,256]{2,1,0:T(8,128)(2,1)S(1)}, bf16[128,8,256]{2,1,0:T(8,128)(2,1)S(1)}, u32[]{:S(2)}, u32[]{:S(2)}) collective-permute-start(bf16[128,8,256]{2,1,0:T(8,128)(2,1)S(1)} %slice.19), channel_id=1, source_target_pairs={{0,96},{16,48},{32,0},{48,80},{64,32},{80,112},{96,64},{112,16},{1... | collective-permute-start | bytes 1572872 | tf_op jit(solution)/shard_map/ppermute | solution.py:596
  91.7 8.3 %collective-permute-start.17 = (bf16[128,8,256]{2,1,0:T(8,128)(2,1)S(1)}, bf16[128,8,256]{2,1,0:T(8,128)(2,1)S(1)}, u32[]{:S(2)}, u32[]{:S(2)}) collective-permute-start(bf16[128,8,256]{2,1,0:T(8,128)(2,1)S(1)} %collective-permute-done.15.refs_0_), channel_id=1, source_target_pairs={{0,16},{16,0},{32,48},{48,32},{64,80},{80,64},{96,112},{112,96},{1... | collective-permute-start | bytes 1572872 | tf_op jit(solution)/shard_map/ppermute | solution.py:596
  94.4 5.7 %collective-permute-start.18 = (bf16[128,8,256]{2,1,0:T(8,128)(2,1)S(1)}, bf16[128,8,256]{2,1,0:T(8,128)(2,1)S(1)}, u32[]{:S(2)}, u32[]{:S(2)}) collective-permute-start(bf16[128,8,256]{2,1,0:T(8,128)(2,1)S(1)} %collective-permute-done.16.refs_1_), channel_id=1, source_target_pairs={{0,16},{16,0},{32,48},{48,32},{64,80},{80,64},{96,112},{112,96},{1... | collective-permute-start | bytes 1572872 | tf_op jit(solution)/shard_map/ppermute | solution.py:596

commit v6 on v5

--- a/solution.py
+++ b/solution.py
@@ -619,8 +619,10 @@
     )
     observed, a, b = lax.optimization_barrier((observed, a, b))
     half = size_x // 2
-    c0, c1 = send(a[:half], 1), send(b[half:], -1)
-    parts = [send(observed, by) for by in (1, -1, 2)]
+    c0 = send(a[:half], 1)
+    c1 = send(b[half:], -1)
+    opposite, up_part = send(observed, 2), send(observed, 1)
+    parts = [up_part, send(observed, -1), opposite]
     near = jnp.concatenate([observed] + parts)
     far = send(near, 0, True)
     far, a, b = lax.optimization_barrier((far, a, b))

time: 103 us -> 103 us (level)
  no operation moved by 1% of the time
where the time goes in v6:
time: 103 us
  Pallas kernels  36 us (35%)
  waiting for transfers between devices  35.7 us (35%)
  starting transfers between devices  29.8 us (29%)
    ppermute x13, waiting for transfers between devices, send(): lax.ppermute(v, 'mem', [(i, i ^ 1) for i in range(n_m)] if swap else to)  25.7 us
    pallas_call x1, Pallas kernels, run_steps(): pl.pallas_call(steps_kernel, in_specs=[HBM_SPEC] * 2 + [VMEM_SPEC] * 6, o...  18.1 us
    ppermute x13, starting transfers between devices, send(): lax.ppermute(v, 'mem', [(i, i ^ 1) for i in range(n_m)] if swap else to)  16.6 us
    ppermute x4, waiting for transfers between devices, local(): lax.ppermute(line, axis, [(i, i ^ span - 1) for i in range(n)])  8.46 us
    ppermute x4, starting transfers between devices, local(): lax.ppermute(line, axis, [(i, i ^ span - 1) for i in range(n)])  5.64 us
    pallas_call x1, Pallas kernels, turn(): pl.pallas_call(turn_kernel, in_specs=[HBM_SPEC] * 2 + [VMEM_SPEC] * 2, ou...  4.27 us
    pallas_call x1, Pallas kernels, begin(): pl.pallas_call(begin_kernel, in_specs=[VMEM_SPEC] * (len(pieces) + 2), ou...  2.96 us
    pallas_call x1, Pallas kernels, ends(): pl.pallas_call(ends_kernel, in_specs=[VMEM_SPEC] + [HBM_SPEC] * 2 + [VMEM...  2.76 us
  transfers between devices with their start and end apart: 21, of which 11 were waited for; matrix products, arithmetic and copies ran while one was open for 1% of the time, Pallas kernels for 12%

profile of v6, /device:TPU:1, one launch (start us, length us, event | category | flops | bytes accessed | tf_op | source)
XLA Modules:
  0.0 102.6 jit_solution(11669249976210418611)
XLA Ops:
  0.0 2.8 %ends.1 = (f32[9,8,256]{2,1,0:T(8,128)}, f32[9,8,256]{2,1,0:T(8,128)}, s32[8,128]{1,0:T(8,128)}, f32[8,128]{1,0:T(8,128)}) custom-call(s32[8,128]{1,0:T(8,128)} %bitcast.4, f32[8,256,256]{2,1,0:T(8,128)} %p_in.1, f32[8,256,256]{2,1,0:T(8,128)} %w_in.1, f32[256,256]{1,0:T(8,128)} %e_ref.5, f32[256,256]{1,0:T(8,128)} %k_ref.5), custom_call_target="tpu_custom_call" | custom-call | tf_op jit(solution)/shard_map/ends/pallas_call | solution.py:75
  2.8 2.5 %collective-permute-start = (f32[9,8,256]{2,1,0:T(8,128)}, f32[9,8,256]{2,1,0:T(8,128)S(1)}, u32[]{:S(2)}, u32[]{:S(2)}) collective-permute-start(f32[9,8,256]{2,1,0:T(8,128)} %get-tuple-element.32.bottom_ref), channel_id=1, source_target_pairs={{0,4},{4,8},{8,12},{12,0},{1,5},{5,9},{9,13},{13,1},{2,6},{6,10},{... | collective-permute-start | bytes 221192 | tf_op jit(solution)/shard_map/ppermute | solution.py:583
  5.3 0.0 copy-start.8
  5.3 2.2 %collective-permute-start.1 = (f32[9,8,256]{2,1,0:T(8,128)}, f32[9,8,256]{2,1,0:T(8,128)S(1)}, u32[]{:S(2)}, u32[]{:S(2)}) collective-permute-start(f32[9,8,256]{2,1,0:T(8,128)} %get-tuple-element.33.top_ref), channel_id=1, source_target_pairs={{0,12},{4,0},{8,4},{12,8},{1,13},{5,1},{9,5},{13,9},{2,14},{6,2},{... | collective-permute-start | bytes 221192 | tf_op jit(solution)/shard_map/ppermute | solution.py:584
  7.6 4.3 %turn.1 = (f32[256,8,256]{2,1,0:T(8,128)}, f32[256,8,256]{2,1,0:T(8,128)}, f32[8,3,8,128]{3,2,1,0:T(8,128)S(1)}, f32[8,3,8,128]{3,2,1,0:T(8,128)S(1)}) custom-call(f32[8,256,256]{2,1,0:T(8,128)} %p_in.1, f32[8,256,256]{2,1,0:T(8,128)} %w_in.1, f32[256,256]{1,0:T(8,128)S(1)} %copy-done, f32[256,256]{1,0:T(8,128)S(1)} %copy-done.1), custom_call_target="tpu_custom_call" | custom-call | flops 10000000 | bytes 9437184 | tf_op jit(solution)/shard_map/turn/pallas_call | solution.py:157
  11.8 0.0 collective-permute-done.up_ref
  11.8 0.0 collective-permute-done.1.down_ref
  11.9 0.1 rows.1
  12.0 1.4 %collective-permute-start.2 = (f32[9,3,8,128]{3,2,1,0:T(8,128)S(1)}, f32[9,3,8,128]{3,2,1,0:T(8,128)S(1)}, u32[]{:S(2)}, u32[]{:S(2)}) collective-permute-start(f32[9,3,8,128]{3,2,1,0:T(8,128)S(1)} %get-tuple-element.38), channel_id=1, source_target_pairs={{0,1},{1,2},{2,3},{3,0},{4,5},{5,6},{6,7},{7,4},{8,9},{9,10},{10,1... | collective-permute-start | bytes 331784 | tf_op jit(solution)/shard_map/ppermute | solution.py:587
  13.4 1.5 %collective-permute-start.3 = (f32[9,3,8,128]{3,2,1,0:T(8,128)S(1)}, f32[9,3,8,128]{3,2,1,0:T(8,128)S(1)}, u32[]{:S(2)}, u32[]{:S(2)}) collective-permute-start(f32[9,3,8,128]{3,2,1,0:T(8,128)S(1)} %get-tuple-element.39), channel_id=1, source_target_pairs={{0,3},{1,0},{2,1},{3,2},{4,7},{5,4},{6,5},{7,6},{8,11},{9,8},{10,9... | collective-permute-start | bytes 331784 | tf_op jit(solution)/shard_map/ppermute | solution.py:588
  14.9 0.3 dynamic_update_slice.6
  15.2 0.2 dynamic_update_slice.7
  15.4 1.5 %collective-permute-done.2.fl_ref = f32[9,3,8,128]{3,2,1,0:T(8,128)S(1)} collective-permute-done((f32[9,3,8,128]{3,2,1,0:T(8,128)S(1)}, f32[9,3,8,128]{3,2,1,0:T(8,128)S(1)}, u32[]{:S(2)}, u32[]{:S(2)}) %collective-permute-start.2) | collective-permute-done | bytes 110624 | tf_op jit(solution)/shard_map/ppermute | solution.py:587
  16.9 0.0 collective-permute-done.3.fr_ref
  17.0 18.1 %steps.1 = (f32[512,8,128]{2,1,0:T(8,128)S(1)}, bf16[256,8,256]{2,1,0:T(8,128)(2,1)S(1)}) custom-call(f32[256,8,256]{2,1,0:T(8,128)} %get-tuple-element.30.pt_in, f32[256,8,256]{2,1,0:T(8,128)} %get-tuple-element.31.wt_in, f32[256,256]{1,0:T(8,128)S(1)} %copy-done, f32[256,256]{1,0:T(8,128)S(1)} %copy-done.1, f32[9,8,256]{2,1,0:T(8,128)S(1)} %get-tuple-element.36.above_ref, ...), custom_call_target="tpu_custom_call" | custom-call | tf_op jit(solution)/shard_map/steps/pallas_call | solution.py:369
  35.1 2.5 %collective-permute-start.5 = (bf16[256,8,256]{2,1,0:T(8,128)(2,1)S(1)}, bf16[256,8,256]{2,1,0:T(8,128)(2,1)S(1)}, u32[]{:S(2)}, u32[]{:S(2)}) collective-permute-start(bf16[256,8,256]{2,1,0:T(8,128)(2,1)S(1)} %get-tuple-element.42.refs_0_), channel_id=1, source_target_pairs={{0,16},{16,0},{32,48},{48,32},{64,80},{80,64},{96,112},{112,96},{1... | collective-permute-start | bytes 3145736 | tf_op jit(solution)/shard_map/ppermute | solution.py:596
  37.6 2.7 %picks.1 = f32[8,1024]{1,0:T(8,128)S(1)} custom-call(s32[8,128]{1,0:T(8,128)S(1)} %copy-done.4, f32[512,8,128]{2,1,0:T(8,128)S(1)} %get-tuple-element.40.f_ref.refs_6_, f32[8,128]{1,0:T(8,128)S(1)} %copy-done.5), custom_call_target="tpu_custom_call" | custom-call | tf_op jit(solution)/shard_map/picks/pallas_call | solution.py:400
  40.3 1.4 %collective-permute-start.4 = (f32[8,2176]{1,0:T(8,128)S(1)}, f32[8,2176]{1,0:T(8,128)S(1)}, u32[]{:S(2)}, u32[]{:S(2)}) collective-permute-start(f32[8,2176]{1,0:T(8,128)S(1)} %pad_maximum_fusion), channel_id=1, source_target_pairs={{0,1},{1,0},{2,3},{3,2},{4,5},{5,4},{6,7},{7,6},{8,9},{9,8},{10,11... | collective-permute-start | bytes 208904 | tf_op jit(solution)/shard_map/ppermute | solution.py:613
  41.7 1.2 %collective-permute-start.10 = (bf16[256,8,256]{2,1,0:T(8,128)(2,1)S(1)}, bf16[256,8,256]{2,1,0:T(8,128)(2,1)S(1)}, u32[]{:S(2)}, u32[]{:S(2)}) collective-permute-start(bf16[256,8,256]{2,1,0:T(8,128)(2,1)S(1)} %get-tuple-element.42.refs_0_), channel_id=1, source_target_pairs={{0,96},{16,48},{32,0},{48,80},{64,32},{80,112},{96,64},{112,16},{1... | collective-permute-start | bytes 3145736 | tf_op jit(solution)/shard_map/ppermute | solution.py:596
  42.9 1.5 %collective-permute-start.9 = (bf16[256,8,256]{2,1,0:T(8,128)(2,1)S(1)}, bf16[256,8,256]{2,1,0:T(8,128)(2,1)S(1)}, u32[]{:S(2)}, u32[]{:S(2)}) collective-permute-start(bf16[256,8,256]{2,1,0:T(8,128)(2,1)S(1)} %get-tuple-element.42.refs_0_), channel_id=1, source_target_pairs={{0,32},{16,112},{32,64},{48,16},{64,96},{80,48},{96,0},{112,80},{1... | collective-permute-start | bytes 3145736 | tf_op jit(solution)/shard_map/ppermute | solution.py:596
  44.4 0.0 collective-permute-done.5.refs_3_
  44.4 2.4 %collective-permute-start.6 = (f32[8,2176]{1,0:T(8,128)S(1)}, f32[8,2176]{1,0:T(8,128)S(1)}, u32[]{:S(2)}, u32[]{:S(2)}) collective-permute-start(f32[8,2176]{1,0:T(8,128)S(1)} %fusion), channel_id=1, source_target_pairs={{0,3},{1,2},{2,1},{3,0},{4,7},{5,6},{6,5},{7,4},{8,11},{9,10},{10,... | collective-permute-start | bytes 208904 | tf_op jit(solution)/shard_map/ppermute | solution.py:613
  46.8 2.0 %collective-permute-done.6 = f32[8,2176]{1,0:T(8,128)S(1)} collective-permute-done((f32[8,2176]{1,0:T(8,128)S(1)}, f32[8,2176]{1,0:T(8,128)S(1)}, u32[]{:S(2)}, u32[]{:S(2)}) %collective-permute-start.6) | collective-permute-done | bytes 69664 | tf_op jit(solution)/shard_map/ppermute | solution.py:613
  48.8 0.1 collective-permute-start.7
  48.9 3.4 %collective-permute-done.7 = f32[8,2176]{1,0:T(8,128)S(1)} collective-permute-done((f32[8,2176]{1,0:T(8,128)S(1)}, f32[8,2176]{1,0:T(8,128)S(1)}, u32[]{:S(2)}, u32[]{:S(2)}) %collective-permute-start.7) | collective-permute-done | bytes 69664 | tf_op jit(solution)/shard_map/ppermute | solution.py:613
  52.4 1.8 %collective-permute-start.8 = (f32[8,2176]{1,0:T(8,128)S(1)}, f32[8,2176]{1,0:T(8,128)S(1)}, u32[]{:S(2)}, u32[]{:S(2)}) collective-permute-start(f32[8,2176]{1,0:T(8,128)S(1)} %add.46), channel_id=1, source_target_pairs={{0,12},{4,8},{8,4},{12,0},{1,13},{5,9},{9,5},{13,1},{2,14},{6,10},... | collective-permute-start | bytes 208904 | tf_op jit(solution)/shard_map/ppermute | solution.py:613
  54.2 3.0 %collective-permute-done.8 = f32[8,2176]{1,0:T(8,128)S(1)} collective-permute-done((f32[8,2176]{1,0:T(8,128)S(1)}, f32[8,2176]{1,0:T(8,128)S(1)}, u32[]{:S(2)}, u32[]{:S(2)}) %collective-permute-start.8) | collective-permute-done | bytes 69664 | tf_op jit(solution)/shard_map/ppermute | solution.py:613
  57.2 7.4 %collective-permute-done.10.refs_2_ = bf16[256,8,256]{2,1,0:T(8,128)(2,1)S(1)} collective-permute-done((bf16[256,8,256]{2,1,0:T(8,128)(2,1)S(1)}, bf16[256,8,256]{2,1,0:T(8,128)(2,1)S(1)}, u32[]{:S(2)}, u32[]{:S(2)}) %collective-permute-start.10) | collective-permute-done | bytes 1048608 | tf_op jit(solution)/shard_map/ppermute | solution.py:596
  64.5 3.1 %collective-permute-done.9.refs_1_ = bf16[256,8,256]{2,1,0:T(8,128)(2,1)S(1)} collective-permute-done((bf16[256,8,256]{2,1,0:T(8,128)(2,1)S(1)}, bf16[256,8,256]{2,1,0:T(8,128)(2,1)S(1)}, u32[]{:S(2)}, u32[]{:S(2)}) %collective-permute-start.9) | collective-permute-done | bytes 1048608 | tf_op jit(solution)/shard_map/ppermute | solution.py:596
  67.6 2.5 %collective-permute-start.11 = (f32[8,1024]{1,0:T(8,128)S(1)}, f32[8,1024]{1,0:T(8,128)S(1)}, u32[]{:S(2)}, u32[]{:S(2)}) collective-permute-start(f32[8,1024]{1,0:T(8,128)S(1)} %get-tuple-element.44), channel_id=1, source_target_pairs={{0,32},{16,112},{32,64},{48,16},{64,96},{80,48},{96,0},{112,80},{1... | collective-permute-start | bytes 98312 | tf_op jit(solution)/shard_map/ppermute | solution.py:596
  70.2 1.5 %collective-permute-start.13 = (f32[8,1024]{1,0:T(8,128)S(1)}, f32[8,1024]{1,0:T(8,128)S(1)}, u32[]{:S(2)}, u32[]{:S(2)}) collective-permute-start(f32[8,1024]{1,0:T(8,128)S(1)} %get-tuple-element.44), channel_id=1, source_target_pairs={{0,64},{16,80},{32,96},{48,112},{64,0},{80,16},{96,32},{112,48},{1... | collective-permute-start | bytes 98312 | tf_op jit(solution)/shard_map/ppermute | solution.py:596
  71.7 2.5 %collective-permute-done.12 = f32[8,1024]{1,0:T(8,128)S(1)} collective-permute-done((f32[8,1024]{1,0:T(8,128)S(1)}, f32[8,1024]{1,0:T(8,128)S(1)}, u32[]{:S(2)}, u32[]{:S(2)}) %collective-permute-start.12) | collective-permute-done | bytes 32800 | tf_op jit(solution)/shard_map/ppermute | solution.py:596
  74.2 0.3 collective-permute-done.13
  74.5 2.6 %collective-permute-start.14 = (f32[32,1024]{1,0:T(8,128)S(1)}, f32[32,1024]{1,0:T(8,128)S(1)}, u32[]{:S(2)}, u32[]{:S(2)}) collective-permute-start(f32[32,1024]{1,0:T(8,128)S(1)} %constant_dynamic-update-slice_fusion.near_ref), channel_id=1, source_target_pairs={{0,16},{16,0},{32,48},{48,32},{64,80},{80,64},{96,112},{112,96},{1... | collective-permute-start | bytes 393224 | tf_op jit(solution)/shard_map/ppermute | solution.py:596
  77.1 1.0 collective-permute-done.14.far_ref
  78.1 0.4 collective-permute-start.19
  78.5 0.1 collective-permute-start.20
  78.7 1.5 %collective-permute-start.15 = (bf16[128,8,256]{2,1,0:T(8,128)(2,1)S(1)}, bf16[128,8,256]{2,1,0:T(8,128)(2,1)S(1)}, u32[]{:S(2)}, u32[]{:S(2)}) collective-permute-start(bf16[128,8,256]{2,1,0:T(8,128)(2,1)S(1)} %slice.18), channel_id=1, source_target_pairs={{0,32},{16,112},{32,64},{48,16},{64,96},{80,48},{96,0},{112,80},{1... | collective-permute-start | bytes 1572872 | tf_op jit(solution)/shard_map/ppermute | solution.py:596
  80.2 0.1 collective-permute-start.16
  80.3 11.4 %collective-permute-done.15.refs_0_ = bf16[128,8,256]{2,1,0:T(8,128)(2,1)S(1)} collective-permute-done((bf16[128,8,256]{2,1,0:T(8,128)(2,1)S(1)}, bf16[128,8,256]{2,1,0:T(8,128)(2,1)S(1)}, u32[]{:S(2)}, u32[]{:S(2)}) %collective-permute-start.15) | collective-permute-done | bytes 524320 | tf_op jit(solution)/shard_map/ppermute | solution.py:596
  91.7 2.6 %collective-permute-start.17 = (bf16[128,8,256]{2,1,0:T(8,128)(2,1)S(1)}, bf16[128,8,256]{2,1,0:T(8,128)(2,1)S(1)}, u32[]{:S(2)}, u32[]{:S(2)}) collective-permute-start(bf16[128,8,256]{2,1,0:T(8,128)(2,1)S(1)} %collective-permute-done.15.refs_0_), channel_id=1, source_target_pairs={{0,16},{16,0},{32,48},{48,32},{64,80},{80,64},{96,112},{112,96},{1... | collective-permute-start | bytes 1572872 | tf_op jit(solution)/shard_map/ppermute | solution.py:596
  94.3 0.1 collective-permute-done.16.refs_1_
  94.4 2.6 %weights.1 = (f32[8,48]{1,0:T(8,128)S(1)}, f32[8,16]{1,0:T(8,128)S(1)}) custom-call(f32[32,1024]{1,0:T(8,128)S(1)} %constant_dynamic-update-slice_fusion.near_ref, f32[32,1024]{1,0:T(8,128)S(1)} %collective-permute-done.14.far_ref, f32[8,1024]{1,0:T(8,128)S(1)} %get-tuple-element.53.target_ref, f32[8,128]{1,0:T(8,128)S(1)} %slice.22.error_ref), custom_call_target="tpu_custom_call" | custom-call | tf_op jit(solution)/shard_map/weights/pallas_call | solution.py:476
  97.0 0.0 collective-permute-done.20.refs_5_
  97.1 3.0 %begin.1.refs_4_ = f32[512,8,128]{2,1,0:T(8,128)S(1)} custom-call(f32[8,48]{1,0:T(8,128)S(1)} %get-tuple-element.49.w_ref, bf16[256,8,256]{2,1,0:T(8,128)(2,1)S(1)} %get-tuple-element.42.refs_0_, bf16[256,8,256]{2,1,0:T(8,128)(2,1)S(1)} %collective-permute-done.9.refs_1_, bf16[256,8,256]{2,1,0:T(8,128)(2,1)S(1)} %collective-permute-done.10.refs_2_, ...), custom_call_target="tpu_custom_call" | custom-call | tf_op jit(solution)/shard_map/begin/pallas_call | solution.py:541
  100.1 0.0 collective-permute-done.17.refs_2_
  100.1 0.0 collective-permute-done.18.refs_3_
  100.1 2.5 %update.1 = f32[8,256,256]{2,1,0:T(8,128)} custom-call(f32[8,16]{1,0:T(8,128)S(1)} %get-tuple-element.48.w_ref, bf16[128,8,256]{2,1,0:T(8,128)(2,1)S(1)} %collective-permute-done.15.refs_0_, bf16[128,8,256]{2,1,0:T(8,128)(2,1)S(1)} %collective-permute-done.16.refs_1_, bf16[128,8,256]{2,1,0:T(8,128)(2,1)S(1)} %collective-permute-done.17.refs_2_, ...), custom_call_target="tpu_custom_call" | custom-call | tf_op jit(solution)/shard_map/update/pallas_call | solution.py:556
  (38 shorter events, 0.2 us)
Async XLA Ops:
  0.0 7.6 %copy-start = (f32[256,256]{1,0:T(8,128)S(1)}, f32[256,256]{1,0:T(8,128)}, u32[]{:S(2)}) copy-start(f32[256,256]{1,0:T(8,128)} %e_ref.5) | copy-start | bytes 786436
  0.0 7.6 %copy-start.1 = (f32[256,256]{1,0:T(8,128)S(1)}, f32[256,256]{1,0:T(8,128)}, u32[]{:S(2)}) copy-start(f32[256,256]{1,0:T(8,128)} %k_ref.5) | copy-start | bytes 786436
  2.8 9.1 %collective-permute-start = (f32[9,8,256]{2,1,0:T(8,128)}, f32[9,8,256]{2,1,0:T(8,128)S(1)}, u32[]{:S(2)}, u32[]{:S(2)}) collective-permute-start(f32[9,8,256]{2,1,0:T(8,128)} %get-tuple-element.32.bottom_ref), channel_id=1, source_target_pairs={{0,4},{4,8},{8,12},{12,0},{1,5},{5,9},{9,13},{13,1},{2,6},{6,10},{... | collective-permute-start | bytes 221192 | tf_op jit(solution)/shard_map/ppermute | solution.py:583
  5.3 6.6 %copy-start.2 = (f32[9,8,256]{2,1,0:T(8,128)S(1)}, f32[9,8,256]{2,1,0:T(8,128)}, u32[]{:S(2)}) copy-start(f32[9,8,256]{2,1,0:T(8,128)} %get-tuple-element.33.top_ref) | copy-start | bytes 221188
  5.3 6.6 %copy-start.3 = (f32[9,8,256]{2,1,0:T(8,128)S(1)}, f32[9,8,256]{2,1,0:T(8,128)}, u32[]{:S(2)}) copy-start(f32[9,8,256]{2,1,0:T(8,128)} %get-tuple-element.32.bottom_ref) | copy-start | bytes 221188
  5.3 9.6 %copy-start.6 = (f32[64,8]{0,1:T(8,128)S(1)}, f32[64,8]{0,1:T(8,128)}, u32[]{:S(2)}) copy-start(f32[64,8]{0,1:T(8,128)} %param.15) | copy-start | bytes 6148
  5.3 9.6 %copy-start.7 = (f32[64]{0:T(128)S(1)}, f32[64]{0:T(128)}, u32[]{:S(2)}) copy-start(f32[64]{0:T(128)} %param.14) | copy-start | bytes 772
  5.3 9.6 %copy-start.8 = (f32[64]{0:T(128)S(1)}, f32[64]{0:T(128)}, u32[]{:S(2)}) copy-start(f32[64]{0:T(128)} %param.13) | copy-start | bytes 772
  5.3 6.5 %collective-permute-start.1 = (f32[9,8,256]{2,1,0:T(8,128)}, f32[9,8,256]{2,1,0:T(8,128)S(1)}, u32[]{:S(2)}, u32[]{:S(2)}) collective-permute-start(f32[9,8,256]{2,1,0:T(8,128)} %get-tuple-element.33.top_ref), channel_id=1, source_target_pairs={{0,12},{4,0},{8,4},{12,8},{1,13},{5,1},{9,5},{13,9},{2,14},{6,2},{... | collective-permute-start | bytes 221192 | tf_op jit(solution)/shard_map/ppermute | solution.py:584
  12.0 4.9 %collective-permute-start.2 = (f32[9,3,8,128]{3,2,1,0:T(8,128)S(1)}, f32[9,3,8,128]{3,2,1,0:T(8,128)S(1)}, u32[]{:S(2)}, u32[]{:S(2)}) collective-permute-start(f32[9,3,8,128]{3,2,1,0:T(8,128)S(1)} %get-tuple-element.38), channel_id=1, source_target_pairs={{0,1},{1,2},{2,3},{3,0},{4,5},{5,6},{6,7},{7,4},{8,9},{9,10},{10,1... | collective-permute-start | bytes 331784 | tf_op jit(solution)/shard_map/ppermute | solution.py:587
  13.4 3.6 %collective-permute-start.3 = (f32[9,3,8,128]{3,2,1,0:T(8,128)S(1)}, f32[9,3,8,128]{3,2,1,0:T(8,128)S(1)}, u32[]{:S(2)}, u32[]{:S(2)}) collective-permute-start(f32[9,3,8,128]{3,2,1,0:T(8,128)S(1)} %get-tuple-element.39), channel_id=1, source_target_pairs={{0,3},{1,0},{2,1},{3,2},{4,7},{5,4},{6,5},{7,6},{8,11},{9,8},{10,9... | collective-permute-start | bytes 331784 | tf_op jit(solution)/shard_map/ppermute | solution.py:588
  17.0 20.6 %copy-start.4 = (s32[8,128]{1,0:T(8,128)S(1)}, s32[8,128]{1,0:T(8,128)}, u32[]{:S(2)}) copy-start(s32[8,128]{1,0:T(8,128)} %get-tuple-element.29.code_ref) | copy-start | bytes 12292
  17.0 20.6 %copy-start.5 = (f32[8,128]{1,0:T(8,128)S(1)}, f32[8,128]{1,0:T(8,128)}, u32[]{:S(2)}) copy-start(f32[8,128]{1,0:T(8,128)} %get-tuple-element.41.inside_ref) | copy-start | bytes 12292
  35.1 9.3 %collective-permute-start.5 = (bf16[256,8,256]{2,1,0:T(8,128)(2,1)S(1)}, bf16[256,8,256]{2,1,0:T(8,128)(2,1)S(1)}, u32[]{:S(2)}, u32[]{:S(2)}) collective-permute-start(bf16[256,8,256]{2,1,0:T(8,128)(2,1)S(1)} %get-tuple-element.42.refs_0_), channel_id=1, source_target_pairs={{0,16},{16,0},{32,48},{48,32},{64,80},{80,64},{96,112},{112,96},{1... | collective-permute-start | bytes 3145736 | tf_op jit(solution)/shard_map/ppermute | solution.py:596
  40.3 4.1 %collective-permute-start.4 = (f32[8,2176]{1,0:T(8,128)S(1)}, f32[8,2176]{1,0:T(8,128)S(1)}, u32[]{:S(2)}, u32[]{:S(2)}) collective-permute-start(f32[8,2176]{1,0:T(8,128)S(1)} %pad_maximum_fusion), channel_id=1, source_target_pairs={{0,1},{1,0},{2,3},{3,2},{4,5},{5,4},{6,7},{7,6},{8,9},{9,8},{10,11... | collective-permute-start | bytes 208904 | tf_op jit(solution)/shard_map/ppermute | solution.py:613
  41.7 22.9 %collective-permute-start.10 = (bf16[256,8,256]{2,1,0:T(8,128)(2,1)S(1)}, bf16[256,8,256]{2,1,0:T(8,128)(2,1)S(1)}, u32[]{:S(2)}, u32[]{:S(2)}) collective-permute-start(bf16[256,8,256]{2,1,0:T(8,128)(2,1)S(1)} %get-tuple-element.42.refs_0_), channel_id=1, source_target_pairs={{0,96},{16,48},{32,0},{48,80},{64,32},{80,112},{96,64},{112,16},{1... | collective-permute-start | bytes 3145736 | tf_op jit(solution)/shard_map/ppermute | solution.py:596
  42.9 24.7 %collective-permute-start.9 = (bf16[256,8,256]{2,1,0:T(8,128)(2,1)S(1)}, bf16[256,8,256]{2,1,0:T(8,128)(2,1)S(1)}, u32[]{:S(2)}, u32[]{:S(2)}) collective-permute-start(bf16[256,8,256]{2,1,0:T(8,128)(2,1)S(1)} %get-tuple-element.42.refs_0_), channel_id=1, source_target_pairs={{0,32},{16,112},{32,64},{48,16},{64,96},{80,48},{96,0},{112,80},{1... | collective-permute-start | bytes 3145736 | tf_op jit(solution)/shard_map/ppermute | solution.py:596
  44.4 4.5 %collective-permute-start.6 = (f32[8,2176]{1,0:T(8,128)S(1)}, f32[8,2176]{1,0:T(8,128)S(1)}, u32[]{:S(2)}, u32[]{:S(2)}) collective-permute-start(f32[8,2176]{1,0:T(8,128)S(1)} %fusion), channel_id=1, source_target_pairs={{0,3},{1,2},{2,1},{3,0},{4,7},{5,6},{6,5},{7,4},{8,11},{9,10},{10,... | collective-permute-start | bytes 208904 | tf_op jit(solution)/shard_map/ppermute | solution.py:613
  48.8 3.5 %collective-permute-start.7 = (f32[8,2176]{1,0:T(8,128)S(1)}, f32[8,2176]{1,0:T(8,128)S(1)}, u32[]{:S(2)}, u32[]{:S(2)}) collective-permute-start(f32[8,2176]{1,0:T(8,128)S(1)} %add.45), channel_id=1, source_target_pairs={{0,4},{4,0},{8,12},{12,8},{1,5},{5,1},{9,13},{13,9},{2,6},{6,2},{1... | collective-permute-start | bytes 208904 | tf_op jit(solution)/shard_map/ppermute | solution.py:613
  52.4 4.7 %collective-permute-start.8 = (f32[8,2176]{1,0:T(8,128)S(1)}, f32[8,2176]{1,0:T(8,128)S(1)}, u32[]{:S(2)}, u32[]{:S(2)}) collective-permute-start(f32[8,2176]{1,0:T(8,128)S(1)} %add.46), channel_id=1, source_target_pairs={{0,12},{4,8},{8,4},{12,0},{1,13},{5,9},{9,5},{13,1},{2,14},{6,10},... | collective-permute-start | bytes 208904 | tf_op jit(solution)/shard_map/ppermute | solution.py:613
  67.6 4.1 %collective-permute-start.11 = (f32[8,1024]{1,0:T(8,128)S(1)}, f32[8,1024]{1,0:T(8,128)S(1)}, u32[]{:S(2)}, u32[]{:S(2)}) collective-permute-start(f32[8,1024]{1,0:T(8,128)S(1)} %get-tuple-element.44), channel_id=1, source_target_pairs={{0,32},{16,112},{32,64},{48,16},{64,96},{80,48},{96,0},{112,80},{1... | collective-permute-start | bytes 98312 | tf_op jit(solution)/shard_map/ppermute | solution.py:596
  70.2 4.0 %collective-permute-start.12 = (f32[8,1024]{1,0:T(8,128)S(1)}, f32[8,1024]{1,0:T(8,128)S(1)}, u32[]{:S(2)}, u32[]{:S(2)}) collective-permute-start(f32[8,1024]{1,0:T(8,128)S(1)} %get-tuple-element.44), channel_id=1, source_target_pairs={{0,96},{16,48},{32,0},{48,80},{64,32},{80,112},{96,64},{112,16},{1... | collective-permute-start | bytes 98312 | tf_op jit(solution)/shard_map/ppermute | solution.py:596
  70.2 4.3 %collective-permute-start.13 = (f32[8,1024]{1,0:T(8,128)S(1)}, f32[8,1024]{1,0:T(8,128)S(1)}, u32[]{:S(2)}, u32[]{:S(2)}) collective-permute-start(f32[8,1024]{1,0:T(8,128)S(1)} %get-tuple-element.44), channel_id=1, source_target_pairs={{0,64},{16,80},{32,96},{48,112},{64,0},{80,16},{96,32},{112,48},{1... | collective-permute-start | bytes 98312 | tf_op jit(solution)/shard_map/ppermute | solution.py:596
  74.5 3.6 %collective-permute-start.14 = (f32[32,1024]{1,0:T(8,128)S(1)}, f32[32,1024]{1,0:T(8,128)S(1)}, u32[]{:S(2)}, u32[]{:S(2)}) collective-permute-start(f32[32,1024]{1,0:T(8,128)S(1)} %constant_dynamic-update-slice_fusion.near_ref), channel_id=1, source_target_pairs={{0,16},{16,0},{32,48},{48,32},{64,80},{80,64},{96,112},{112,96},{1... | collective-permute-start | bytes 393224 | tf_op jit(solution)/shard_map/ppermute | solution.py:596
  78.1 18.9 %collective-permute-start.19 = (bf16[256,8,256]{2,1,0:T(8,128)(2,1)S(1)}, bf16[256,8,256]{2,1,0:T(8,128)(2,1)S(1)}, u32[]{:S(2)}, u32[]{:S(2)}) collective-permute-start(bf16[256,8,256]{2,1,0:T(8,128)(2,1)S(1)} %collective-permute-done.9.refs_1_), channel_id=1, source_target_pairs={{0,16},{16,0},{32,48},{48,32},{64,80},{80,64},{96,112},{112,96},{1... | collective-permute-start | bytes 3145736 | tf_op jit(solution)/shard_map/ppermute | solution.py:596
  78.5 18.6 %collective-permute-start.20 = (bf16[256,8,256]{2,1,0:T(8,128)(2,1)S(1)}, bf16[256,8,256]{2,1,0:T(8,128)(2,1)S(1)}, u32[]{:S(2)}, u32[]{:S(2)}) collective-permute-start(bf16[256,8,256]{2,1,0:T(8,128)(2,1)S(1)} %collective-permute-done.10.refs_2_), channel_id=1, source_target_pairs={{0,16},{16,0},{32,48},{48,32},{64,80},{80,64},{96,112},{112,96},{1... | collective-permute-start | bytes 3145736 | tf_op jit(solution)/shard_map/ppermute | solution.py:596
  78.7 13.1 %collective-permute-start.15 = (bf16[128,8,256]{2,1,0:T(8,128)(2,1)S(1)}, bf16[128,8,256]{2,1,0:T(8,128)(2,1)S(1)}, u32[]{:S(2)}, u32[]{:S(2)}) collective-permute-start(bf16[128,8,256]{2,1,0:T(8,128)(2,1)S(1)} %slice.18), channel_id=1, source_target_pairs={{0,32},{16,112},{32,64},{48,16},{64,96},{80,48},{96,0},{112,80},{1... | collective-permute-start | bytes 1572872 | tf_op jit(solution)/shard_map/ppermute | solution.py:596
  80.2 14.2 %collective-permute-start.16 = (bf16[128,8,256]{2,1,0:T(8,128)(2,1)S(1)}, bf16[128,8,256]{2,1,0:T(8,128)(2,1)S(1)}, u32[]{:S(2)}, u32[]{:S(2)}) collective-permute-start(bf16[128,8,256]{2,1,0:T(8,128)(2,1)S(1)} %slice.19), channel_id=1, source_target_pairs={{0,96},{16,48},{32,0},{48,80},{64,32},{80,112},{96,64},{112,16},{1... | collective-permute-start | bytes 1572872 | tf_op jit(solution)/shard_map/ppermute | solution.py:596
  91.7 8.3 %collective-permute-start.17 = (bf16[128,8,256]{2,1,0:T(8,128)(2,1)S(1)}, bf16[128,8,256]{2,1,0:T(8,128)(2,1)S(1)}, u32[]{:S(2)}, u32[]{:S(2)}) collective-permute-start(bf16[128,8,256]{2,1,0:T(8,128)(2,1)S(1)} %collective-permute-done.15.refs_0_), channel_id=1, source_target_pairs={{0,16},{16,0},{32,48},{48,32},{64,80},{80,64},{96,112},{112,96},{1... | collective-permute-start | bytes 1572872 | tf_op jit(solution)/shard_map/ppermute | solution.py:596
  94.4 5.7 %collective-permute-start.18 = (bf16[128,8,256]{2,1,0:T(8,128)(2,1)S(1)}, bf16[128,8,256]{2,1,0:T(8,128)(2,1)S(1)}, u32[]{:S(2)}, u32[]{:S(2)}) collective-permute-start(bf16[128,8,256]{2,1,0:T(8,128)(2,1)S(1)} %collective-permute-done.16.refs_1_), channel_id=1, source_target_pairs={{0,16},{16,0},{32,48},{48,32},{64,80},{80,64},{96,112},{112,96},{1... | collective-permute-start | bytes 1572872 | tf_op jit(solution)/shard_map/ppermute | solution.py:596

commit v7 on v5

--- a/solution.py
+++ b/solution.py
@@ -50,7 +50,7 @@
     )
     x, y = x & (size_x - 1), y & (size_y - 1)
     tile = x * (size_y // 128) + lax.shift_right_logical(y, 7)
-    code_ref[...] = tile * 128 + ((lanes() - y) & 127)
+    code_ref[...] = tile * 1024 + ((lanes() - y) & 127)
     inside_ref[...] = jnp.where(mine, F32(1), F32(0))
     for c in copies:
         c.wait()
@@ -387,7 +387,8 @@
         acc = jnp.zeros((8, 128), F32)
         for u in range(128):
             code = code_ref[g, u]
-            v = pltpu.roll(f_ref[lax.shift_right_logical(code, 7)], code, 1)
+            at = pl.multiple_of(lax.shift_right_logical(code, 7), 8)
+            v = pltpu.roll(f_ref[pl.ds(at, 8), :], code, 1)
             acc = jnp.where(lane == u, v, acc)
         keep = wide(inside_ref[pl.ds(g, 1), :]) > F32(0.5)
         pick_ref[:, pl.ds(pl.multiple_of(g * 128, 128), 128)] = jnp.where(keep, acc, F32(0))
@@ -405,7 +406,7 @@
         out_shape=jax.ShapeDtypeStruct((8, code.size), F32),
         compiler_params=pltpu.CompilerParams(vmem_limit_bytes=8 * 2**20),
         name="picks",
-    )(code, forecast, inside)
+    )(code, forecast.reshape(-1, 128), inside)
 
 
 def weights_kernel(near_ref, far_ref, target_ref, error_ref, first_ref, last_ref, x_s, m_s):
@@ -500,13 +501,13 @@
     w = w_ref[...].astype(BF16)
 
     def chunk(g, _):
-        for r in range(16):
-            x = g * 16 + r
+        for r in range(64):
+            x = g * 64 + r
             for t, v in enumerate(shifted(w, pieces, f_ref, x, x)):
                 out_ref[2 * x + t] = v
         return 0
 
-    lax.fori_loop(0, pieces[0].shape[0] // 16, chunk, 0)
+    lax.fori_loop(0, pieces[0].shape[0] // 64, chunk, 0)
 
 
 def update_kernel(w_ref, *refs):

time: 103 us -> 101 us (0.981)
  Pallas kernels: 36 us -> 34.3 us
    pallas_call x1, Pallas kernels: 2.96 us -> 1.41 us  [begin(): pl.pallas_call(begin_kernel, in_specs=[VMEM_SPEC] * (len(pieces) + 2), ou...]
  transfers between devices with their start and end apart: 21 -> 21, of which waited for: 11 -> 11; matrix products, arithmetic and copies ran while one was open for 1% -> 1% of each run, Pallas kernels for 12% -> 11%
where the time goes in v7:
time: 101 us
  waiting for transfers between devices  35.7 us (35%)
  Pallas kernels  34.3 us (34%)
  starting transfers between devices  29.8 us (30%)
    ppermute x13, waiting for transfers between devices, send(): lax.ppermute(v, 'mem', [(i, i ^ 1) for i in range(n_m)] if swap else to)  25.7 us
    pallas_call x1, Pallas kernels, run_steps(): pl.pallas_call(steps_kernel, in_specs=[HBM_SPEC] * 2 + [VMEM_SPEC] * 6, o...  18.1 us
    ppermute x13, starting transfers between devices, send(): lax.ppermute(v, 'mem', [(i, i ^ 1) for i in range(n_m)] if swap else to)  16.6 us
    ppermute x4, waiting for transfers between devices, local(): lax.ppermute(line, axis, [(i, i ^ span - 1) for i in range(n)])  8.46 us
    ppermute x4, starting transfers between devices, local(): lax.ppermute(line, axis, [(i, i ^ span - 1) for i in range(n)])  5.64 us
    pallas_call x1, Pallas kernels, turn(): pl.pallas_call(turn_kernel, in_specs=[HBM_SPEC] * 2 + [VMEM_SPEC] * 2, ou...  4.27 us
    pallas_call x1, Pallas kernels, ends(): pl.pallas_call(ends_kernel, in_specs=[VMEM_SPEC] + [HBM_SPEC] * 2 + [VMEM...  2.76 us
    pallas_call x1, Pallas kernels, solve_weights(): pl.pallas_call(weights_kernel, in_specs=[VMEM_SPEC] * 4, out_specs=[VMEM_...  2.62 us
  transfers between devices with their start and end apart: 21, of which 11 were waited for; matrix products, arithmetic and copies ran while one was open for 1% of the time, Pallas kernels for 11%

profile of v7, /device:TPU:1, one launch (start us, length us, event | category | flops | bytes accessed | tf_op | source)
XLA Modules:
  0.0 100.8 jit_solution(9969507682213049189)
XLA Ops:
  0.0 2.8 %ends.1 = (f32[9,8,256]{2,1,0:T(8,128)}, f32[9,8,256]{2,1,0:T(8,128)}, s32[8,128]{1,0:T(8,128)}, f32[8,128]{1,0:T(8,128)}) custom-call(s32[8,128]{1,0:T(8,128)} %bitcast.6, f32[8,256,256]{2,1,0:T(8,128)} %p_in.1, f32[8,256,256]{2,1,0:T(8,128)} %w_in.1, f32[256,256]{1,0:T(8,128)} %e_ref.5, f32[256,256]{1,0:T(8,128)} %k_ref.5), custom_call_target="tpu_custom_call" | custom-call | tf_op jit(solution)/shard_map/ends/pallas_call | solution.py:75
  2.8 2.5 %collective-permute-start = (f32[9,8,256]{2,1,0:T(8,128)}, f32[9,8,256]{2,1,0:T(8,128)S(1)}, u32[]{:S(2)}, u32[]{:S(2)}) collective-permute-start(f32[9,8,256]{2,1,0:T(8,128)} %get-tuple-element.32.bottom_ref), channel_id=1, source_target_pairs={{0,4},{4,8},{8,12},{12,0},{1,5},{5,9},{9,13},{13,1},{2,6},{6,10},{... | collective-permute-start | bytes 221192 | tf_op jit(solution)/shard_map/ppermute | solution.py:584
  5.3 0.0 copy-start.8
  5.3 2.2 %collective-permute-start.1 = (f32[9,8,256]{2,1,0:T(8,128)}, f32[9,8,256]{2,1,0:T(8,128)S(1)}, u32[]{:S(2)}, u32[]{:S(2)}) collective-permute-start(f32[9,8,256]{2,1,0:T(8,128)} %get-tuple-element.33.top_ref), channel_id=1, source_target_pairs={{0,12},{4,0},{8,4},{12,8},{1,13},{5,1},{9,5},{13,9},{2,14},{6,2},{... | collective-permute-start | bytes 221192 | tf_op jit(solution)/shard_map/ppermute | solution.py:585
  7.6 4.3 %turn.1 = (f32[256,8,256]{2,1,0:T(8,128)}, f32[256,8,256]{2,1,0:T(8,128)}, f32[8,3,8,128]{3,2,1,0:T(8,128)S(1)}, f32[8,3,8,128]{3,2,1,0:T(8,128)S(1)}) custom-call(f32[8,256,256]{2,1,0:T(8,128)} %p_in.1, f32[8,256,256]{2,1,0:T(8,128)} %w_in.1, f32[256,256]{1,0:T(8,128)S(1)} %copy-done, f32[256,256]{1,0:T(8,128)S(1)} %copy-done.1), custom_call_target="tpu_custom_call" | custom-call | flops 10000000 | bytes 9437184 | tf_op jit(solution)/shard_map/turn/pallas_call | solution.py:157
  11.8 0.0 collective-permute-done.up_ref
  11.8 0.0 collective-permute-done.1.down_ref
  11.9 0.1 rows.1
  12.0 1.4 %collective-permute-start.2 = (f32[9,3,8,128]{3,2,1,0:T(8,128)S(1)}, f32[9,3,8,128]{3,2,1,0:T(8,128)S(1)}, u32[]{:S(2)}, u32[]{:S(2)}) collective-permute-start(f32[9,3,8,128]{3,2,1,0:T(8,128)S(1)} %get-tuple-element.38), channel_id=1, source_target_pairs={{0,1},{1,2},{2,3},{3,0},{4,5},{5,6},{6,7},{7,4},{8,9},{9,10},{10,1... | collective-permute-start | bytes 331784 | tf_op jit(solution)/shard_map/ppermute | solution.py:588
  13.4 1.5 %collective-permute-start.3 = (f32[9,3,8,128]{3,2,1,0:T(8,128)S(1)}, f32[9,3,8,128]{3,2,1,0:T(8,128)S(1)}, u32[]{:S(2)}, u32[]{:S(2)}) collective-permute-start(f32[9,3,8,128]{3,2,1,0:T(8,128)S(1)} %get-tuple-element.39), channel_id=1, source_target_pairs={{0,3},{1,0},{2,1},{3,2},{4,7},{5,4},{6,5},{7,6},{8,11},{9,8},{10,9... | collective-permute-start | bytes 331784 | tf_op jit(solution)/shard_map/ppermute | solution.py:589
  14.9 0.3 dynamic_update_slice.6
  15.2 0.2 dynamic_update_slice.7
  15.4 1.5 %collective-permute-done.2.fl_ref = f32[9,3,8,128]{3,2,1,0:T(8,128)S(1)} collective-permute-done((f32[9,3,8,128]{3,2,1,0:T(8,128)S(1)}, f32[9,3,8,128]{3,2,1,0:T(8,128)S(1)}, u32[]{:S(2)}, u32[]{:S(2)}) %collective-permute-start.2) | collective-permute-done | bytes 110624 | tf_op jit(solution)/shard_map/ppermute | solution.py:588
  16.9 0.0 collective-permute-done.3.fr_ref
  17.0 18.1 %steps.1 = (f32[512,8,128]{2,1,0:T(8,128)S(1)}, bf16[256,8,256]{2,1,0:T(8,128)(2,1)S(1)}) custom-call(f32[256,8,256]{2,1,0:T(8,128)} %get-tuple-element.30.pt_in, f32[256,8,256]{2,1,0:T(8,128)} %get-tuple-element.31.wt_in, f32[256,256]{1,0:T(8,128)S(1)} %copy-done, f32[256,256]{1,0:T(8,128)S(1)} %copy-done.1, f32[9,8,256]{2,1,0:T(8,128)S(1)} %get-tuple-element.36.above_ref, ...), custom_call_target="tpu_custom_call" | custom-call | tf_op jit(solution)/shard_map/steps/pallas_call | solution.py:369
  35.1 2.5 %collective-permute-start.5 = (bf16[256,8,256]{2,1,0:T(8,128)(2,1)S(1)}, bf16[256,8,256]{2,1,0:T(8,128)(2,1)S(1)}, u32[]{:S(2)}, u32[]{:S(2)}) collective-permute-start(bf16[256,8,256]{2,1,0:T(8,128)(2,1)S(1)} %get-tuple-element.42.refs_0_), channel_id=1, source_target_pairs={{0,16},{16,0},{32,48},{48,32},{64,80},{80,64},{96,112},{112,96},{1... | collective-permute-start | bytes 3145736 | tf_op jit(solution)/shard_map/ppermute | solution.py:597
  37.6 2.5 %picks.1 = f32[8,1024]{1,0:T(8,128)S(1)} custom-call(s32[8,128]{1,0:T(8,128)S(1)} %copy-done.4, f32[4096,128]{1,0:T(8,128)S(1)} %bitcast.5, f32[8,128]{1,0:T(8,128)S(1)} %copy-done.5), custom_call_target="tpu_custom_call" | custom-call | tf_op jit(solution)/shard_map/picks/pallas_call | solution.py:401
  40.1 1.4 %collective-permute-start.4 = (f32[8,2176]{1,0:T(8,128)S(1)}, f32[8,2176]{1,0:T(8,128)S(1)}, u32[]{:S(2)}, u32[]{:S(2)}) collective-permute-start(f32[8,2176]{1,0:T(8,128)S(1)} %pad_maximum_fusion), channel_id=1, source_target_pairs={{0,1},{1,0},{2,3},{3,2},{4,5},{5,4},{6,7},{7,6},{8,9},{9,8},{10,11... | collective-permute-start | bytes 208904 | tf_op jit(solution)/shard_map/ppermute | solution.py:614
  41.5 1.2 %collective-permute-start.10 = (bf16[256,8,256]{2,1,0:T(8,128)(2,1)S(1)}, bf16[256,8,256]{2,1,0:T(8,128)(2,1)S(1)}, u32[]{:S(2)}, u32[]{:S(2)}) collective-permute-start(bf16[256,8,256]{2,1,0:T(8,128)(2,1)S(1)} %get-tuple-element.42.refs_0_), channel_id=1, source_target_pairs={{0,96},{16,48},{32,0},{48,80},{64,32},{80,112},{96,64},{112,16},{1... | collective-permute-start | bytes 3145736 | tf_op jit(solution)/shard_map/ppermute | solution.py:597
  42.7 1.5 %collective-permute-start.9 = (bf16[256,8,256]{2,1,0:T(8,128)(2,1)S(1)}, bf16[256,8,256]{2,1,0:T(8,128)(2,1)S(1)}, u32[]{:S(2)}, u32[]{:S(2)}) collective-permute-start(bf16[256,8,256]{2,1,0:T(8,128)(2,1)S(1)} %get-tuple-element.42.refs_0_), channel_id=1, source_target_pairs={{0,32},{16,112},{32,64},{48,16},{64,96},{80,48},{96,0},{112,80},{1... | collective-permute-start | bytes 3145736 | tf_op jit(solution)/shard_map/ppermute | solution.py:597
  44.1 0.0 collective-permute-done.4
  44.1 0.0 collective-permute-done.5.refs_3_
  44.2 2.4 %collective-permute-start.6 = (f32[8,2176]{1,0:T(8,128)S(1)}, f32[8,2176]{1,0:T(8,128)S(1)}, u32[]{:S(2)}, u32[]{:S(2)}) collective-permute-start(f32[8,2176]{1,0:T(8,128)S(1)} %fusion), channel_id=1, source_target_pairs={{0,3},{1,2},{2,1},{3,0},{4,7},{5,6},{6,5},{7,4},{8,11},{9,10},{10,... | collective-permute-start | bytes 208904 | tf_op jit(solution)/shard_map/ppermute | solution.py:614
  46.6 2.0 %collective-permute-done.6 = f32[8,2176]{1,0:T(8,128)S(1)} collective-permute-done((f32[8,2176]{1,0:T(8,128)S(1)}, f32[8,2176]{1,0:T(8,128)S(1)}, u32[]{:S(2)}, u32[]{:S(2)}) %collective-permute-start.6) | collective-permute-done | bytes 69664 | tf_op jit(solution)/shard_map/ppermute | solution.py:614
  48.6 0.1 collective-permute-start.7
  48.7 3.4 %collective-permute-done.7 = f32[8,2176]{1,0:T(8,128)S(1)} collective-permute-done((f32[8,2176]{1,0:T(8,128)S(1)}, f32[8,2176]{1,0:T(8,128)S(1)}, u32[]{:S(2)}, u32[]{:S(2)}) %collective-permute-start.7) | collective-permute-done | bytes 69664 | tf_op jit(solution)/shard_map/ppermute | solution.py:614
  52.2 1.8 %collective-permute-start.8 = (f32[8,2176]{1,0:T(8,128)S(1)}, f32[8,2176]{1,0:T(8,128)S(1)}, u32[]{:S(2)}, u32[]{:S(2)}) collective-permute-start(f32[8,2176]{1,0:T(8,128)S(1)} %add.46), channel_id=1, source_target_pairs={{0,12},{4,8},{8,4},{12,0},{1,13},{5,9},{9,5},{13,1},{2,14},{6,10},... | collective-permute-start | bytes 208904 | tf_op jit(solution)/shard_map/ppermute | solution.py:614
  54.0 3.0 %collective-permute-done.8 = f32[8,2176]{1,0:T(8,128)S(1)} collective-permute-done((f32[8,2176]{1,0:T(8,128)S(1)}, f32[8,2176]{1,0:T(8,128)S(1)}, u32[]{:S(2)}, u32[]{:S(2)}) %collective-permute-start.8) | collective-permute-done | bytes 69664 | tf_op jit(solution)/shard_map/ppermute | solution.py:614
  56.9 7.4 %collective-permute-done.10.refs_2_ = bf16[256,8,256]{2,1,0:T(8,128)(2,1)S(1)} collective-permute-done((bf16[256,8,256]{2,1,0:T(8,128)(2,1)S(1)}, bf16[256,8,256]{2,1,0:T(8,128)(2,1)S(1)}, u32[]{:S(2)}, u32[]{:S(2)}) %collective-permute-start.10) | collective-permute-done | bytes 1048608 | tf_op jit(solution)/shard_map/ppermute | solution.py:597
  64.3 3.1 %collective-permute-done.9.refs_1_ = bf16[256,8,256]{2,1,0:T(8,128)(2,1)S(1)} collective-permute-done((bf16[256,8,256]{2,1,0:T(8,128)(2,1)S(1)}, bf16[256,8,256]{2,1,0:T(8,128)(2,1)S(1)}, u32[]{:S(2)}, u32[]{:S(2)}) %collective-permute-start.9) | collective-permute-done | bytes 1048608 | tf_op jit(solution)/shard_map/ppermute | solution.py:597
  67.4 2.5 %collective-permute-start.11 = (f32[8,1024]{1,0:T(8,128)S(1)}, f32[8,1024]{1,0:T(8,128)S(1)}, u32[]{:S(2)}, u32[]{:S(2)}) collective-permute-start(f32[8,1024]{1,0:T(8,128)S(1)} %get-tuple-element.44), channel_id=1, source_target_pairs={{0,32},{16,112},{32,64},{48,16},{64,96},{80,48},{96,0},{112,80},{1... | collective-permute-start | bytes 98312 | tf_op jit(solution)/shard_map/ppermute | solution.py:597
  70.0 1.5 %collective-permute-start.13 = (f32[8,1024]{1,0:T(8,128)S(1)}, f32[8,1024]{1,0:T(8,128)S(1)}, u32[]{:S(2)}, u32[]{:S(2)}) collective-permute-start(f32[8,1024]{1,0:T(8,128)S(1)} %get-tuple-element.44), channel_id=1, source_target_pairs={{0,64},{16,80},{32,96},{48,112},{64,0},{80,16},{96,32},{112,48},{1... | collective-permute-start | bytes 98312 | tf_op jit(solution)/shard_map/ppermute | solution.py:597
  71.5 2.5 %collective-permute-done.12 = f32[8,1024]{1,0:T(8,128)S(1)} collective-permute-done((f32[8,1024]{1,0:T(8,128)S(1)}, f32[8,1024]{1,0:T(8,128)S(1)}, u32[]{:S(2)}, u32[]{:S(2)}) %collective-permute-start.12) | collective-permute-done | bytes 32800 | tf_op jit(solution)/shard_map/ppermute | solution.py:597
  73.9 0.3 collective-permute-done.13
  74.3 2.6 %collective-permute-start.14 = (f32[32,1024]{1,0:T(8,128)S(1)}, f32[32,1024]{1,0:T(8,128)S(1)}, u32[]{:S(2)}, u32[]{:S(2)}) collective-permute-start(f32[32,1024]{1,0:T(8,128)S(1)} %constant_dynamic-update-slice_fusion.near_ref), channel_id=1, source_target_pairs={{0,16},{16,0},{32,48},{48,32},{64,80},{80,64},{96,112},{112,96},{1... | collective-permute-start | bytes 393224 | tf_op jit(solution)/shard_map/ppermute | solution.py:597
  76.9 1.0 collective-permute-done.14.far_ref
  77.9 0.4 collective-permute-start.19
  78.3 0.1 collective-permute-start.20
  78.4 1.5 %collective-permute-start.15 = (bf16[128,8,256]{2,1,0:T(8,128)(2,1)S(1)}, bf16[128,8,256]{2,1,0:T(8,128)(2,1)S(1)}, u32[]{:S(2)}, u32[]{:S(2)}) collective-permute-start(bf16[128,8,256]{2,1,0:T(8,128)(2,1)S(1)} %slice.18), channel_id=1, source_target_pairs={{0,32},{16,112},{32,64},{48,16},{64,96},{80,48},{96,0},{112,80},{1... | collective-permute-start | bytes 1572872 | tf_op jit(solution)/shard_map/ppermute | solution.py:597
  80.0 0.1 collective-permute-start.16
  80.1 11.4 %collective-permute-done.15.refs_0_ = bf16[128,8,256]{2,1,0:T(8,128)(2,1)S(1)} collective-permute-done((bf16[128,8,256]{2,1,0:T(8,128)(2,1)S(1)}, bf16[128,8,256]{2,1,0:T(8,128)(2,1)S(1)}, u32[]{:S(2)}, u32[]{:S(2)}) %collective-permute-start.15) | collective-permute-done | bytes 524320 | tf_op jit(solution)/shard_map/ppermute | solution.py:597
  91.5 2.6 %collective-permute-start.17 = (bf16[128,8,256]{2,1,0:T(8,128)(2,1)S(1)}, bf16[128,8,256]{2,1,0:T(8,128)(2,1)S(1)}, u32[]{:S(2)}, u32[]{:S(2)}) collective-permute-start(bf16[128,8,256]{2,1,0:T(8,128)(2,1)S(1)} %collective-permute-done.15.refs_0_), channel_id=1, source_target_pairs={{0,16},{16,0},{32,48},{48,32},{64,80},{80,64},{96,112},{112,96},{1... | collective-permute-start | bytes 1572872 | tf_op jit(solution)/shard_map/ppermute | solution.py:597
  94.1 0.1 collective-permute-done.16.refs_1_
  94.2 2.6 %weights.1 = (f32[8,48]{1,0:T(8,128)S(1)}, f32[8,16]{1,0:T(8,128)S(1)}) custom-call(f32[32,1024]{1,0:T(8,128)S(1)} %constant_dynamic-update-slice_fusion.near_ref, f32[32,1024]{1,0:T(8,128)S(1)} %collective-permute-done.14.far_ref, f32[8,1024]{1,0:T(8,128)S(1)} %get-tuple-element.53.target_ref, f32[8,128]{1,0:T(8,128)S(1)} %slice.22.error_ref), custom_call_target="tpu_custom_call" | custom-call | tf_op jit(solution)/shard_map/weights/pallas_call | solution.py:477
  96.8 0.0 collective-permute-done.20.refs_5_
  96.9 1.4 %begin.1.refs_4_ = f32[512,8,128]{2,1,0:T(8,128)S(1)} custom-call(f32[8,48]{1,0:T(8,128)S(1)} %get-tuple-element.49.w_ref, bf16[256,8,256]{2,1,0:T(8,128)(2,1)S(1)} %get-tuple-element.42.refs_0_, bf16[256,8,256]{2,1,0:T(8,128)(2,1)S(1)} %collective-permute-done.9.refs_1_, bf16[256,8,256]{2,1,0:T(8,128)(2,1)S(1)} %collective-permute-done.10.refs_2_, ...), custom_call_target="tpu_custom_call" | custom-call | tf_op jit(solution)/shard_map/begin/pallas_call | solution.py:542
  98.3 0.0 collective-permute-done.17.refs_2_
  98.3 2.5 %update.1 = f32[8,256,256]{2,1,0:T(8,128)} custom-call(f32[8,16]{1,0:T(8,128)S(1)} %get-tuple-element.48.w_ref, bf16[128,8,256]{2,1,0:T(8,128)(2,1)S(1)} %collective-permute-done.15.refs_0_, bf16[128,8,256]{2,1,0:T(8,128)(2,1)S(1)} %collective-permute-done.16.refs_1_, bf16[128,8,256]{2,1,0:T(8,128)(2,1)S(1)} %collective-permute-done.17.refs_2_, ...), custom_call_target="tpu_custom_call" | custom-call | tf_op jit(solution)/shard_map/update/pallas_call | solution.py:557
  (38 shorter events, 0.2 us)
Async XLA Ops:
  0.0 7.6 %copy-start = (f32[256,256]{1,0:T(8,128)S(1)}, f32[256,256]{1,0:T(8,128)}, u32[]{:S(2)}) copy-start(f32[256,256]{1,0:T(8,128)} %e_ref.5) | copy-start | bytes 786436
  0.0 7.6 %copy-start.1 = (f32[256,256]{1,0:T(8,128)S(1)}, f32[256,256]{1,0:T(8,128)}, u32[]{:S(2)}) copy-start(f32[256,256]{1,0:T(8,128)} %k_ref.5) | copy-start | bytes 786436
  2.8 9.1 %collective-permute-start = (f32[9,8,256]{2,1,0:T(8,128)}, f32[9,8,256]{2,1,0:T(8,128)S(1)}, u32[]{:S(2)}, u32[]{:S(2)}) collective-permute-start(f32[9,8,256]{2,1,0:T(8,128)} %get-tuple-element.32.bottom_ref), channel_id=1, source_target_pairs={{0,4},{4,8},{8,12},{12,0},{1,5},{5,9},{9,13},{13,1},{2,6},{6,10},{... | collective-permute-start | bytes 221192 | tf_op jit(solution)/shard_map/ppermute | solution.py:584
  5.3 6.6 %copy-start.2 = (f32[9,8,256]{2,1,0:T(8,128)S(1)}, f32[9,8,256]{2,1,0:T(8,128)}, u32[]{:S(2)}) copy-start(f32[9,8,256]{2,1,0:T(8,128)} %get-tuple-element.33.top_ref) | copy-start | bytes 221188
  5.3 6.6 %copy-start.3 = (f32[9,8,256]{2,1,0:T(8,128)S(1)}, f32[9,8,256]{2,1,0:T(8,128)}, u32[]{:S(2)}) copy-start(f32[9,8,256]{2,1,0:T(8,128)} %get-tuple-element.32.bottom_ref) | copy-start | bytes 221188
  5.3 9.6 %copy-start.6 = (f32[64,8]{0,1:T(8,128)S(1)}, f32[64,8]{0,1:T(8,128)}, u32[]{:S(2)}) copy-start(f32[64,8]{0,1:T(8,128)} %param.15) | copy-start | bytes 6148
  5.3 9.6 %copy-start.7 = (f32[64]{0:T(128)S(1)}, f32[64]{0:T(128)}, u32[]{:S(2)}) copy-start(f32[64]{0:T(128)} %param.14) | copy-start | bytes 772
  5.3 9.6 %copy-start.8 = (f32[64]{0:T(128)S(1)}, f32[64]{0:T(128)}, u32[]{:S(2)}) copy-start(f32[64]{0:T(128)} %param.13) | copy-start | bytes 772
  5.3 6.5 %collective-permute-start.1 = (f32[9,8,256]{2,1,0:T(8,128)}, f32[9,8,256]{2,1,0:T(8,128)S(1)}, u32[]{:S(2)}, u32[]{:S(2)}) collective-permute-start(f32[9,8,256]{2,1,0:T(8,128)} %get-tuple-element.33.top_ref), channel_id=1, source_target_pairs={{0,12},{4,0},{8,4},{12,8},{1,13},{5,1},{9,5},{13,9},{2,14},{6,2},{... | collective-permute-start | bytes 221192 | tf_op jit(solution)/shard_map/ppermute | solution.py:585
  12.0 4.9 %collective-permute-start.2 = (f32[9,3,8,128]{3,2,1,0:T(8,128)S(1)}, f32[9,3,8,128]{3,2,1,0:T(8,128)S(1)}, u32[]{:S(2)}, u32[]{:S(2)}) collective-permute-start(f32[9,3,8,128]{3,2,1,0:T(8,128)S(1)} %get-tuple-element.38), channel_id=1, source_target_pairs={{0,1},{1,2},{2,3},{3,0},{4,5},{5,6},{6,7},{7,4},{8,9},{9,10},{10,1... | collective-permute-start | bytes 331784 | tf_op jit(solution)/shard_map/ppermute | solution.py:588
  13.4 3.6 %collective-permute-start.3 = (f32[9,3,8,128]{3,2,1,0:T(8,128)S(1)}, f32[9,3,8,128]{3,2,1,0:T(8,128)S(1)}, u32[]{:S(2)}, u32[]{:S(2)}) collective-permute-start(f32[9,3,8,128]{3,2,1,0:T(8,128)S(1)} %get-tuple-element.39), channel_id=1, source_target_pairs={{0,3},{1,0},{2,1},{3,2},{4,7},{5,4},{6,5},{7,6},{8,11},{9,8},{10,9... | collective-permute-start | bytes 331784 | tf_op jit(solution)/shard_map/ppermute | solution.py:589
  17.0 20.6 %copy-start.4 = (s32[8,128]{1,0:T(8,128)S(1)}, s32[8,128]{1,0:T(8,128)}, u32[]{:S(2)}) copy-start(s32[8,128]{1,0:T(8,128)} %get-tuple-element.29.code_ref) | copy-start | bytes 12292
  17.0 20.6 %copy-start.5 = (f32[8,128]{1,0:T(8,128)S(1)}, f32[8,128]{1,0:T(8,128)}, u32[]{:S(2)}) copy-start(f32[8,128]{1,0:T(8,128)} %get-tuple-element.41.inside_ref) | copy-start | bytes 12292
  35.1 9.1 %collective-permute-start.5 = (bf16[256,8,256]{2,1,0:T(8,128)(2,1)S(1)}, bf16[256,8,256]{2,1,0:T(8,128)(2,1)S(1)}, u32[]{:S(2)}, u32[]{:S(2)}) collective-permute-start(bf16[256,8,256]{2,1,0:T(8,128)(2,1)S(1)} %get-tuple-element.42.refs_0_), channel_id=1, source_target_pairs={{0,16},{16,0},{32,48},{48,32},{64,80},{80,64},{96,112},{112,96},{1... | collective-permute-start | bytes 3145736 | tf_op jit(solution)/shard_map/ppermute | solution.py:597
  40.1 4.1 %collective-permute-start.4 = (f32[8,2176]{1,0:T(8,128)S(1)}, f32[8,2176]{1,0:T(8,128)S(1)}, u32[]{:S(2)}, u32[]{:S(2)}) collective-permute-start(f32[8,2176]{1,0:T(8,128)S(1)} %pad_maximum_fusion), channel_id=1, source_target_pairs={{0,1},{1,0},{2,3},{3,2},{4,5},{5,4},{6,7},{7,6},{8,9},{9,8},{10,11... | collective-permute-start | bytes 208904 | tf_op jit(solution)/shard_map/ppermute | solution.py:614
  41.5 22.9 %collective-permute-start.10 = (bf16[256,8,256]{2,1,0:T(8,128)(2,1)S(1)}, bf16[256,8,256]{2,1,0:T(8,128)(2,1)S(1)}, u32[]{:S(2)}, u32[]{:S(2)}) collective-permute-start(bf16[256,8,256]{2,1,0:T(8,128)(2,1)S(1)} %get-tuple-element.42.refs_0_), channel_id=1, source_target_pairs={{0,96},{16,48},{32,0},{48,80},{64,32},{80,112},{96,64},{112,16},{1... | collective-permute-start | bytes 3145736 | tf_op jit(solution)/shard_map/ppermute | solution.py:597
  42.7 24.7 %collective-permute-start.9 = (bf16[256,8,256]{2,1,0:T(8,128)(2,1)S(1)}, bf16[256,8,256]{2,1,0:T(8,128)(2,1)S(1)}, u32[]{:S(2)}, u32[]{:S(2)}) collective-permute-start(bf16[256,8,256]{2,1,0:T(8,128)(2,1)S(1)} %get-tuple-element.42.refs_0_), channel_id=1, source_target_pairs={{0,32},{16,112},{32,64},{48,16},{64,96},{80,48},{96,0},{112,80},{1... | collective-permute-start | bytes 3145736 | tf_op jit(solution)/shard_map/ppermute | solution.py:597
  44.2 4.5 %collective-permute-start.6 = (f32[8,2176]{1,0:T(8,128)S(1)}, f32[8,2176]{1,0:T(8,128)S(1)}, u32[]{:S(2)}, u32[]{:S(2)}) collective-permute-start(f32[8,2176]{1,0:T(8,128)S(1)} %fusion), channel_id=1, source_target_pairs={{0,3},{1,2},{2,1},{3,0},{4,7},{5,6},{6,5},{7,4},{8,11},{9,10},{10,... | collective-permute-start | bytes 208904 | tf_op jit(solution)/shard_map/ppermute | solution.py:614
  48.6 3.5 %collective-permute-start.7 = (f32[8,2176]{1,0:T(8,128)S(1)}, f32[8,2176]{1,0:T(8,128)S(1)}, u32[]{:S(2)}, u32[]{:S(2)}) collective-permute-start(f32[8,2176]{1,0:T(8,128)S(1)} %add.45), channel_id=1, source_target_pairs={{0,4},{4,0},{8,12},{12,8},{1,5},{5,1},{9,13},{13,9},{2,6},{6,2},{1... | collective-permute-start | bytes 208904 | tf_op jit(solution)/shard_map/ppermute | solution.py:614
  52.2 4.7 %collective-permute-start.8 = (f32[8,2176]{1,0:T(8,128)S(1)}, f32[8,2176]{1,0:T(8,128)S(1)}, u32[]{:S(2)}, u32[]{:S(2)}) collective-permute-start(f32[8,2176]{1,0:T(8,128)S(1)} %add.46), channel_id=1, source_target_pairs={{0,12},{4,8},{8,4},{12,0},{1,13},{5,9},{9,5},{13,1},{2,14},{6,10},... | collective-permute-start | bytes 208904 | tf_op jit(solution)/shard_map/ppermute | solution.py:614
  67.4 4.1 %collective-permute-start.11 = (f32[8,1024]{1,0:T(8,128)S(1)}, f32[8,1024]{1,0:T(8,128)S(1)}, u32[]{:S(2)}, u32[]{:S(2)}) collective-permute-start(f32[8,1024]{1,0:T(8,128)S(1)} %get-tuple-element.44), channel_id=1, source_target_pairs={{0,32},{16,112},{32,64},{48,16},{64,96},{80,48},{96,0},{112,80},{1... | collective-permute-start | bytes 98312 | tf_op jit(solution)/shard_map/ppermute | solution.py:597
  70.0 4.0 %collective-permute-start.12 = (f32[8,1024]{1,0:T(8,128)S(1)}, f32[8,1024]{1,0:T(8,128)S(1)}, u32[]{:S(2)}, u32[]{:S(2)}) collective-permute-start(f32[8,1024]{1,0:T(8,128)S(1)} %get-tuple-element.44), channel_id=1, source_target_pairs={{0,96},{16,48},{32,0},{48,80},{64,32},{80,112},{96,64},{112,16},{1... | collective-permute-start | bytes 98312 | tf_op jit(solution)/shard_map/ppermute | solution.py:597
  70.0 4.3 %collective-permute-start.13 = (f32[8,1024]{1,0:T(8,128)S(1)}, f32[8,1024]{1,0:T(8,128)S(1)}, u32[]{:S(2)}, u32[]{:S(2)}) collective-permute-start(f32[8,1024]{1,0:T(8,128)S(1)} %get-tuple-element.44), channel_id=1, source_target_pairs={{0,64},{16,80},{32,96},{48,112},{64,0},{80,16},{96,32},{112,48},{1... | collective-permute-start | bytes 98312 | tf_op jit(solution)/shard_map/ppermute | solution.py:597
  74.3 3.6 %collective-permute-start.14 = (f32[32,1024]{1,0:T(8,128)S(1)}, f32[32,1024]{1,0:T(8,128)S(1)}, u32[]{:S(2)}, u32[]{:S(2)}) collective-permute-start(f32[32,1024]{1,0:T(8,128)S(1)} %constant_dynamic-update-slice_fusion.near_ref), channel_id=1, source_target_pairs={{0,16},{16,0},{32,48},{48,32},{64,80},{80,64},{96,112},{112,96},{1... | collective-permute-start | bytes 393224 | tf_op jit(solution)/shard_map/ppermute | solution.py:597
  77.9 18.9 %collective-permute-start.19 = (bf16[256,8,256]{2,1,0:T(8,128)(2,1)S(1)}, bf16[256,8,256]{2,1,0:T(8,128)(2,1)S(1)}, u32[]{:S(2)}, u32[]{:S(2)}) collective-permute-start(bf16[256,8,256]{2,1,0:T(8,128)(2,1)S(1)} %collective-permute-done.9.refs_1_), channel_id=1, source_target_pairs={{0,16},{16,0},{32,48},{48,32},{64,80},{80,64},{96,112},{112,96},{1... | collective-permute-start | bytes 3145736 | tf_op jit(solution)/shard_map/ppermute | solution.py:597
  78.3 18.6 %collective-permute-start.20 = (bf16[256,8,256]{2,1,0:T(8,128)(2,1)S(1)}, bf16[256,8,256]{2,1,0:T(8,128)(2,1)S(1)}, u32[]{:S(2)}, u32[]{:S(2)}) collective-permute-start(bf16[256,8,256]{2,1,0:T(8,128)(2,1)S(1)} %collective-permute-done.10.refs_2_), channel_id=1, source_target_pairs={{0,16},{16,0},{32,48},{48,32},{64,80},{80,64},{96,112},{112,96},{1... | collective-permute-start | bytes 3145736 | tf_op jit(solution)/shard_map/ppermute | solution.py:597
  78.4 13.1 %collective-permute-start.15 = (bf16[128,8,256]{2,1,0:T(8,128)(2,1)S(1)}, bf16[128,8,256]{2,1,0:T(8,128)(2,1)S(1)}, u32[]{:S(2)}, u32[]{:S(2)}) collective-permute-start(bf16[128,8,256]{2,1,0:T(8,128)(2,1)S(1)} %slice.18), channel_id=1, source_target_pairs={{0,32},{16,112},{32,64},{48,16},{64,96},{80,48},{96,0},{112,80},{1... | collective-permute-start | bytes 1572872 | tf_op jit(solution)/shard_map/ppermute | solution.py:597
  80.0 14.2 %collective-permute-start.16 = (bf16[128,8,256]{2,1,0:T(8,128)(2,1)S(1)}, bf16[128,8,256]{2,1,0:T(8,128)(2,1)S(1)}, u32[]{:S(2)}, u32[]{:S(2)}) collective-permute-start(bf16[128,8,256]{2,1,0:T(8,128)(2,1)S(1)} %slice.19), channel_id=1, source_target_pairs={{0,96},{16,48},{32,0},{48,80},{64,32},{80,112},{96,64},{112,16},{1... | collective-permute-start | bytes 1572872 | tf_op jit(solution)/shard_map/ppermute | solution.py:597
  91.5 6.8 %collective-permute-start.17 = (bf16[128,8,256]{2,1,0:T(8,128)(2,1)S(1)}, bf16[128,8,256]{2,1,0:T(8,128)(2,1)S(1)}, u32[]{:S(2)}, u32[]{:S(2)}) collective-permute-start(bf16[128,8,256]{2,1,0:T(8,128)(2,1)S(1)} %collective-permute-done.15.refs_0_), channel_id=1, source_target_pairs={{0,16},{16,0},{32,48},{48,32},{64,80},{80,64},{96,112},{112,96},{1... | collective-permute-start | bytes 1572872 | tf_op jit(solution)/shard_map/ppermute | solution.py:597
  94.2 4.1 %collective-permute-start.18 = (bf16[128,8,256]{2,1,0:T(8,128)(2,1)S(1)}, bf16[128,8,256]{2,1,0:T(8,128)(2,1)S(1)}, u32[]{:S(2)}, u32[]{:S(2)}) collective-permute-start(bf16[128,8,256]{2,1,0:T(8,128)(2,1)S(1)} %collective-permute-done.16.refs_1_), channel_id=1, source_target_pairs={{0,16},{16,0},{32,48},{48,32},{64,80},{80,64},{96,112},{112,96},{1... | collective-permute-start | bytes 1572872 | tf_op jit(solution)/shard_map/ppermute | solution.py:597
